TPU v7x, 256 devices: a whole 4x4x8 slice. The times are simulated.
256 devices in a mesh: dp: 16 (over z, core), mp: 16 (over y, x).
Axes of the slice: x: 4, y: 4, z: 8, core: 2. Of those that a mesh axis runs over, the one named last changes fastest.
Arguments:
- records: bfloat16 [1024, 128, 1024], P(('dp', 'mp')), may hold values from -21 to 21
- w_query: bfloat16 [1024, 1024], replicated, may hold values from -0.1875 to 0.1875
- w_key: bfloat16 [1024, 1024], replicated, may hold values from -0.1875 to 0.1875
- w_value: bfloat16 [1024, 1024], replicated, may hold values from -0.1875 to 0.1875
- pair_owner: int32 [1024], P(('dp', 'mp')), may hold values from 0 to 1023, as said below
- pair_partner: int32 [1024], P(('dp', 'mp')), may hold values from 0 to 1023, as said below
- confidence: int32 [1024], P(('dp', 'mp')), may hold values from 16 to 256
- labels: int32 [1024], P(('dp', 'mp')), may hold values from 0 to 1
Outputs:
- loss: float32 [], replicated
- record_grad: float32 [1024, 128, 1024], P(('dp', 'mp'))
Inputs may be any that keep to these rules, and one draw needn't show every extreme that they name: `pair_owner`: the 4 pairs held by a device have their owners among the records held by that device. `pair_partner`: a partner follows its owner by 1 to 8 records in the circular record order (ids taken modulo 1024); in every draw some pair's partner is exactly 8 records after its owner.
All inputs are finite; a program needn't handle non-finite values.
Results may differ from a plain program's by a relative error of at most 0.03.
The roundings to bfloat16 on the way count: a program that leaves them out, or rounds other values in their place, can miss the bound.
Values may be sent and summed in bfloat16 or wider, within the bound.
No kernel may reach another device: no remote copies, remote signals or barrier semaphores. Data moves between devices by JAX's collectives and lax.ppermute only.
A program may use at most 128 MiB of HBM per device.

v0:
```python
import jax
import jax.numpy as jnp
from jax import lax
from jax.sharding import PartitionSpec as P

HEADS = 16


def from_behind(block, axis, distance):
    devices = range(lax.axis_size(axis))
    route = [((i - distance) % len(devices), i) for i in devices]
    return lax.ppermute(block, axis, route)


def attend(query, keys, values):
    size = keys.shape[-1] // HEADS
    qh = query.astype(jnp.float32).reshape(query.shape[0], HEADS, size)
    kh = keys.astype(jnp.float32).reshape(keys.shape[0], HEADS, size)
    vh = values.astype(jnp.float32).reshape(values.shape[0], HEADS, size)
    scores = jnp.einsum("qhd,khd->hqk", qh, kh) / jnp.sqrt(jnp.float32(size))
    chance = jax.nn.softmax(scores, axis=-1).astype(jnp.bfloat16)
    mixed = jnp.einsum("hqk,khd->qhd", chance.astype(jnp.float32), vh)
    return jnp.mean(mixed, axis=0)


def pair_link(q_own, k_own, v_own, q_other, k_other, v_other):
    return 4.0 * jnp.sum(attend(q_own, k_other, v_other) * attend(q_other, k_own, v_own))


def project(rows, weight):
    shape = rows.shape
    flat_rows = rows.reshape(shape[0] * shape[1], shape[2])
    out = jnp.dot(flat_rows, weight, preferred_element_type=jnp.float32)
    return out.astype(jnp.bfloat16).reshape(shape[0], shape[1], weight.shape[1])


def back_terms(three, weights):
    shape = three[0].shape
    total = jnp.zeros((shape[0] * shape[1], shape[2]), jnp.float32)
    for grad_part, weight in zip(three, weights):
        flat_grad = grad_part.reshape(shape[0] * shape[1], shape[2])
        total = total + lax.dot_general(
            flat_grad, weight, (((1,), (1,)), ((), ())), preferred_element_type=jnp.float32
        )
    return total.reshape(shape)


def on_device(records, w_query, w_key, w_value, pair_owner, pair_partner, confidence, labels):
    rec_count = records.shape[0]
    devices = lax.axis_size(("dp", "mp"))
    first_id = lax.axis_index(("dp", "mp")) * rec_count
    rec_total = rec_count * devices
    own_q = project(records, w_query)
    own_k = project(records, w_key)
    own_v = project(records, w_value)
    owner_slot = pair_owner - first_id
    partner_slot = jnp.mod(pair_partner - first_id, rec_total)
    window = [(own_q, own_k, own_v)]
    for distance in (1, 2):
        window.append(from_behind((own_q, own_k, own_v), ("dp", "mp"), -distance))
    part_q = jnp.concatenate([item[0] for item in window], axis=0)[partner_slot]
    part_k = jnp.concatenate([item[1] for item in window], axis=0)[partner_slot]
    part_v = jnp.concatenate([item[2] for item in window], axis=0)[partner_slot]
    inputs = (own_q[owner_slot], own_k[owner_slot], own_v[owner_slot], part_q, part_k, part_v)
    link_z, pullback = jax.vjp(jax.vmap(pair_link), *inputs)
    weight = confidence.astype(jnp.float32) / 256.0
    target = labels.astype(jnp.float32)
    loss_local = jnp.sum(weight * (jax.nn.softplus(link_z) - target * link_z))
    pair_cotangent = records.shape[1] * weight * (jax.nn.sigmoid(link_z) - target)
    grads = pullback(pair_cotangent)
    weights = (w_query, w_key, w_value)
    owner_term = back_terms(grads[0:3], weights)
    partner_term = back_terms(grads[3:6], weights)
    slots = jnp.arange(3 * rec_count, dtype=jnp.int32)
    owner_hot = (owner_slot[:, None] == slots[None, :]).astype(jnp.float32)
    partner_hot = (partner_slot[:, None] == slots[None, :]).astype(jnp.float32)
    gathered = jnp.einsum("ps,ptd->std", owner_hot, owner_term, precision=lax.Precision.HIGHEST)
    gathered = gathered + jnp.einsum(
        "ps,ptd->std", partner_hot, partner_term, precision=lax.Precision.HIGHEST
    )
    record_grad = gathered[:rec_count]
    for distance in (1, 2):
        piece = gathered[distance * rec_count : (distance + 1) * rec_count].astype(jnp.bfloat16)
        arrived = from_behind(piece, ("dp", "mp"), distance)
        record_grad = record_grad + arrived.astype(jnp.float32)
    loss = lax.psum(loss_local, ("dp", "mp")) / (pair_owner.shape[0] * devices)
    return (loss, record_grad)


def solution(mesh):
    in_specs = (
        P(("dp", "mp"), None, None),
        P(),
        P(),
        P(),
        P(("dp", "mp")),
        P(("dp", "mp")),
        P(("dp", "mp")),
        P(("dp", "mp")),
    )
    out_specs = (P(), P(("dp", "mp"), None, None))
    return jax.shard_map(
        on_device, mesh=mesh, in_specs=in_specs, out_specs=out_specs, check_vma=False
    )
```

profile of v0, /device:TPU:1, one launch (start us, length us, event | category | flops | bytes accessed | tf_op | source)
XLA Modules:
  0.0 341.0 jit_solution(2247746023525884819)
XLA Ops:
  0.7 4.3 %convolution_convert_fusion.10 = bf16[512,1024]{1,0:T(8,128)(2,1)} fusion(bf16[512,1024]{1,0:T(8,128)(2,1)} %bitcast.126, bf16[1024,1024]{1,0:T(8,128)(2,1)} %param.11), kind=kOutput, calls=%fused_computation.53 | convolution fusion | flops 1074266112 | bytes 4194304 | tf_op jit(solution)/shard_map/dot_general | solution.py:33
  4.9 6.6 %collective-permute-start.1 = (bf16[4,128,1024]{2,1,0:T(8,128)(2,1)}, bf16[4,128,1024]{2,1,0:T(8,128)(2,1)}, u32[]{:S(2)}, u32[]{:S(2)}) collective-permute-start(bf16[4,128,1024]{2,1,0:T(8,128)(2,1)} %bitcast.1), channel_id=1, source_target_pairs={{2,0},{3,1},{4,2},{5,3},{6,4},{7,5},{8,6},{9,7},{10,8},{11,9},{12,... | collective-permute-start | bytes 3145736 | tf_op jit(solution)/shard_map/ppermute | solution.py:12
  12.7 2.3 convolution_convert_fusion.9
  14.9 1.7 collective-permute-start.5
  16.6 2.0 collective-permute-start.4
  18.7 2.2 convolution_convert_fusion.8
  20.9 13.9 %collective-permute-done.1 = bf16[4,128,1024]{2,1,0:T(8,128)(2,1)} collective-permute-done((bf16[4,128,1024]{2,1,0:T(8,128)(2,1)}, bf16[4,128,1024]{2,1,0:T(8,128)(2,1)}, u32[]{:S(2)}, u32[]{:S(2)}) %collective-permute-start.1) | collective-permute-done | bytes 1048608 | tf_op jit(solution)/shard_map/ppermute | solution.py:12
  34.8 50.9 %collective-permute-start.2 = (bf16[4,128,1024]{2,1,0:T(8,128)(2,1)}, bf16[4,128,1024]{2,1,0:T(8,128)(2,1)}, u32[]{:S(2)}, u32[]{:S(2)}) collective-permute-start(bf16[4,128,1024]{2,1,0:T(8,128)(2,1)} %bitcast.5), channel_id=1, source_target_pairs={{1,0},{2,1},{3,2},{4,3},{5,4},{6,5},{7,6},{8,7},{9,8},{10,9},{11,1... | collective-permute-start | bytes 3145736 | tf_op jit(solution)/shard_map/ppermute | solution.py:12
  85.8 2.9 gather_fusion.5
  88.6 2.8 gather_fusion.1
  91.5 1.8 gather_fusion.3
  93.3 2.3 copy.33
  95.5 2.3 copy.28
  97.9 1.3 copy.31
  99.2 3.1 collective-permute-done
  102.2 3.2 pad_maximum_fusion
  105.4 3.5 %gather_fusion = bf16[4,128,1024]{2,1,0:T(8,128)(2,1)} fusion(bf16[12,128,1024]{2,1,0:T(8,128)(2,1)} %pad_maximum_fusion, s32[1024]{0:T(1024)S(1)} %pad_clamp_fusion.1), kind=kCustom, calls=%fused_computation | custom fusion | bytes 2097168 | tf_op jit(solution)/shard_map/gather | solution.py:63
  108.9 1.6 copy.27
  110.5 26.2 %collective-permute-done.4 = bf16[4,128,1024]{2,1,0:T(8,128)(2,1)} collective-permute-done((bf16[4,128,1024]{2,1,0:T(8,128)(2,1)}, bf16[4,128,1024]{2,1,0:T(8,128)(2,1)}, u32[]{:S(2)}, u32[]{:S(2)}) %collective-permute-start.4) | collective-permute-done | bytes 1048608 | tf_op jit(solution)/shard_map/ppermute | solution.py:12
  136.7 3.2 pad_maximum_fusion.2
  139.9 3.5 %gather_fusion.4 = bf16[4,128,1024]{2,1,0:T(8,128)(2,1)} fusion(bf16[12,128,1024]{2,1,0:T(8,128)(2,1)} %pad_maximum_fusion.2, s32[1024]{0:T(1024)S(1)} %pad_clamp_fusion.1), kind=kCustom, calls=%fused_computation.4 | custom fusion | bytes 2097168 | tf_op jit(solution)/shard_map/gather | solution.py:61
  143.4 2.3 copy.32
  145.6 13.6 %collective-permute-done.2 = bf16[4,128,1024]{2,1,0:T(8,128)(2,1)} collective-permute-done((bf16[4,128,1024]{2,1,0:T(8,128)(2,1)}, bf16[4,128,1024]{2,1,0:T(8,128)(2,1)}, u32[]{:S(2)}, u32[]{:S(2)}) %collective-permute-start.2) | collective-permute-done | bytes 1048608 | tf_op jit(solution)/shard_map/ppermute | solution.py:12
  159.2 3.2 pad_maximum_fusion.1
  162.4 3.5 %gather_fusion.2 = bf16[4,128,1024]{2,1,0:T(8,128)(2,1)} fusion(bf16[12,128,1024]{2,1,0:T(8,128)(2,1)} %pad_maximum_fusion.1, s32[1024]{0:T(1024)S(1)} %pad_clamp_fusion.1), kind=kCustom, calls=%fused_computation.2 | custom fusion | bytes 2097168 | tf_op jit(solution)/shard_map/gather | solution.py:62
  165.8 2.3 copy.29
  168.1 5.1 %fusion.74 = (f32[4,16,128]{2,1,0:T(8,128)S(1)}, f32[4,16,128,128]{2,3,1,0:T(8,128)}) fusion(bf16[4,128,16,64]{1,3,2,0:T(8,128)(2,1)} %bitcast.114, bf16[4,128,16,64]{1,3,2,0:T(8,128)(2,1)} %bitcast.118), kind=kOutput, calls=%fused_computation.115 | convolution fusion | flops 137363584 | bytes 6324224 | tf_op jit(solution)/shard_map/jvp(vmap())/sub | solution.py:21
  173.3 4.1 %divide_convert_fusion.1 = bf16[4,16,128,128]{2,3,1,0:T(8,128)(2,1)} fusion(f32[4,16,128,128]{2,3,1,0:T(8,128)} %get-tuple-element.19, f32[4,16,128]{2,1,0:T(8,128)S(1)} %get-tuple-element.18), kind=kLoop, calls=%fused_computation.24 | loop fusion | flops 2097152 | bytes 6324224 | tf_op jit(solution)/shard_map/jvp(vmap())/convert_element_type | solution.py:21
  177.4 5.1 %fusion.73 = (f32[4,16,128]{2,1,0:T(8,128)S(1)}, f32[4,16,128,128]{2,3,1,0:T(8,128)}) fusion(bf16[4,128,16,64]{1,3,2,0:T(8,128)(2,1)} %bitcast.120, bf16[4,128,16,64]{1,3,2,0:T(8,128)(2,1)} %bitcast.116), kind=kOutput, calls=%fused_computation.114 | convolution fusion | flops 137363584 | bytes 6324224 | tf_op jit(solution)/shard_map/jvp(vmap())/sub | solution.py:21
  182.5 2.9 divide_convert_fusion
  188.3 1.5 fusion.26
  189.9 1.9 fusion.11
  193.0 1.5 fusion.25
  194.5 1.5 fusion.29
  196.1 2.3 fusion.6
  198.4 1.6 fusion.28
  204.6 1.3 fusion.35
  205.9 1.3 fusion.40
  209.1 1.3 fusion.32
  210.4 1.5 fusion.43
  212.0 1.3 add_add_fusion.1
  213.3 5.0 %fusion.20 = f32[12,128,1024]{2,0,1:T(8,128)S(1)} fusion(f32[4,128,1024]{2,1,0:T(8,128)S(1)} %bitcast.111, s32[4]{0:T(128)S(1)} %get-tuple-element.9), kind=kOutput, calls=%fused_computation.37 | convolution fusion | flops 75497520 | bytes 8388624 | tf_op jit(solution)/shard_map/ps,ptd->std/dot_general | solution.py:77
  218.4 1.3 add_add_fusion
  219.7 7.4 %fusion.75 = (bf16[12,128,1024]{2,0,1:T(8,128)(2,1)S(1)}, f32[12,128,1024]{2,0,1:T(8,128)}) fusion(f32[12,128,1024]{2,0,1:T(8,128)S(1)} %fusion.20, f32[4,128,1024]{2,1,0:T(8,128)S(1)} %bitcast.110, s32[4]{0:T(128)S(1)} %get-tuple-element.27), kind=kOutput, calls=%fused_computation.116 | convolution fusion | flops 78643248 | bytes 17825808 | tf_op jit(solution)/shard_map/ps,ptd->std/dot_general | solution.py:78
  227.1 2.3 fusion.72
  229.7 103.3 %psum.7 = f32[]{:T(128)} all-reduce(f32[]{:T(128)} %get-tuple-element.13), channel_id=1, replica_groups=mesh['dp'=16,'mp'=16] {'dp','mp'}, use_global_device_ids=true, to_apply=%region_8.9 | all-reduce | flops 1 | bytes 8 | tf_op jit(solution)/shard_map/psum | solution.py:86
  333.7 3.4 fusion.18
  337.1 2.5 copy.49
  (62 shorter events, 12.0 us)
Async XLA Ops:
  0.6 18.1 %copy-start = (bf16[1024,1024]{1,0:T(8,128)(2,1)S(1)}, bf16[1024,1024]{1,0:T(8,128)(2,1)}, u32[]{:S(2)}) copy-start(bf16[1024,1024]{1,0:T(8,128)(2,1)} %param.10) | copy-start | bytes 6291460
  0.6 12.0 %copy-start.14 = (bf16[1024,1024]{1,0:T(8,128)(2,1)S(1)}, bf16[1024,1024]{1,0:T(8,128)(2,1)}, u32[]{:S(2)}) copy-start(bf16[1024,1024]{1,0:T(8,128)(2,1)} %param.9) | copy-start | bytes 6291460
  0.7 12.0 %copy-start.16 = (bf16[4,128,1024]{2,1,0:T(8,128)(2,1)S(1)}, bf16[4,128,1024]{2,1,0:T(8,128)(2,1)}, u32[]{:S(2)}) copy-start(bf16[4,128,1024]{2,1,0:T(8,128)(2,1)} %param.8) | copy-start | bytes 3145732
  4.9 29.9 %collective-permute-start.1 = (bf16[4,128,1024]{2,1,0:T(8,128)(2,1)}, bf16[4,128,1024]{2,1,0:T(8,128)(2,1)}, u32[]{:S(2)}, u32[]{:S(2)}) collective-permute-start(bf16[4,128,1024]{2,1,0:T(8,128)(2,1)} %bitcast.1), channel_id=1, source_target_pairs={{2,0},{3,1},{4,2},{5,3},{6,4},{7,5},{8,6},{9,7},{10,8},{11,9},{12,... | collective-permute-start | bytes 3145736 | tf_op jit(solution)/shard_map/ppermute | solution.py:12
  11.5 90.7 %collective-permute-start = (bf16[4,128,1024]{2,1,0:T(8,128)(2,1)}, bf16[4,128,1024]{2,1,0:T(8,128)(2,1)}, u32[]{:S(2)}, u32[]{:S(2)}) collective-permute-start(bf16[4,128,1024]{2,1,0:T(8,128)(2,1)} %bitcast.1), channel_id=1, source_target_pairs={{1,0},{2,1},{3,2},{4,3},{5,4},{6,5},{7,6},{8,7},{9,8},{10,9},{11,1... | collective-permute-start | bytes 3145736 | tf_op jit(solution)/shard_map/ppermute | solution.py:12
  14.9 70.8 %copy-start.10 = (s32[4]{0:T(128)S(1)}, s32[4]{0:T(128)}, u32[]{:S(2)}) copy-start(s32[4]{0:T(128)} %param.12) | copy-start | bytes 52
  14.9 70.8 %copy-start.11 = (s32[4]{0:T(128)S(1)}, s32[4]{0:T(128)}, u32[]{:S(2)}) copy-start(s32[4]{0:T(128)} %param.13) | copy-start | bytes 52
  14.9 95.6 %collective-permute-start.5 = (bf16[4,128,1024]{2,1,0:T(8,128)(2,1)}, bf16[4,128,1024]{2,1,0:T(8,128)(2,1)}, u32[]{:S(2)}, u32[]{:S(2)}) collective-permute-start(bf16[4,128,1024]{2,1,0:T(8,128)(2,1)} %bitcast.3), channel_id=1, source_target_pairs={{2,0},{3,1},{4,2},{5,3},{6,4},{7,5},{8,6},{9,7},{10,8},{11,9},{12,... | collective-permute-start | bytes 3145736 | tf_op jit(solution)/shard_map/ppermute | solution.py:12
  16.6 120.1 %collective-permute-start.4 = (bf16[4,128,1024]{2,1,0:T(8,128)(2,1)}, bf16[4,128,1024]{2,1,0:T(8,128)(2,1)}, u32[]{:S(2)}, u32[]{:S(2)}) collective-permute-start(bf16[4,128,1024]{2,1,0:T(8,128)(2,1)} %bitcast.3), channel_id=1, source_target_pairs={{1,0},{2,1},{3,2},{4,3},{5,4},{6,5},{7,6},{8,7},{9,8},{10,9},{11,1... | collective-permute-start | bytes 3145736 | tf_op jit(solution)/shard_map/ppermute | solution.py:12
  20.9 124.7 %collective-permute-start.3 = (bf16[4,128,1024]{2,1,0:T(8,128)(2,1)}, bf16[4,128,1024]{2,1,0:T(8,128)(2,1)}, u32[]{:S(2)}, u32[]{:S(2)}) collective-permute-start(bf16[4,128,1024]{2,1,0:T(8,128)(2,1)} %bitcast.5), channel_id=1, source_target_pairs={{2,0},{3,1},{4,2},{5,3},{6,4},{7,5},{8,6},{9,7},{10,8},{11,9},{12,... | collective-permute-start | bytes 3145736 | tf_op jit(solution)/shard_map/ppermute | solution.py:12
  34.8 124.4 %collective-permute-start.2 = (bf16[4,128,1024]{2,1,0:T(8,128)(2,1)}, bf16[4,128,1024]{2,1,0:T(8,128)(2,1)}, u32[]{:S(2)}, u32[]{:S(2)}) collective-permute-start(bf16[4,128,1024]{2,1,0:T(8,128)(2,1)} %bitcast.5), channel_id=1, source_target_pairs={{1,0},{2,1},{3,2},{4,3},{5,4},{6,5},{7,6},{8,7},{9,8},{10,9},{11,1... | collective-permute-start | bytes 3145736 | tf_op jit(solution)/shard_map/ppermute | solution.py:12
  182.5 3.0 copy-start.1
  185.5 1.2 copy-start.4
  185.5 2.1 copy-start.12
  185.5 2.1 copy-start.13
  186.7 3.1 copy-start.3
  189.9 1.9 copy-start.7
  191.8 1.2 copy-start.9
  193.0 3.1 copy-start.2
  196.1 2.3 copy-start.6
  198.4 1.6 copy-start.8
  201.9 2.7 copy-start.15
  210.4 1.6 copy-start.5
  229.4 104.3 %collective-permute-start.6 = (bf16[4,128,1024]{2,0,1:T(4,128)(2,1)}, bf16[4,128,1024]{2,0,1:T(4,128)(2,1)S(1)}, u32[]{:S(2)}, u32[]{:S(2)}) collective-permute-start(bf16[4,128,1024]{2,0,1:T(4,128)(2,1)} %get-tuple-element.10), channel_id=1, source_target_pairs={{255,0},{0,1},{1,2},{2,3},{3,4},{4,5},{5,6},{6,7},{7,8},{8,9},{9,1... | collective-permute-start | bytes 3145736 | tf_op jit(solution)/shard_map/ppermute | solution.py:12
  229.6 104.1 %collective-permute-start.7 = (bf16[4,128,1024]{2,0,1:T(4,128)(2,1)}, bf16[4,128,1024]{2,0,1:T(4,128)(2,1)}, u32[]{:S(2)}, u32[]{:S(2)}) collective-permute-start(bf16[4,128,1024]{2,0,1:T(4,128)(2,1)} %get-tuple-element.11), channel_id=1, source_target_pairs={{254,0},{255,1},{0,2},{1,3},{2,4},{3,5},{4,6},{5,7},{6,8},{7,9},{8... | collective-permute-start | bytes 3145736 | tf_op jit(solution)/shard_map/ppermute | solution.py:12
where the time goes:
time: 347 us; the launch traced here: 341 us
  blocking collectives  103 us (30%)
  starting transfers between devices  62.6 us (18%)
  waiting for transfers between devices  56.8 us (16%)
  matrix products  53.6 us (15%)
  local copies, waits for them, and re-layouts  40.8 us (12%)
  other arithmetic  20.8 us (6%)
    psum x1, blocking collectives, on_device(): loss = lax.psum(loss_local, ('dp', 'mp')) / (pair_owner.shape[0] * devices)  103 us
    ppermute x8, starting transfers between devices, from_behind(): return lax.ppermute(block, axis, route)  62.6 us
    ppermute x8, waiting for transfers between devices, from_behind(): return lax.ppermute(block, axis, route)  56.8 us
    sub x2, matrix products, attend(): chance = jax.nn.softmax(scores, axis=-1).astype(jnp.bfloat16)  10.3 us
    dot_general x3, matrix products, project(): out = jnp.dot(flat_rows, weight, preferred_element_type=jnp.float32)  8.79 us
    dot_general x6, matrix products, attend(): mixed = jnp.einsum('hqk,khd->qhd', chance.astype(jnp.float32), vh)  8.75 us
    dot_general x6, matrix products, back_terms(): lax.dot_general(flat_grad, weight, (((1,), (1,)), ((), ())), preferred_el...  8.17 us
    dot_general x1, matrix products, on_device(): jnp.einsum('ps,ptd->std', partner_hot, partner_term, precision=lax.Precis...  7.4 us
  transfers between devices with their start and end apart: 8, of which 4 were waited for; matrix products, arithmetic and copies ran while one was open for 10% of the time, Pallas kernels for 0%

commit v1 on v0

v1 whole, which is shorter than its diff:
```python
import functools

import jax
import jax.numpy as jnp
from jax import lax
from jax.experimental import pallas as pl
from jax.experimental.pallas import tpu as pltpu
from jax.sharding import PartitionSpec as P

AXES = ("dp", "mp")
HEADS = 16
LOG2_E = 1.4426950408889634
NT = (((1,), (1,)), ((), ()))
TN = (((0,), (0,)), ((), ()))
VMEM = pl.BlockSpec(memory_space=pltpu.VMEM)
SMEM = pl.BlockSpec(memory_space=pltpu.SMEM)
ANY = pl.BlockSpec(memory_space=pl.ANY)


def mm(a, b, dims=(((1,), (0,)), ((), ()))):
    return lax.dot_general(a, b, dims, preferred_element_type=jnp.float32)


def from_behind(block, distance):
    count = lax.axis_size(AXES)
    return lax.ppermute(block, AXES, [((i - distance) % count, i) for i in range(count)])


def project_kernel(x_ref, wq_ref, wk_ref, wv_ref, out_ref, *, tile):
    width = x_ref.shape[1]
    for n, w_ref in enumerate((wq_ref, wk_ref, wv_ref)):

        def columns(i, _, n=n, w_ref=w_ref):
            at = pl.multiple_of(i * tile, tile)
            made = mm(x_ref[...], w_ref[:, pl.ds(at, tile)])
            out_ref[:, pl.ds(pl.multiple_of(n * width + at, tile), tile)] = made.astype(jnp.bfloat16)
            return 0

        lax.fori_loop(0, width // tile, columns, 0)


def project(records, weights):
    count, seq, width = records.shape
    out = pl.pallas_call(
        functools.partial(project_kernel, tile=256),
        out_shape=jax.ShapeDtypeStruct((count * seq, 3 * width), jnp.bfloat16),
        in_specs=[VMEM] * 4,
        out_specs=VMEM,
        compiler_params=pltpu.CompilerParams(vmem_limit_bytes=40 << 20),
        cost_estimate=pl.CostEstimate(
            flops=6 * count * seq * width * width, bytes_accessed=14 << 20, transcendentals=0
        ),
        name="project",
    )(records.reshape(count * seq, width), *weights)
    return out.reshape(count, seq, 3 * width)


def attend(q, k, v, first, ends):
    zero = jnp.zeros_like(q)
    qs = jnp.concatenate([jnp.where(first, q, zero), jnp.where(first, zero, q)], axis=0)
    scores = mm(k, qs, NT)
    top = jnp.max(scores, axis=0, keepdims=True)
    e = jnp.exp2((scores - top) * (LOG2_E / 8.0))
    p = e * (1.0 / jnp.sum(e, axis=0, keepdims=True))
    mass = mm(p.astype(jnp.bfloat16), ends)
    pooled = jnp.sum(mass * v.astype(jnp.float32), axis=0, keepdims=True) * (1.0 / k.shape[0])
    return qs, p, mass, pooled


def attend_back(dp, qs, p, mass, k, v, first):
    dv = (mass * dp).astype(jnp.bfloat16)
    dpb = jnp.broadcast_to((dp * 0.125).astype(jnp.bfloat16), k.shape)
    zero = jnp.zeros_like(dpb)
    spread = jnp.concatenate([jnp.where(first, dpb, zero), jnp.where(first, zero, dpb)], axis=0)
    t = mm(v, spread, NT).astype(jnp.bfloat16).astype(jnp.float32)
    r = jnp.sum(p * t, axis=0, keepdims=True)
    ds = (p * (t - r)).astype(jnp.bfloat16)
    dk = mm(ds, qs).astype(jnp.bfloat16)
    both = mm(ds, k, TN)
    seq = k.shape[0]
    dq = jnp.where(first, both[:seq], both[seq:]).astype(jnp.bfloat16)
    return dq, dk, dv


def pairs_kernel(info_ref, left_ref, own_ref, right_ref, grads_ref, z_ref, a_buf, b_buf, sems):
    count, seq, full = a_buf.shape
    recs = left_ref.shape[0]
    width = full // 3

    def copy_a(p):
        return pltpu.make_async_copy(left_ref.at[info_ref[p]], a_buf.at[p], sems.at[0, p])

    def copy_b(p, source, slot):
        return pltpu.make_async_copy(source.at[slot], b_buf.at[p], sems.at[1, p])

    for p in range(count):
        copy_a(p).start()
        slot = info_ref[count + p]
        for n, source in enumerate((left_ref, own_ref, right_ref)):

            @pl.when((slot >= n * recs) & (slot < (n + 1) * recs))
            def _(p=p, n=n, source=source, slot=slot):
                copy_b(p, source, slot - n * recs).start()

    lane = lax.broadcasted_iota(jnp.int32, (seq, 128), 1)
    first = lane < 64
    row = lax.broadcasted_iota(jnp.int32, (2 * seq, 128), 0)
    col = lax.broadcasted_iota(jnp.int32, (2 * seq, 128), 1)
    ends = jnp.where((row < seq) == (col < 64), 1.0, 0.0).astype(jnp.bfloat16)
    for p in range(count):
        copy_a(p).wait()
        copy_b(p, own_ref, 0).wait()
        a, b = a_buf.at[p], b_buf.at[p]

        def head_pair(i, z, a=a, b=b, p=p):
            at = [pl.ds(pl.multiple_of(n * width + i * 128, 128), 128) for n in range(3)]
            qa, ka, va = (a[:, s] for s in at)
            qb, kb, vb = (b[:, s] for s in at)
            qs_ab, p_ab, mass_ab, pooled_ab = attend(qa, kb, vb, first, ends)
            qs_ba, p_ba, mass_ba, pooled_ba = attend(qb, ka, va, first, ends)
            z = z + pooled_ab * pooled_ba
            unit = 4.0 / seq
            dqa, dkb, dvb = attend_back(pooled_ba * unit, qs_ab, p_ab, mass_ab, kb, vb, first)
            dqb, dka, dva = attend_back(pooled_ab * unit, qs_ba, p_ba, mass_ba, ka, va, first)
            for s, value in zip(at, (dqa, dka, dva)):
                grads_ref[pl.ds(p * seq, seq), s] = value
            for s, value in zip(at, (dqb, dkb, dvb)):
                grads_ref[pl.ds((count + p) * seq, seq), s] = value
            return z

        z = lax.fori_loop(0, width // 128, head_pair, jnp.zeros((1, 128), jnp.float32))
        z_ref[p] = 4.0 * jnp.sum(z)


def pairs(info, left, own, right, count):
    recs, seq, full = own.shape
    return pl.pallas_call(
        pairs_kernel,
        out_shape=(
            jax.ShapeDtypeStruct((2 * count * seq, full), jnp.bfloat16),
            jax.ShapeDtypeStruct((count,), jnp.float32),
        ),
        in_specs=[SMEM, ANY, ANY, ANY],
        out_specs=(VMEM, SMEM),
        scratch_shapes=[
            pltpu.VMEM((count, seq, full), jnp.bfloat16),
            pltpu.VMEM((count, seq, full), jnp.bfloat16),
            pltpu.SemaphoreType.DMA((2, count)),
        ],
        compiler_params=pltpu.CompilerParams(vmem_limit_bytes=40 << 20),
        cost_estimate=pl.CostEstimate(flops=12 << 30, bytes_accessed=12 << 20, transcendentals=2 << 20),
        name="pairs",
    )(info, left, own, right)


def terms_kernel(info_ref, z_ref, g_ref, wq_ref, wk_ref, wv_ref, left_ref, own_ref, right_ref, acc, *, tile, count, recs):
    seq = g_ref.shape[0] // (2 * count)
    width = wq_ref.shape[1]
    scales = []
    for p in range(count):
        z = jnp.full((8, 128), z_ref[p], jnp.float32)
        c = info_ref[2 * count + p].astype(jnp.float32) * (1.0 / 256.0)
        y = info_ref[3 * count + p].astype(jnp.float32)
        scales.append((seq * c * (jax.nn.sigmoid(z) - y))[0:1, 0:1])

    def columns(i, _):
        at = pl.multiple_of(i * tile, tile)
        made = None
        for n, w_ref in enumerate((wq_ref, wk_ref, wv_ref)):
            part = mm(g_ref[:, n * width : (n + 1) * width], w_ref[pl.ds(at, tile), :], NT)
            made = part if made is None else made + part
        acc[...] = jnp.zeros_like(acc)
        for n in range(2 * count):
            slot = info_ref[n]
            acc[slot] += made[n * seq : (n + 1) * seq] * scales[n % count]
        for n, out in enumerate((left_ref, own_ref, right_ref)):
            out[:, :, pl.ds(at, tile)] = acc[n * recs : (n + 1) * recs].astype(jnp.bfloat16)
        return 0

    lax.fori_loop(0, wq_ref.shape[0] // tile, columns, 0)


def terms(info, z, grads, weights, recs, count):
    seq = grads.shape[0] // (2 * count)
    width, columns = weights[0].shape[1], weights[0].shape[0]
    made = jax.ShapeDtypeStruct((recs, seq, columns), jnp.bfloat16)
    tile = 256
    return pl.pallas_call(
        functools.partial(terms_kernel, tile=tile, count=count, recs=recs),
        out_shape=(made, made, made),
        in_specs=[SMEM, SMEM] + [VMEM] * 4,
        out_specs=(VMEM,) * 3,
        scratch_shapes=[pltpu.VMEM((3 * recs, seq, tile), jnp.float32)],
        compiler_params=pltpu.CompilerParams(vmem_limit_bytes=40 << 20),
        cost_estimate=pl.CostEstimate(
            flops=2 * grads.shape[0] * 3 * width * columns, bytes_accessed=20 << 20, transcendentals=0
        ),
        name="terms",
    )(info, z, grads, *weights)


def total_over_devices(value):
    count, step = lax.axis_size(AXES), 1
    while step < count:
        value = value + lax.ppermute(value, AXES, [(i, i ^ step) for i in range(count)])
        step *= 2
    return value


def on_device(records, w_query, w_key, w_value, pair_owner, pair_partner, confidence, labels):
    recs, seq, width = records.shape
    count = pair_owner.shape[0]
    devices = lax.axis_size(AXES)
    first_id = lax.axis_index(AXES) * recs
    weights = (w_query, w_key, w_value)

    own_info = jnp.concatenate(
        [pair_owner - first_id, jnp.mod(pair_partner - first_id, recs * devices), confidence, labels]
    )
    info = from_behind(own_info, 1)
    left_records = from_behind(records, 1)
    right_records = from_behind(records, -1)
    own = project(records, weights)
    left = project(left_records, weights)
    right = project(right_records, weights)

    grads, z = pairs(info, left, own, right, count)
    to_left, kept, to_right = terms(info, z, grads, weights, recs, count)
    from_right = from_behind(to_left, -1)
    from_left = from_behind(to_right, 1)

    c = info[2 * count : 3 * count].astype(jnp.float32) / 256.0
    y = info[3 * count :].astype(jnp.float32)
    loss = jnp.sum(c * (jax.nn.softplus(z) - y * z))
    loss = total_over_devices(loss) / (count * devices)
    record_grad = (
        from_right.astype(jnp.float32) + kept.astype(jnp.float32) + from_left.astype(jnp.float32)
    )
    return (loss, record_grad)


def solution(mesh):
    blocks = P(AXES, None, None)
    in_specs = (blocks, P(), P(), P(), P(AXES), P(AXES), P(AXES), P(AXES))
    return jax.shard_map(
        on_device, mesh=mesh, in_specs=in_specs, out_specs=(P(), blocks), check_vma=False
    )
```

time: 347 us -> 168 us (0.48)
  the two profiles are of different devices: /device:TPU:1 before, /device:TPU:2 now
where the time goes in v1:
time: 168 us
  Pallas kernels  70.8 us (42%)
  waiting for transfers between devices  50.3 us (30%)
  starting transfers between devices  24.2 us (14%)
  local copies, waits for them, and re-layouts  9.53 us (6%)
  between operations  7.55 us (4%)
  other arithmetic  5.55 us (3%)
    pallas_call x1, Pallas kernels, pairs(): pl.pallas_call(pairs_kernel, out_shape=(jax.ShapeDtypeStruct((2 * count *...  43.8 us
    ppermute x8, waiting for transfers between devices, total_over_devices(): lax.ppermute(value, AXES, [(i, i ^ step) for i in range(count)])  41.6 us
    ppermute x8, starting transfers between devices, total_over_devices(): lax.ppermute(value, AXES, [(i, i ^ step) for i in range(count)])  18.5 us
    pallas_call x3, Pallas kernels, project(): pl.pallas_call(functools.partial(project_kernel, tile=256), out_shape=jax...  16.2 us
    pallas_call x1, Pallas kernels, terms(): pl.pallas_call(functools.partial(terms_kernel, tile=tile, count=count, re...  10.8 us
    unnamed x18, local copies, waits for them, and re-layouts  9.53 us
    ppermute x5, waiting for transfers between devices, from_behind(): lax.ppermute(block, AXES, [((i - distance) % count, i) for i in range(cou...  8.74 us
    ppermute x5, starting transfers between devices, from_behind(): lax.ppermute(block, AXES, [((i - distance) % count, i) for i in range(cou...  5.72 us
  transfers between devices with their start and end apart: 13, of which 9 were waited for; matrix products, arithmetic and copies ran while one was open for 1% of the time, Pallas kernels for 10%

profile of v1, /device:TPU:2, one launch (start us, length us, event | category | flops | bytes accessed | tf_op | source)
XLA Modules:
  0.0 168.0 jit_solution(11799956308084244393)
XLA Ops:
  0.6 2.4 %collective-permute-start.2 = (bf16[4,128,1024]{2,1,0:T(8,128)(2,1)}, bf16[4,128,1024]{2,1,0:T(8,128)(2,1)S(1)}, u32[]{:S(2)}, u32[]{:S(2)}) collective-permute-start(bf16[4,128,1024]{2,1,0:T(8,128)(2,1)} %param.8), channel_id=1, source_target_pairs={{1,0},{2,1},{3,2},{4,3},{5,4},{6,5},{7,6},{8,7},{9,8},{10,9},{11,1... | collective-permute-start | bytes 3145736 | tf_op jit(solution)/shard_map/ppermute | solution.py:26
  3.0 0.0 collective-permute-start.1
  3.0 0.7 and_select_fusion
  3.7 0.7 pad_add_fusion
  4.4 1.3 collective-permute-start
  5.7 1.6 copy-done
  7.3 0.0 copy-start.2
  7.3 1.6 copy-done.2
  8.9 0.0 copy-start.4
  8.9 1.6 copy-done.4
  10.5 1.2 copy-done.6
  11.7 5.4 %project.4 = bf16[512,3072]{1,0:T(8,128)(2,1)S(1)} custom-call(bf16[512,1024]{1,0:T(8,128)(2,1)S(1)} %bitcast.6, bf16[1024,1024]{1,0:T(8,128)(2,1)S(1)} %copy-done, bf16[1024,1024]{1,0:T(8,128)(2,1)S(1)} %copy-done.2, bf16[1024,1024]{1,0:T(8,128)(2,1)S(1)} %copy-done.4), custom_call_target="tpu_custom_call" | custom-call | flops 3221225472 | bytes 14680064 | tf_op jit(solution)/shard_map/project/pallas_call | solution.py:44
  17.1 8.7 %collective-permute-done.2 = bf16[4,128,1024]{2,1,0:T(8,128)(2,1)S(1)} collective-permute-done((bf16[4,128,1024]{2,1,0:T(8,128)(2,1)}, bf16[4,128,1024]{2,1,0:T(8,128)(2,1)S(1)}, u32[]{:S(2)}, u32[]{:S(2)}) %collective-permute-start.2) | collective-permute-done | bytes 1048608 | tf_op jit(solution)/shard_map/ppermute | solution.py:26
  25.8 5.4 %project.5 = bf16[512,3072]{1,0:T(8,128)(2,1)S(1)} custom-call(bf16[512,1024]{1,0:T(8,128)(2,1)S(1)} %bitcast.8, bf16[1024,1024]{1,0:T(8,128)(2,1)S(1)} %copy-done, bf16[1024,1024]{1,0:T(8,128)(2,1)S(1)} %copy-done.2, bf16[1024,1024]{1,0:T(8,128)(2,1)S(1)} %copy-done.4), custom_call_target="tpu_custom_call" | custom-call | flops 3221225472 | bytes 14680064 | tf_op jit(solution)/shard_map/project/pallas_call | solution.py:44
  31.2 0.0 copy-start.7
  31.2 1.6 copy-done.7
  32.9 0.0 collective-permute-done.1
  32.9 0.0 copy-done.1
  32.9 5.4 %project.3 = bf16[512,3072]{1,0:T(8,128)(2,1)S(1)} custom-call(bf16[512,1024]{1,0:T(8,128)(2,1)S(1)} %bitcast.7, bf16[1024,1024]{1,0:T(8,128)(2,1)S(1)} %copy-done.1, bf16[1024,1024]{1,0:T(8,128)(2,1)S(1)} %copy-done.2, bf16[1024,1024]{1,0:T(8,128)(2,1)S(1)} %copy-done.4), custom_call_target="tpu_custom_call" | custom-call | flops 3221225472 | bytes 14680064 | tf_op jit(solution)/shard_map/project/pallas_call | solution.py:44
  38.3 0.0 collective-permute-done.info_ref
  38.3 0.0 copy-start.8
  38.3 1.9 %copy-done.8 = bf16[512,3072]{1,0:T(8,128)(2,1)S(1)} copy-done((bf16[512,3072]{1,0:T(8,128)(2,1)S(1)}, bf16[512,3072]{1,0:T(8,128)(2,1)}, u32[]{:S(2)}) %copy-start.8) | copy-done | bytes 3145752
  40.2 43.8 %pairs.1 = (bf16[1024,3072]{1,0:T(8,128)(2,1)}, f32[4]{0:T(128)S(1)}) custom-call(s32[16]{0:T(128)S(1)} %collective-permute-done.info_ref, bf16[4,128,3072]{2,1,0:T(8,128)(2,1)S(1)} %bitcast.11, bf16[4,128,3072]{2,1,0:T(8,128)(2,1)S(1)} %bitcast.9, bf16[4,128,3072]{2,1,0:T(8,128)(2,1)S(1)} %bitcast.10), custom_call_target="tpu_custom_call" | custom-call | flops 12884901888 | bytes 12582912 | tf_op jit(solution)/shard_map/pairs/pallas_call | solution.py:137
  84.0 0.0 copy-done.3
  84.0 0.0 copy-done.5
  84.0 10.8 %terms.1 = (bf16[4,128,1024]{2,1,0:T(8,128)(2,1)S(1)}, bf16[4,128,1024]{2,1,0:T(8,128)(2,1)S(1)}, bf16[4,128,1024]{2,1,0:T(8,128)(2,1)S(1)}) custom-call(s32[16]{0:T(128)S(1)} %collective-permute-done.info_ref, f32[4]{0:T(128)S(1)} %get-tuple-element.7.z_ref, bf16[1024,3072]{1,0:T(8,128)(2,1)} %get-tuple-element.8.g_ref, bf16[1024,1024]{1,0:T(8,128)(2,1)S(1)} %copy-done.1, ...), custom_call_target="tpu_custom_call" | custom-call | flops 6442450944 | bytes 20971520 | tf_op jit(solution)/shard_map/terms/pallas_call | solution.py:188
  94.8 0.4 collective-permute-start.11
  95.2 1.7 %collective-permute-start.12 = (bf16[4,128,1024]{2,1,0:T(8,128)(2,1)S(1)}, bf16[4,128,1024]{2,1,0:T(8,128)(2,1)}, u32[]{:S(2)}, u32[]{:S(2)}) collective-permute-start(bf16[4,128,1024]{2,1,0:T(8,128)(2,1)S(1)} %get-tuple-element.11), channel_id=1, source_target_pairs={{255,0},{0,1},{1,2},{2,3},{3,4},{4,5},{5,6},{6,7},{7,8},{8,9},{9,1... | collective-permute-start | bytes 3145736 | tf_op jit(solution)/shard_map/ppermute | solution.py:26
  96.9 0.7 fusion.3
  97.6 6.0 %collective-permute-start.3 = (f32[]{:T(128)}, f32[]{:T(128)}, u32[]{:S(2)}, u32[]{:S(2)}) collective-permute-start(f32[]{:T(128)} %fusion.3), channel_id=1, source_target_pairs={{0,1},{1,0},{2,3},{3,2},{4,5},{5,4},{6,7},{7,6},{8,9},{9,8},{10,11... | collective-permute-start | bytes 20 | tf_op jit(solution)/shard_map/ppermute | solution.py:205
  103.6 22.5 %collective-permute-done.3 = f32[]{:T(128)} collective-permute-done((f32[]{:T(128)}, f32[]{:T(128)}, u32[]{:S(2)}, u32[]{:S(2)}) %collective-permute-start.3) | collective-permute-done | bytes 36 | tf_op jit(solution)/shard_map/ppermute | solution.py:205
  127.4 1.4 collective-permute-start.4
  128.8 3.8 %collective-permute-done.4 = f32[]{:T(128)} collective-permute-done((f32[]{:T(128)}, f32[]{:T(128)}, u32[]{:S(2)}, u32[]{:S(2)}) %collective-permute-start.4) | collective-permute-done | bytes 36 | tf_op jit(solution)/shard_map/ppermute | solution.py:205
  133.3 1.4 collective-permute-start.5
  134.7 2.3 %collective-permute-done.5 = f32[]{:T(128)} collective-permute-done((f32[]{:T(128)}, f32[]{:T(128)}, u32[]{:S(2)}, u32[]{:S(2)}) %collective-permute-start.5) | collective-permute-done | bytes 36 | tf_op jit(solution)/shard_map/ppermute | solution.py:205
  137.7 1.4 collective-permute-start.6
  139.0 3.8 %collective-permute-done.6 = f32[]{:T(128)} collective-permute-done((f32[]{:T(128)}, f32[]{:T(128)}, u32[]{:S(2)}, u32[]{:S(2)}) %collective-permute-start.6) | collective-permute-done | bytes 36 | tf_op jit(solution)/shard_map/ppermute | solution.py:205
  143.5 1.0 collective-permute-start.7
  144.6 0.3 collective-permute-done.7
  145.5 1.4 collective-permute-start.8
  146.9 2.3 %collective-permute-done.8 = f32[]{:T(128)} collective-permute-done((f32[]{:T(128)}, f32[]{:T(128)}, u32[]{:S(2)}, u32[]{:S(2)}) %collective-permute-start.8) | collective-permute-done | bytes 36 | tf_op jit(solution)/shard_map/ppermute | solution.py:205
  149.8 1.4 collective-permute-start.9
  151.2 3.2 %collective-permute-done.9 = f32[]{:T(128)} collective-permute-done((f32[]{:T(128)}, f32[]{:T(128)}, u32[]{:S(2)}, u32[]{:S(2)}) %collective-permute-start.9) | collective-permute-done | bytes 36 | tf_op jit(solution)/shard_map/ppermute | solution.py:205
  155.1 4.5 %collective-permute-start.10 = (f32[]{:T(128)}, f32[]{:T(128)}, u32[]{:S(2)}, u32[]{:S(2)}) collective-permute-start(f32[]{:T(128)} %add.52), channel_id=1, source_target_pairs={{0,128},{1,129},{2,130},{3,131},{4,132},{5,133},{6,134},{7,135},{8... | collective-permute-start | bytes 20 | tf_op jit(solution)/shard_map/ppermute | solution.py:205
  159.6 3.2 %collective-permute-done.10 = f32[]{:T(128)} collective-permute-done((f32[]{:T(128)}, f32[]{:T(128)}, u32[]{:S(2)}, u32[]{:S(2)}) %collective-permute-start.10) | collective-permute-done | bytes 36 | tf_op jit(solution)/shard_map/ppermute | solution.py:205
  163.4 0.0 collective-permute-done.11
  163.4 0.0 collective-permute-done.12
  163.4 3.4 %convert_add_fusion = f32[4,128,1024]{2,1,0:T(8,128)} fusion(bf16[4,128,1024]{2,1,0:T(8,128)(2,1)} %collective-permute-done.12, bf16[4,128,1024]{2,1,0:T(8,128)(2,1)S(1)} %get-tuple-element.10, bf16[4,128,1024]{2,1,0:T(8,128)(2,1)} %collective-permute-done.11), kind=kLoop, calls=%fused_computation | loop fusion | flops 2621440 | bytes 5242880 | tf_op jit(solution)/shard_map/add | solution.py:237
  (5 shorter events, 0.0 us)
Async XLA Ops:
  0.6 25.2 %collective-permute-start.2 = (bf16[4,128,1024]{2,1,0:T(8,128)(2,1)}, bf16[4,128,1024]{2,1,0:T(8,128)(2,1)S(1)}, u32[]{:S(2)}, u32[]{:S(2)}) collective-permute-start(bf16[4,128,1024]{2,1,0:T(8,128)(2,1)} %param.8), channel_id=1, source_target_pairs={{1,0},{2,1},{3,2},{4,3},{5,4},{6,5},{7,6},{8,7},{9,8},{10,9},{11,1... | collective-permute-start | bytes 3145736 | tf_op jit(solution)/shard_map/ppermute | solution.py:26
  3.0 29.9 %collective-permute-start.1 = (bf16[4,128,1024]{2,1,0:T(8,128)(2,1)}, bf16[4,128,1024]{2,1,0:T(8,128)(2,1)S(1)}, u32[]{:S(2)}, u32[]{:S(2)}) collective-permute-start(bf16[4,128,1024]{2,1,0:T(8,128)(2,1)} %param.8), channel_id=1, source_target_pairs={{255,0},{0,1},{1,2},{2,3},{3,4},{4,5},{5,6},{6,7},{7,8},{8,9},{9,1... | collective-permute-start | bytes 3145736 | tf_op jit(solution)/shard_map/ppermute | solution.py:26
  4.4 33.9 %collective-permute-start = (s32[16]{0:T(128)S(1)}, s32[16]{0:T(128)S(1)}, u32[]{:S(2)}, u32[]{:S(2)}) collective-permute-start(s32[16]{0:T(128)S(1)} %pad_add_fusion), channel_id=1, source_target_pairs={{255,0},{0,1},{1,2},{2,3},{3,4},{4,5},{5,6},{6,7},{7,8},{8,9},{9,1... | collective-permute-start | bytes 200 | tf_op jit(solution)/shard_map/ppermute | solution.py:26
  5.7 1.6 copy-start
  7.3 1.6 copy-start.2
  8.9 1.6 copy-start.4
  10.4 1.2 copy-start.6
  25.8 7.1 %copy-start.1 = (bf16[1024,1024]{1,0:T(8,128)(2,1)S(1)}, bf16[1024,1024]{1,0:T(8,128)(2,1)}, u32[]{:S(2)}) copy-start(bf16[1024,1024]{1,0:T(8,128)(2,1)} %wq_ref.7) | copy-start | bytes 6291460
  31.2 1.6 copy-start.7
  38.3 1.9 %copy-start.8 = (bf16[512,3072]{1,0:T(8,128)(2,1)S(1)}, bf16[512,3072]{1,0:T(8,128)(2,1)}, u32[]{:S(2)}) copy-start(bf16[512,3072]{1,0:T(8,128)(2,1)} %copy-done.7) | copy-start | bytes 9437188
  40.2 43.8 %copy-start.3 = (bf16[1024,1024]{1,0:T(8,128)(2,1)S(1)}, bf16[1024,1024]{1,0:T(8,128)(2,1)}, u32[]{:S(2)}) copy-start(bf16[1024,1024]{1,0:T(8,128)(2,1)} %wk_ref.7) | copy-start | bytes 6291460
  40.2 43.8 %copy-start.5 = (bf16[1024,1024]{1,0:T(8,128)(2,1)S(1)}, bf16[1024,1024]{1,0:T(8,128)(2,1)}, u32[]{:S(2)}) copy-start(bf16[1024,1024]{1,0:T(8,128)(2,1)} %wv_ref.7) | copy-start | bytes 6291460
  94.8 68.5 %collective-permute-start.11 = (bf16[4,128,1024]{2,1,0:T(8,128)(2,1)S(1)}, bf16[4,128,1024]{2,1,0:T(8,128)(2,1)}, u32[]{:S(2)}, u32[]{:S(2)}) collective-permute-start(bf16[4,128,1024]{2,1,0:T(8,128)(2,1)S(1)} %get-tuple-element.9), channel_id=1, source_target_pairs={{1,0},{2,1},{3,2},{4,3},{5,4},{6,5},{7,6},{8,7},{9,8},{10,9},{11,1... | collective-permute-start | bytes 3145736 | tf_op jit(solution)/shard_map/ppermute | solution.py:26
  95.2 68.2 %collective-permute-start.12 = (bf16[4,128,1024]{2,1,0:T(8,128)(2,1)S(1)}, bf16[4,128,1024]{2,1,0:T(8,128)(2,1)}, u32[]{:S(2)}, u32[]{:S(2)}) collective-permute-start(bf16[4,128,1024]{2,1,0:T(8,128)(2,1)S(1)} %get-tuple-element.11), channel_id=1, source_target_pairs={{255,0},{0,1},{1,2},{2,3},{3,4},{4,5},{5,6},{6,7},{7,8},{8,9},{9,1... | collective-permute-start | bytes 3145736 | tf_op jit(solution)/shard_map/ppermute | solution.py:26
  97.6 28.5 %collective-permute-start.3 = (f32[]{:T(128)}, f32[]{:T(128)}, u32[]{:S(2)}, u32[]{:S(2)}) collective-permute-start(f32[]{:T(128)} %fusion.3), channel_id=1, source_target_pairs={{0,1},{1,0},{2,3},{3,2},{4,5},{5,4},{6,7},{7,6},{8,9},{9,8},{10,11... | collective-permute-start | bytes 20 | tf_op jit(solution)/shard_map/ppermute | solution.py:205
  127.4 5.2 %collective-permute-start.4 = (f32[]{:T(128)}, f32[]{:T(128)}, u32[]{:S(2)}, u32[]{:S(2)}) collective-permute-start(f32[]{:T(128)} %add.46), channel_id=1, source_target_pairs={{0,2},{1,3},{2,0},{3,1},{4,6},{5,7},{6,4},{7,5},{8,10},{9,11},{10,... | collective-permute-start | bytes 20 | tf_op jit(solution)/shard_map/ppermute | solution.py:205
  133.3 3.7 %collective-permute-start.5 = (f32[]{:T(128)}, f32[]{:T(128)}, u32[]{:S(2)}, u32[]{:S(2)}) collective-permute-start(f32[]{:T(128)} %add.47), channel_id=1, source_target_pairs={{0,4},{1,5},{2,6},{3,7},{4,0},{5,1},{6,2},{7,3},{8,12},{9,13},{10,... | collective-permute-start | bytes 20 | tf_op jit(solution)/shard_map/ppermute | solution.py:205
  137.7 5.2 %collective-permute-start.6 = (f32[]{:T(128)}, f32[]{:T(128)}, u32[]{:S(2)}, u32[]{:S(2)}) collective-permute-start(f32[]{:T(128)} %add.48), channel_id=1, source_target_pairs={{0,8},{1,9},{2,10},{3,11},{4,12},{5,13},{6,14},{7,15},{8,0},{9,1},... | collective-permute-start | bytes 20 | tf_op jit(solution)/shard_map/ppermute | solution.py:205
  143.5 1.3 collective-permute-start.7
  145.5 3.7 %collective-permute-start.8 = (f32[]{:T(128)}, f32[]{:T(128)}, u32[]{:S(2)}, u32[]{:S(2)}) collective-permute-start(f32[]{:T(128)} %add.50), channel_id=1, source_target_pairs={{0,32},{1,33},{2,34},{3,35},{4,36},{5,37},{6,38},{7,39},{8,40},{9,... | collective-permute-start | bytes 20 | tf_op jit(solution)/shard_map/ppermute | solution.py:205
  149.8 4.6 %collective-permute-start.9 = (f32[]{:T(128)}, f32[]{:T(128)}, u32[]{:S(2)}, u32[]{:S(2)}) collective-permute-start(f32[]{:T(128)} %add.51), channel_id=1, source_target_pairs={{0,64},{1,65},{2,66},{3,67},{4,68},{5,69},{6,70},{7,71},{8,72},{9,... | collective-permute-start | bytes 20 | tf_op jit(solution)/shard_map/ppermute | solution.py:205
  155.1 7.6 %collective-permute-start.10 = (f32[]{:T(128)}, f32[]{:T(128)}, u32[]{:S(2)}, u32[]{:S(2)}) collective-permute-start(f32[]{:T(128)} %add.52), channel_id=1, source_target_pairs={{0,128},{1,129},{2,130},{3,131},{4,132},{5,133},{6,134},{7,135},{8... | collective-permute-start | bytes 20 | tf_op jit(solution)/shard_map/ppermute | solution.py:205

commit v2 on v0

v2 whole, which is shorter than its diff:
```python
import functools

import jax
import jax.numpy as jnp
from jax import lax
from jax.experimental import pallas as pl
from jax.experimental.pallas import tpu as pltpu
from jax.sharding import PartitionSpec as P

AXES = ("dp", "mp")
LATE = 1
LOG2_E = 1.4426950408889634
NT = (((1,), (1,)), ((), ()))
TN = (((0,), (0,)), ((), ()))
VMEM = pl.BlockSpec(memory_space=pltpu.VMEM)
SMEM = pl.BlockSpec(memory_space=pltpu.SMEM)
ANY = pl.BlockSpec(memory_space=pl.ANY)


def mm(a, b, dims=(((1,), (0,)), ((), ()))):
    return lax.dot_general(a, b, dims, preferred_element_type=jnp.float32)


def from_behind(block, distance):
    count = lax.axis_size(AXES)
    return lax.ppermute(block, AXES, [((i - distance) % count, i) for i in range(count)])


def project_kernel(*refs):
    blocks = (len(refs) - 3) // 2
    xs, weights, outs = refs[:blocks], refs[blocks : blocks + 3], refs[blocks + 3 :]
    for n, w_ref in enumerate(weights):
        for x_ref, out_ref in zip(xs, outs):
            recs, seq, width = x_ref.shape
            made = mm(x_ref[...].reshape(recs * seq, width), w_ref[...])
            out_ref[:, :, n * width : (n + 1) * width] = made.astype(jnp.bfloat16).reshape(recs, seq, width)


def project(blocks, weights):
    rows = sum(block.shape[0] * block.shape[1] for block in blocks)
    width = blocks[0].shape[2]
    return pl.pallas_call(
        project_kernel,
        out_shape=[jax.ShapeDtypeStruct(block.shape[:2] + (3 * width,), jnp.bfloat16) for block in blocks],
        in_specs=[VMEM] * (len(blocks) + 3),
        out_specs=[VMEM] * len(blocks),
        compiler_params=pltpu.CompilerParams(vmem_limit_bytes=18 << 20),
        cost_estimate=pl.CostEstimate(flops=6 * rows * width * width, bytes_accessed=14 << 20, transcendentals=0),
        name="project",
    )(*blocks, *weights)


def pairs_kernel(
    info_ref, left_ref, own_ref, right_ref, left_x, right_x, wq_ref, wk_ref, wv_ref, grads_ref, z_ref, win, sems, *, count
):
    total, seq, full = win.shape
    recs, early, late = own_ref.shape[0], left_ref.shape[0], left_x.shape[0]
    width = full // 3
    copies = [
        pltpu.make_async_copy(ref, win.at[pl.ds(start, ref.shape[0])], sems.at[n])
        for n, (ref, start) in enumerate(((left_ref, 0), (own_ref, recs), (right_ref, 2 * recs)))
    ]
    for copy in copies:
        copy.start()
    rows = late * seq
    x = jnp.concatenate([left_x[...].reshape(rows, width), right_x[...].reshape(rows, width)], axis=0)
    for n, w_ref in enumerate((wq_ref, wk_ref, wv_ref)):
        made = mm(x, w_ref[...]).astype(jnp.bfloat16)
        at = slice(n * width, (n + 1) * width)
        win[early:recs, :, at] = made[:rows].reshape(late, seq, width)
        win[2 * recs + early :, :, at] = made[rows:].reshape(late, seq, width)

    lane = lax.broadcasted_iota(jnp.int32, (seq, 128), 1)
    first = lane < 64
    row = lax.broadcasted_iota(jnp.int32, (2 * seq, 128), 0)
    col = lax.broadcasted_iota(jnp.int32, (2 * seq, 128), 1)
    ends = jnp.where((row < seq) == (col < 64), 1.0, 0.0).astype(jnp.bfloat16)
    zero = jnp.zeros((seq, 128), jnp.bfloat16)
    for copy in copies:
        copy.wait()

    def one_pair(p, _):
        a, b = info_ref[p], info_ref[count + p]
        jobs = []
        for i in range(width // 128):
            at = [slice(n * width + i * 128, n * width + (i + 1) * 128) for n in range(3)]
            qa, ka, va = (win[a, :, s] for s in at)
            qb, kb, vb = (win[b, :, s] for s in at)
            jobs.append((at, 0, count, qa, kb, vb))
            jobs.append((at, count, 0, qb, ka, va))
        qs = [
            jnp.concatenate([jnp.where(first, job[3], zero), jnp.where(first, zero, job[3])], axis=0) for job in jobs
        ]
        scores = [mm(job[4], q, NT) for job, q in zip(jobs, qs)]
        probs = []
        for s in scores:
            top = jnp.max(s, axis=0, keepdims=True)
            e = jnp.exp2((s - top) * (LOG2_E / 8.0))
            probs.append(e * (1.0 / jnp.sum(e, axis=0, keepdims=True)))
        mass = [mm(prob.astype(jnp.bfloat16), ends) for prob in probs]
        pooled = [
            jnp.sum(m * job[5].astype(jnp.float32), axis=0, keepdims=True) * (1.0 / seq) for m, job in zip(mass, jobs)
        ]
        z = jnp.zeros((1, 128), jnp.float32)
        for i in range(width // 128):
            z = z + pooled[2 * i] * pooled[2 * i + 1]
        z_ref[p] = 4.0 * jnp.sum(z)
        dps = [pooled[n ^ 1] * (4.0 / seq) for n in range(len(jobs))]
        ts = [
            mm((job[5].astype(jnp.float32) * (dp * 0.125)).astype(jnp.bfloat16), ends, NT)
            for dp, job in zip(dps, jobs)
        ]
        dss = []
        for prob, t in zip(probs, ts):
            r = jnp.sum(prob * t, axis=0, keepdims=True)
            dss.append((prob * (t - r)).astype(jnp.bfloat16))
        dks = [mm(ds, q) for ds, q in zip(dss, qs)]
        dqs = [mm(ds, job[4], TN) for ds, job in zip(dss, jobs)]
        for n, (at, qrow, krow, _, _, _) in enumerate(jobs):
            grads_ref[krow + p, :, at[2]] = (mass[n] * dps[n]).astype(jnp.bfloat16)
            grads_ref[krow + p, :, at[1]] = dks[n].astype(jnp.bfloat16)
            grads_ref[qrow + p, :, at[0]] = jnp.where(first, dqs[n][:seq], dqs[n][seq:]).astype(jnp.bfloat16)
        return 0

    lax.fori_loop(0, count, one_pair, 0)


def pairs(info, left, own, right, left_x, right_x, weights, count):
    recs, seq, full = own.shape
    return pl.pallas_call(
        functools.partial(pairs_kernel, count=count),
        out_shape=(
            jax.ShapeDtypeStruct((2 * count, seq, full), jnp.bfloat16),
            jax.ShapeDtypeStruct((count,), jnp.float32),
        ),
        in_specs=[SMEM, ANY, ANY, ANY] + [VMEM] * 5,
        out_specs=(VMEM, SMEM),
        scratch_shapes=[pltpu.VMEM((3 * recs, seq, full), jnp.bfloat16), pltpu.SemaphoreType.DMA((3,))],
        compiler_params=pltpu.CompilerParams(vmem_limit_bytes=28 << 20),
        cost_estimate=pl.CostEstimate(flops=12 << 30, bytes_accessed=12 << 20, transcendentals=2 << 20),
        name="pairs",
    )(info, left, own, right, left_x, right_x, *weights)


def terms_kernel(
    info_ref, z_ref, g_ref, wq_ref, wk_ref, wv_ref, left_ref, own_ref, right_ref, acc, *, columns, count, recs
):
    _, seq, full = g_ref.shape
    width = full // 3
    made = None
    for n, w_ref in enumerate((wq_ref, wk_ref, wv_ref)):
        grads = g_ref[:, :, n * width : (n + 1) * width].reshape(2 * count * seq, width)
        part = mm(grads, w_ref[columns, :], NT)
        made = part if made is None else made + part
    acc[...] = jnp.zeros_like(acc)
    for n in range(2 * count):
        p = n % count
        z = jnp.full((8, 128), z_ref[p], jnp.float32)
        c = info_ref[2 * count + p].astype(jnp.float32) * (1.0 / 256.0)
        y = info_ref[3 * count + p].astype(jnp.float32)
        g = (seq * c * (jax.nn.sigmoid(z) - y))[0:1, 0:1]
        acc[info_ref[n]] += made[n * seq : (n + 1) * seq] * g
    for n, out in enumerate((left_ref, own_ref, right_ref)):
        out[...] = acc[n * recs : (n + 1) * recs].astype(jnp.bfloat16)


def terms(info, z, grads, weights, recs, count, columns):
    _, seq, full = grads.shape
    size = columns.stop - columns.start
    made = jax.ShapeDtypeStruct((recs, seq, size), jnp.bfloat16)
    return pl.pallas_call(
        functools.partial(terms_kernel, columns=columns, count=count, recs=recs),
        out_shape=(made, made, made),
        in_specs=[SMEM, SMEM] + [VMEM] * 4,
        out_specs=(VMEM,) * 3,
        scratch_shapes=[pltpu.VMEM((3 * recs, seq, size), jnp.float32)],
        compiler_params=pltpu.CompilerParams(vmem_limit_bytes=18 << 20),
        cost_estimate=pl.CostEstimate(
            flops=4 * count * seq * full * size, bytes_accessed=12 << 20, transcendentals=0
        ),
        name="terms",
    )(info, z, grads, *weights)


def swap(value, step):
    return value + lax.ppermute(value, AXES, [(i, i ^ step) for i in range(lax.axis_size(AXES))])


def on_device(records, w_query, w_key, w_value, pair_owner, pair_partner, confidence, labels):
    recs, seq, width = records.shape
    count = pair_owner.shape[0]
    devices = lax.axis_size(AXES)
    first_id = lax.axis_index(AXES) * recs
    weights = (w_query, w_key, w_value)
    early = recs - LATE

    left_early, right_early = (from_behind(records[:early], d) for d in (1, -1))
    left_late, right_late = (from_behind(records[early:], d) for d in (1, -1))
    own_info = jnp.concatenate(
        [pair_owner - first_id, jnp.mod(pair_partner - first_id, recs * devices), confidence, labels]
    )
    info = from_behind(own_info, 1)
    (own,) = project([records], weights)
    left, right = project([left_early, right_early], weights)
    grads, z = pairs(info, left, own, right, left_late, right_late, weights, count)

    c = info[2 * count : 3 * count].astype(jnp.float32) / 256.0
    y = info[3 * count :].astype(jnp.float32)
    loss = jnp.sum(c * (jax.nn.softplus(z) - y * z))
    z, loss = lax.optimization_barrier((z, loss))
    half = width // 2
    loss = swap(loss, 1)
    to_left, kept_a, to_right = terms(info, z, grads, weights, recs, count, slice(0, half))
    to_left, to_right, z, loss = lax.optimization_barrier((to_left, to_right, z, loss))
    loss = swap(loss, 2)
    from_right_a, from_left_a = from_behind(to_left, -1), from_behind(to_right, 1)
    to_left, kept_b, to_right = terms(info, z, grads, weights, recs, count, slice(half, width))
    to_left, to_right, loss = lax.optimization_barrier((to_left, to_right, loss))
    from_right_b, from_left_b = from_behind(to_left, -1), from_behind(to_right, 1)
    step = devices // 2
    while step > 2:
        loss = swap(loss, step)
        step //= 2
    loss = loss / (count * devices)

    def added(first, second, third):
        return first.astype(jnp.float32) + second.astype(jnp.float32) + third.astype(jnp.float32)

    record_grad = jnp.concatenate(
        [added(from_right_a, kept_a, from_left_a), added(from_right_b, kept_b, from_left_b)], axis=2
    )
    return (loss, record_grad)


def solution(mesh):
    blocks = P(AXES, None, None)
    in_specs = (blocks, P(), P(), P(), P(AXES), P(AXES), P(AXES), P(AXES))
    return jax.shard_map(
        on_device, mesh=mesh, in_specs=in_specs, out_specs=(P(), blocks), check_vma=False
    )
```

time: 347 us -> 118 us (0.34); the launches traced: 341 us -> 117 us
  blocking collectives: 103 us -> 0 us
  matrix products: 53.6 us -> 0 us
  waiting for transfers between devices: 56.8 us -> 17.8 us
  Pallas kernels: 0 us -> 31.1 us
  local copies, waits for them, and re-layouts: 40.8 us -> 15.9 us
  starting transfers between devices: 62.6 us -> 41.2 us
  other arithmetic: 20.8 us -> 3.95 us
  between operations: 3.06 us -> 7.42 us
    psum x1 -> x0, blocking collectives: 103 us -> none  [on_device(): loss = lax.psum(loss_local, ('dp', 'mp')) / (pair_owner.shape[0] * devices)]
    dot_general x21 -> x0, matrix products: 43.3 us -> none  [the longest x3 8.79 us: project(): out = jnp.dot(flat_rows, weight, preferred_element_type=jnp.float32)]
    ppermute x8 -> x17, waiting for transfers between devices: 56.8 us -> 17.8 us  [the longest x9 11.4 us: from_behind(): lax.ppermute(block, AXES, [((i - distance) % count, i) for i in range(cou...]
    pallas_call x0 -> x5, Pallas kernels: none -> 31.1 us  [the longest x1 12.3 us: pairs(): pl.pallas_call(functools.partial(pairs_kernel, count=count), out_shape=(j...]
    gather x12 -> x0, local copies, waits for them, and re-layouts: 30 us -> none  [the longest x2 5.76 us: on_device(): part_k = jnp.concatenate([item[1] for item in window], axis=0)[partner_slot]]
    ppermute x8 -> x17, starting transfers between devices: 62.6 us -> 41.2 us  [the longest x8 22.4 us: swap(): lax.ppermute(value, AXES, [(i, i ^ step) for i in range(lax.axis_size(AXE...]
    sub x2 -> x0, matrix products: 10.3 us -> none  [attend(): chance = jax.nn.softmax(scores, axis=-1).astype(jnp.bfloat16)]
    unnamed x35 -> x32, local copies, waits for them, and re-layouts: 3.24 us -> 12 us
  transfers between devices with their start and end apart: 8 -> 17, of which waited for: 4 -> 7; matrix products, arithmetic and copies ran while one was open for 10% -> 3% of each run, Pallas kernels for 0% -> 16%
where the time goes in v2:
time: 118 us; the launch traced here: 117 us
  starting transfers between devices  41.2 us (35%)
  Pallas kernels  31.1 us (26%)
  waiting for transfers between devices  17.8 us (15%)
  local copies, waits for them, and re-layouts  15.9 us (13%)
  between operations  7.42 us (6%)
  other arithmetic  3.95 us (3%)
    ppermute x8, starting transfers between devices, swap(): lax.ppermute(value, AXES, [(i, i ^ step) for i in range(lax.axis_size(AXE...  22.4 us
    ppermute x9, starting transfers between devices, from_behind(): lax.ppermute(block, AXES, [((i - distance) % count, i) for i in range(cou...  18.8 us
    pallas_call x1, Pallas kernels, pairs(): pl.pallas_call(functools.partial(pairs_kernel, count=count), out_shape=(j...  12.3 us
    unnamed x32, local copies, waits for them, and re-layouts  12 us
    ppermute x9, waiting for transfers between devices, from_behind(): lax.ppermute(block, AXES, [((i - distance) % count, i) for i in range(cou...  11.4 us
    pallas_call x2, Pallas kernels, project(): pl.pallas_call(project_kernel, out_shape=[jax.ShapeDtypeStruct(block.shap...  9.6 us
    pallas_call x2, Pallas kernels, terms(): pl.pallas_call(functools.partial(terms_kernel, columns=columns, count=cou...  9.21 us
    ppermute x8, waiting for transfers between devices, swap(): lax.ppermute(value, AXES, [(i, i ^ step) for i in range(lax.axis_size(AXE...  6.43 us
  transfers between devices with their start and end apart: 17, of which 7 were waited for; matrix products, arithmetic and copies ran while one was open for 3% of the time, Pallas kernels for 16%

profile of v2, /device:TPU:1, one launch (start us, length us, event | category | flops | bytes accessed | tf_op | source)
XLA Modules:
  0.0 117.3 jit_solution(4683958415009584112)
XLA Ops:
  0.7 2.2 %slice.14 = bf16[3,128,1024]{2,1,0:T(8,128)(2,1)} slice(bf16[4,128,1024]{2,1,0:T(8,128)(2,1)} %refs_0_.1), slice={[0:3], [0:128], [0:1024]} | slice | bytes 1572864 | tf_op jit(solution)/shard_map/slice | solution.py:197
  2.9 6.3 %collective-permute-start.2 = (bf16[3,128,1024]{2,1,0:T(8,128)(2,1)}, bf16[3,128,1024]{2,1,0:T(8,128)(2,1)S(1)}, u32[]{:S(2)}, u32[]{:S(2)}) collective-permute-start(bf16[3,128,1024]{2,1,0:T(8,128)(2,1)} %slice.14), channel_id=1, source_target_pairs={{1,0},{2,1},{3,2},{4,3},{5,4},{6,5},{7,6},{8,7},{9,8},{10,9},{11,1... | collective-permute-start | bytes 2359304 | tf_op jit(solution)/shard_map/ppermute | solution.py:26
  9.2 1.7 %slice.15 = bf16[1,128,1024]{2,1,0:T(8,128)(2,1)} slice(bf16[4,128,1024]{2,1,0:T(8,128)(2,1)} %refs_0_.1), slice={[3:4], [0:128], [0:1024]} | slice | bytes 524288 | tf_op jit(solution)/shard_map/slice | solution.py:198
  10.9 5.1 %collective-permute-start.4 = (bf16[1,128,1024]{2,1,0:T(8,128)(2,1)}, bf16[1,128,1024]{2,1,0:T(8,128)(2,1)S(1)}, u32[]{:S(2)}, u32[]{:S(2)}) collective-permute-start(bf16[1,128,1024]{2,1,0:T(8,128)(2,1)} %slice.15), channel_id=1, source_target_pairs={{1,0},{2,1},{3,2},{4,3},{5,4},{6,5},{7,6},{8,7},{9,8},{10,9},{11,1... | collective-permute-start | bytes 786440 | tf_op jit(solution)/shard_map/ppermute | solution.py:26
  16.0 0.0 collective-permute-start.3
  16.0 0.1 pad_add_fusion
  16.1 0.2 collective-permute-start
  16.3 0.0 copy-start.3
  16.3 1.6 %copy-done.3 = bf16[1024,1024]{1,0:T(8,128)(2,1)S(1)} copy-done((bf16[1024,1024]{1,0:T(8,128)(2,1)S(1)}, bf16[1024,1024]{1,0:T(8,128)(2,1)}, u32[]{:S(2)}) %copy-start.3) | copy-done | bytes 2097176
  17.9 1.6 %copy-done.6 = bf16[1024,1024]{1,0:T(8,128)(2,1)S(1)} copy-done((bf16[1024,1024]{1,0:T(8,128)(2,1)S(1)}, bf16[1024,1024]{1,0:T(8,128)(2,1)}, u32[]{:S(2)}) %copy-start.6) | copy-done | bytes 2097176
  19.5 1.2 %copy-done.9 = bf16[4,128,1024]{2,1,0:T(8,128)(2,1)S(1)} copy-done((bf16[4,128,1024]{2,1,0:T(8,128)(2,1)S(1)}, bf16[4,128,1024]{2,1,0:T(8,128)(2,1)}, u32[]{:S(2)}) %copy-start.9) | copy-done | bytes 1048600
  20.7 3.4 %project.3.own_ref = bf16[4,128,3072]{2,1,0:T(8,128)(2,1)S(1)} custom-call(bf16[4,128,1024]{2,1,0:T(8,128)(2,1)S(1)} %copy-done.9, bf16[1024,1024]{1,0:T(8,128)(2,1)S(1)} %copy-done.2, bf16[1024,1024]{1,0:T(8,128)(2,1)S(1)} %copy-done.3, bf16[1024,1024]{1,0:T(8,128)(2,1)S(1)} %copy-done.6), custom_call_target="tpu_custom_call" | custom-call | flops 3221225472 | bytes 14680064 | tf_op jit(solution)/shard_map/project/pallas_call | solution.py:42
  24.2 0.0 copy-start.7
  24.2 5.5 %collective-permute-done.2.refs_1_ = bf16[3,128,1024]{2,1,0:T(8,128)(2,1)S(1)} collective-permute-done((bf16[3,128,1024]{2,1,0:T(8,128)(2,1)}, bf16[3,128,1024]{2,1,0:T(8,128)(2,1)S(1)}, u32[]{:S(2)}, u32[]{:S(2)}) %collective-permute-start.2) | collective-permute-done | bytes 786464 | tf_op jit(solution)/shard_map/ppermute | solution.py:26
  29.7 5.8 %collective-permute-done.1.refs_0_ = bf16[3,128,1024]{2,1,0:T(8,128)(2,1)} collective-permute-done((bf16[3,128,1024]{2,1,0:T(8,128)(2,1)}, bf16[3,128,1024]{2,1,0:T(8,128)(2,1)}, u32[]{:S(2)}, u32[]{:S(2)}) %collective-permute-start.1) | collective-permute-done | bytes 786464 | tf_op jit(solution)/shard_map/ppermute | solution.py:26
  35.5 6.2 %project.2 = (bf16[3,128,3072]{2,1,0:T(8,128)(2,1)S(1)}, bf16[3,128,3072]{2,1,0:T(8,128)(2,1)S(1)}) custom-call(bf16[3,128,1024]{2,1,0:T(8,128)(2,1)} %collective-permute-done.1.refs_0_, bf16[3,128,1024]{2,1,0:T(8,128)(2,1)S(1)} %collective-permute-done.2.refs_1_, bf16[1024,1024]{1,0:T(8,128)(2,1)S(1)} %copy-done.2, bf16[1024,1024]{1,0:T(8,128)(2,1)S(1)} %copy-done.4, ...), custom_call_target="tpu_custom_call" | custom-call | flops 4831838208 | bytes 14680064 | tf_op jit(solution)/shard_map/project/pallas_call | solution.py:42
  41.7 0.0 collective-permute-done.info_ref
  41.7 0.0 collective-permute-done.4.right_x
  41.7 12.3 %pairs.1 = (bf16[8,128,3072]{2,1,0:T(8,128)(2,1)S(1)}, f32[4]{0:T(128)S(1)}) custom-call(s32[16]{0:T(128)S(1)} %collective-permute-done.info_ref, bf16[3,128,3072]{2,1,0:T(8,128)(2,1)S(1)} %get-tuple-element.21.left_ref, bf16[4,128,3072]{2,1,0:T(8,128)(2,1)S(1)} %project.3.own_ref, bf16[3,128,3072]{2,1,0:T(8,128)(2,1)S(1)} %get-tuple-element.22.right_ref, ...), custom_call_target="tpu_custom_call" | custom-call | flops 12884901888 | bytes 12582912 | tf_op jit(solution)/shard_map/pairs/pallas_call | solution.py:130
  54.0 0.8 fusion.3
  54.8 0.0 collective-permute-start.5
  54.8 5.0 %terms.2 = (bf16[4,128,512]{2,1,0:T(8,128)(2,1)}, bf16[4,128,512]{2,1,0:T(8,128)(2,1)S(1)}, bf16[4,128,512]{2,1,0:T(8,128)(2,1)}) custom-call(s32[16]{0:T(128)S(1)} %collective-permute-done.info_ref, f32[4]{0:T(128)S(1)} %get-tuple-element.29.z_ref, bf16[8,128,3072]{2,1,0:T(8,128)(2,1)S(1)} %get-tuple-element.25.g_ref, bf16[1024,1024]{1,0:T(8,128)(2,1)S(1)} %copy-done.2, ...), custom_call_target="tpu_custom_call" | custom-call | flops 3221225472 | bytes 12582912 | tf_op jit(solution)/shard_map/terms/pallas_call | solution.py:171
  61.2 0.8 collective-permute-start.6
  62.0 2.0 %collective-permute-start.13 = (bf16[4,128,512]{2,1,0:T(8,128)(2,1)}, bf16[4,128,512]{2,1,0:T(8,128)(2,1)}, u32[]{:S(2)}, u32[]{:S(2)}) collective-permute-start(bf16[4,128,512]{2,1,0:T(8,128)(2,1)} %get-tuple-element.34), channel_id=1, source_target_pairs={{1,0},{2,1},{3,2},{4,3},{5,4},{6,5},{7,6},{8,7},{9,8},{10,9},{11,1... | collective-permute-start | bytes 1572872 | tf_op jit(solution)/shard_map/ppermute | solution.py:26
  64.1 2.8 %copy-done.1 = bf16[8,128,3072]{2,1,0:T(8,128)(2,1)S(1)} copy-done((bf16[8,128,3072]{2,1,0:T(8,128)(2,1)S(1)}, bf16[8,128,3072]{2,1,0:T(8,128)(2,1)}, u32[]{:S(2)}) %copy-start.1) | copy-done | bytes 6291480
  66.9 1.6 %copy-done.5 = bf16[1024,1024]{1,0:T(8,128)(2,1)S(1)} copy-done((bf16[1024,1024]{1,0:T(8,128)(2,1)S(1)}, bf16[1024,1024]{1,0:T(8,128)(2,1)}, u32[]{:S(2)}) %copy-start.5) | copy-done | bytes 2097176
  68.4 1.6 %copy-done.8 = bf16[1024,1024]{1,0:T(8,128)(2,1)S(1)} copy-done((bf16[1024,1024]{1,0:T(8,128)(2,1)S(1)}, bf16[1024,1024]{1,0:T(8,128)(2,1)}, u32[]{:S(2)}) %copy-start.8) | copy-done | bytes 2097176
  70.0 4.2 %terms.3 = (bf16[4,128,512]{2,1,0:T(8,128)(2,1)S(1)}, bf16[4,128,512]{2,1,0:T(8,128)(2,1)S(1)}, bf16[4,128,512]{2,1,0:T(8,128)(2,1)S(1)}) custom-call(s32[16]{0:T(128)S(1)} %collective-permute-done.info_ref, f32[4]{0:T(128)S(1)} %get-tuple-element.29.z_ref, bf16[8,128,3072]{2,1,0:T(8,128)(2,1)S(1)} %copy-done.1, bf16[1024,1024]{1,0:T(8,128)(2,1)S(1)} %copy-done.2, ...), custom_call_target="tpu_custom_call" | custom-call | flops 3221225472 | bytes 12582912 | tf_op jit(solution)/shard_map/terms/pallas_call | solution.py:171
  74.2 0.0 copy-start.10
  74.2 0.8 copy-done.10
  75.0 0.8 copy-done.11
  76.5 5.1 %collective-permute-start.15 = (bf16[4,128,512]{2,1,0:T(8,128)(2,1)}, bf16[4,128,512]{2,1,0:T(8,128)(2,1)S(1)}, u32[]{:S(2)}, u32[]{:S(2)}) collective-permute-start(bf16[4,128,512]{2,1,0:T(8,128)(2,1)} %copy-done.11), channel_id=1, source_target_pairs={{1,0},{2,1},{3,2},{4,3},{5,4},{6,5},{7,6},{8,7},{9,8},{10,9},{11,1... | collective-permute-start | bytes 1572872 | tf_op jit(solution)/shard_map/ppermute | solution.py:26
  81.6 0.0 collective-permute-start.16
  81.6 7.6 %collective-permute-start.7 = (f32[]{:T(128)}, f32[]{:T(128)}, u32[]{:S(2)}, u32[]{:S(2)}) collective-permute-start(f32[]{:T(128)} %add.53), channel_id=1, source_target_pairs={{0,128},{1,129},{2,130},{3,131},{4,132},{5,133},{6,134},{7,135},{8... | collective-permute-start | bytes 20 | tf_op jit(solution)/shard_map/ppermute | solution.py:186
  89.2 0.2 collective-permute-done.7
  90.0 2.6 %collective-permute-start.8 = (f32[]{:T(128)}, f32[]{:T(128)}, u32[]{:S(2)}, u32[]{:S(2)}) collective-permute-start(f32[]{:T(128)} %add.54), channel_id=1, source_target_pairs={{0,64},{1,65},{2,66},{3,67},{4,68},{5,69},{6,70},{7,71},{8,72},{9,... | collective-permute-start | bytes 20 | tf_op jit(solution)/shard_map/ppermute | solution.py:186
  92.6 0.7 collective-permute-done.8
  93.9 2.0 %collective-permute-start.9 = (f32[]{:T(128)}, f32[]{:T(128)}, u32[]{:S(2)}, u32[]{:S(2)}) collective-permute-start(f32[]{:T(128)} %add.55), channel_id=1, source_target_pairs={{0,32},{1,33},{2,34},{3,35},{4,36},{5,37},{6,38},{7,39},{8,40},{9,... | collective-permute-start | bytes 20 | tf_op jit(solution)/shard_map/ppermute | solution.py:186
  95.8 0.8 collective-permute-done.9
  97.2 7.8 %collective-permute-start.10 = (f32[]{:T(128)}, f32[]{:T(128)}, u32[]{:S(2)}, u32[]{:S(2)}) collective-permute-start(f32[]{:T(128)} %add.56), channel_id=1, source_target_pairs={{0,16},{1,17},{2,18},{3,19},{4,20},{5,21},{6,22},{7,23},{8,24},{9,... | collective-permute-start | bytes 20 | tf_op jit(solution)/shard_map/ppermute | solution.py:186
  105.6 0.8 collective-permute-start.11
  106.4 3.1 %collective-permute-done.11 = f32[]{:T(128)} collective-permute-done((f32[]{:T(128)}, f32[]{:T(128)}, u32[]{:S(2)}, u32[]{:S(2)}) %collective-permute-start.11) | collective-permute-done | bytes 36 | tf_op jit(solution)/shard_map/ppermute | solution.py:186
  110.1 0.8 collective-permute-start.12
  110.9 1.6 %collective-permute-done.12 = f32[]{:T(128)} collective-permute-done((f32[]{:T(128)}, f32[]{:T(128)}, u32[]{:S(2)}, u32[]{:S(2)}) %collective-permute-start.12) | collective-permute-done | bytes 36 | tf_op jit(solution)/shard_map/ppermute | solution.py:186
  113.1 0.0 collective-permute-done.13
  113.1 1.4 %convert_add_fusion.1 = f32[4,128,512]{2,1,0:T(8,128)S(1)} fusion(bf16[4,128,512]{2,1,0:T(8,128)(2,1)} %collective-permute-done.14, bf16[4,128,512]{2,1,0:T(8,128)(2,1)S(1)} %get-tuple-element.35, bf16[4,128,512]{2,1,0:T(8,128)(2,1)} %collective-permute-done.13), kind=kLoop, calls=%fused_computation.2 | loop fusion | flops 1310720 | bytes 2621440 | tf_op jit(solution)/shard_map/add | solution.py:227
  114.5 0.2 convert_add_fusion
  114.8 1.5 %pad_maximum_fusion = f32[4,128,1024]{2,1,0:T(8,128)} fusion(f32[4,128,512]{2,1,0:T(8,128)S(1)} %convert_add_fusion, f32[4,128,512]{2,1,0:T(8,128)S(1)} %convert_add_fusion.1), kind=kLoop, calls=%fused_computation | loop fusion | flops 524288 | bytes 4194304 | tf_op jit(solution)/shard_map/concatenate | solution.py:229
  (31 shorter events, 0.1 us)
Async XLA Ops:
  0.6 15.3 %copy-start.12 = (s32[4]{0:T(128)S(1)}, s32[4]{0:T(128)}, u32[]{:S(2)}) copy-start(s32[4]{0:T(128)} %param.13) | copy-start | bytes 52
  0.6 15.3 %copy-start.13 = (s32[4]{0:T(128)S(1)}, s32[4]{0:T(128)}, u32[]{:S(2)}) copy-start(s32[4]{0:T(128)} %param.12) | copy-start | bytes 52
  0.7 15.3 %copy-start.14 = (s32[4]{0:T(128)S(1)}, s32[4]{0:T(128)}, u32[]{:S(2)}) copy-start(s32[4]{0:T(128)} %param.15) | copy-start | bytes 52
  0.7 15.3 %copy-start.15 = (s32[4]{0:T(128)S(1)}, s32[4]{0:T(128)}, u32[]{:S(2)}) copy-start(s32[4]{0:T(128)} %param.14) | copy-start | bytes 52
  0.7 15.6 %copy-start.2 = (bf16[1024,1024]{1,0:T(8,128)(2,1)S(1)}, bf16[1024,1024]{1,0:T(8,128)(2,1)}, u32[]{:S(2)}) copy-start(bf16[1024,1024]{1,0:T(8,128)(2,1)} %wq_ref.5) | copy-start | bytes 6291460
  2.9 26.8 %collective-permute-start.2 = (bf16[3,128,1024]{2,1,0:T(8,128)(2,1)}, bf16[3,128,1024]{2,1,0:T(8,128)(2,1)S(1)}, u32[]{:S(2)}, u32[]{:S(2)}) collective-permute-start(bf16[3,128,1024]{2,1,0:T(8,128)(2,1)} %slice.14), channel_id=1, source_target_pairs={{1,0},{2,1},{3,2},{4,3},{5,4},{6,5},{7,6},{8,7},{9,8},{10,9},{11,1... | collective-permute-start | bytes 2359304 | tf_op jit(solution)/shard_map/ppermute | solution.py:26
  9.2 26.3 %collective-permute-start.1 = (bf16[3,128,1024]{2,1,0:T(8,128)(2,1)}, bf16[3,128,1024]{2,1,0:T(8,128)(2,1)}, u32[]{:S(2)}, u32[]{:S(2)}) collective-permute-start(bf16[3,128,1024]{2,1,0:T(8,128)(2,1)} %slice.14), channel_id=1, source_target_pairs={{255,0},{0,1},{1,2},{2,3},{3,4},{4,5},{5,6},{6,7},{7,8},{8,9},{9,1... | collective-permute-start | bytes 2359304 | tf_op jit(solution)/shard_map/ppermute | solution.py:26
  10.9 30.8 %collective-permute-start.4 = (bf16[1,128,1024]{2,1,0:T(8,128)(2,1)}, bf16[1,128,1024]{2,1,0:T(8,128)(2,1)S(1)}, u32[]{:S(2)}, u32[]{:S(2)}) collective-permute-start(bf16[1,128,1024]{2,1,0:T(8,128)(2,1)} %slice.15), channel_id=1, source_target_pairs={{1,0},{2,1},{3,2},{4,3},{5,4},{6,5},{7,6},{8,7},{9,8},{10,9},{11,1... | collective-permute-start | bytes 786440 | tf_op jit(solution)/shard_map/ppermute | solution.py:26
  16.0 25.8 %collective-permute-start.3 = (bf16[1,128,1024]{2,1,0:T(8,128)(2,1)}, bf16[1,128,1024]{2,1,0:T(8,128)(2,1)S(1)}, u32[]{:S(2)}, u32[]{:S(2)}) collective-permute-start(bf16[1,128,1024]{2,1,0:T(8,128)(2,1)} %slice.15), channel_id=1, source_target_pairs={{255,0},{0,1},{1,2},{2,3},{3,4},{4,5},{5,6},{6,7},{7,8},{8,9},{9,1... | collective-permute-start | bytes 786440 | tf_op jit(solution)/shard_map/ppermute | solution.py:26
  16.1 25.6 %collective-permute-start = (s32[16]{0:T(128)S(1)}, s32[16]{0:T(128)S(1)}, u32[]{:S(2)}, u32[]{:S(2)}) collective-permute-start(s32[16]{0:T(128)S(1)} %pad_add_fusion), channel_id=1, source_target_pairs={{255,0},{0,1},{1,2},{2,3},{3,4},{4,5},{5,6},{6,7},{7,8},{8,9},{9,1... | collective-permute-start | bytes 200 | tf_op jit(solution)/shard_map/ppermute | solution.py:26
  16.3 1.6 %copy-start.3 = (bf16[1024,1024]{1,0:T(8,128)(2,1)S(1)}, bf16[1024,1024]{1,0:T(8,128)(2,1)}, u32[]{:S(2)}) copy-start(bf16[1024,1024]{1,0:T(8,128)(2,1)} %wk_ref.5) | copy-start | bytes 6291460
  17.9 1.6 %copy-start.6 = (bf16[1024,1024]{1,0:T(8,128)(2,1)S(1)}, bf16[1024,1024]{1,0:T(8,128)(2,1)}, u32[]{:S(2)}) copy-start(bf16[1024,1024]{1,0:T(8,128)(2,1)} %wv_ref.5) | copy-start | bytes 6291460
  19.5 1.2 %copy-start.9 = (bf16[4,128,1024]{2,1,0:T(8,128)(2,1)S(1)}, bf16[4,128,1024]{2,1,0:T(8,128)(2,1)}, u32[]{:S(2)}) copy-start(bf16[4,128,1024]{2,1,0:T(8,128)(2,1)} %refs_0_.1) | copy-start | bytes 3145732
  20.7 14.8 %copy-start.4 = (bf16[1024,1024]{1,0:T(8,128)(2,1)S(1)}, bf16[1024,1024]{1,0:T(8,128)(2,1)}, u32[]{:S(2)}) copy-start(bf16[1024,1024]{1,0:T(8,128)(2,1)} %wk_ref.5) | copy-start | bytes 6291460
  24.2 17.6 %copy-start.7 = (bf16[1024,1024]{1,0:T(8,128)(2,1)S(1)}, bf16[1024,1024]{1,0:T(8,128)(2,1)}, u32[]{:S(2)}) copy-start(bf16[1024,1024]{1,0:T(8,128)(2,1)} %wv_ref.5) | copy-start | bytes 6291460
  54.0 5.9 %copy-start = (bf16[8,128,3072]{2,1,0:T(8,128)(2,1)}, bf16[8,128,3072]{2,1,0:T(8,128)(2,1)S(1)}, u32[]{:S(2)}) copy-start(bf16[8,128,3072]{2,1,0:T(8,128)(2,1)S(1)} %get-tuple-element.25.g_ref) | copy-start | bytes 18874372
  54.8 5.0 %collective-permute-start.5 = (f32[]{:T(128)}, f32[]{:T(128)}, u32[]{:S(2)}, u32[]{:S(2)}) collective-permute-start(f32[]{:T(128)} %fusion.3), channel_id=1, source_target_pairs={{0,1},{1,0},{2,3},{3,2},{4,5},{5,4},{6,7},{7,6},{8,9},{9,8},{10,11... | collective-permute-start | bytes 20 | tf_op jit(solution)/shard_map/ppermute | solution.py:186
  61.2 14.6 %collective-permute-start.6 = (f32[]{:T(128)}, f32[]{:T(128)}, u32[]{:S(2)}, u32[]{:S(2)}) collective-permute-start(f32[]{:T(128)} %add.52), channel_id=1, source_target_pairs={{0,2},{1,3},{2,0},{3,1},{4,6},{5,7},{6,4},{7,5},{8,10},{9,11},{10,... | collective-permute-start | bytes 20 | tf_op jit(solution)/shard_map/ppermute | solution.py:186
  62.0 51.1 %collective-permute-start.13 = (bf16[4,128,512]{2,1,0:T(8,128)(2,1)}, bf16[4,128,512]{2,1,0:T(8,128)(2,1)}, u32[]{:S(2)}, u32[]{:S(2)}) collective-permute-start(bf16[4,128,512]{2,1,0:T(8,128)(2,1)} %get-tuple-element.34), channel_id=1, source_target_pairs={{1,0},{2,1},{3,2},{4,3},{5,4},{6,5},{7,6},{8,7},{9,8},{10,9},{11,1... | collective-permute-start | bytes 1572872 | tf_op jit(solution)/shard_map/ppermute | solution.py:26
  64.1 49.1 %collective-permute-start.14 = (bf16[4,128,512]{2,1,0:T(8,128)(2,1)}, bf16[4,128,512]{2,1,0:T(8,128)(2,1)}, u32[]{:S(2)}, u32[]{:S(2)}) collective-permute-start(bf16[4,128,512]{2,1,0:T(8,128)(2,1)} %get-tuple-element.36), channel_id=1, source_target_pairs={{255,0},{0,1},{1,2},{2,3},{3,4},{4,5},{5,6},{6,7},{7,8},{8,9},{9,1... | collective-permute-start | bytes 1572872 | tf_op jit(solution)/shard_map/ppermute | solution.py:26
  64.1 2.8 %copy-start.1 = (bf16[8,128,3072]{2,1,0:T(8,128)(2,1)S(1)}, bf16[8,128,3072]{2,1,0:T(8,128)(2,1)}, u32[]{:S(2)}) copy-start(bf16[8,128,3072]{2,1,0:T(8,128)(2,1)} %copy-done) | copy-start | bytes 18874372
  66.9 1.6 %copy-start.5 = (bf16[1024,1024]{1,0:T(8,128)(2,1)S(1)}, bf16[1024,1024]{1,0:T(8,128)(2,1)}, u32[]{:S(2)}) copy-start(bf16[1024,1024]{1,0:T(8,128)(2,1)} %wk_ref.5) | copy-start | bytes 6291460
  68.4 1.6 %copy-start.8 = (bf16[1024,1024]{1,0:T(8,128)(2,1)S(1)}, bf16[1024,1024]{1,0:T(8,128)(2,1)}, u32[]{:S(2)}) copy-start(bf16[1024,1024]{1,0:T(8,128)(2,1)} %wv_ref.5) | copy-start | bytes 6291460
  74.2 0.8 copy-start.10
  75.0 0.8 copy-start.11
  76.5 38.1 %collective-permute-start.15 = (bf16[4,128,512]{2,1,0:T(8,128)(2,1)}, bf16[4,128,512]{2,1,0:T(8,128)(2,1)S(1)}, u32[]{:S(2)}, u32[]{:S(2)}) collective-permute-start(bf16[4,128,512]{2,1,0:T(8,128)(2,1)} %copy-done.11), channel_id=1, source_target_pairs={{1,0},{2,1},{3,2},{4,3},{5,4},{6,5},{7,6},{8,7},{9,8},{10,9},{11,1... | collective-permute-start | bytes 1572872 | tf_op jit(solution)/shard_map/ppermute | solution.py:26
  81.6 32.9 %collective-permute-start.16 = (bf16[4,128,512]{2,1,0:T(8,128)(2,1)}, bf16[4,128,512]{2,1,0:T(8,128)(2,1)S(1)}, u32[]{:S(2)}, u32[]{:S(2)}) collective-permute-start(bf16[4,128,512]{2,1,0:T(8,128)(2,1)} %copy-done.10), channel_id=1, source_target_pairs={{255,0},{0,1},{1,2},{2,3},{3,4},{4,5},{5,6},{6,7},{7,8},{8,9},{9,1... | collective-permute-start | bytes 1572872 | tf_op jit(solution)/shard_map/ppermute | solution.py:26
  81.6 7.8 %collective-permute-start.7 = (f32[]{:T(128)}, f32[]{:T(128)}, u32[]{:S(2)}, u32[]{:S(2)}) collective-permute-start(f32[]{:T(128)} %add.53), channel_id=1, source_target_pairs={{0,128},{1,129},{2,130},{3,131},{4,132},{5,133},{6,134},{7,135},{8... | collective-permute-start | bytes 20 | tf_op jit(solution)/shard_map/ppermute | solution.py:186
  90.0 3.3 %collective-permute-start.8 = (f32[]{:T(128)}, f32[]{:T(128)}, u32[]{:S(2)}, u32[]{:S(2)}) collective-permute-start(f32[]{:T(128)} %add.54), channel_id=1, source_target_pairs={{0,64},{1,65},{2,66},{3,67},{4,68},{5,69},{6,70},{7,71},{8,72},{9,... | collective-permute-start | bytes 20 | tf_op jit(solution)/shard_map/ppermute | solution.py:186
  93.9 2.8 %collective-permute-start.9 = (f32[]{:T(128)}, f32[]{:T(128)}, u32[]{:S(2)}, u32[]{:S(2)}) collective-permute-start(f32[]{:T(128)} %add.55), channel_id=1, source_target_pairs={{0,32},{1,33},{2,34},{3,35},{4,36},{5,37},{6,38},{7,39},{8,40},{9,... | collective-permute-start | bytes 20 | tf_op jit(solution)/shard_map/ppermute | solution.py:186
  97.2 7.8 %collective-permute-start.10 = (f32[]{:T(128)}, f32[]{:T(128)}, u32[]{:S(2)}, u32[]{:S(2)}) collective-permute-start(f32[]{:T(128)} %add.56), channel_id=1, source_target_pairs={{0,16},{1,17},{2,18},{3,19},{4,20},{5,21},{6,22},{7,23},{8,24},{9,... | collective-permute-start | bytes 20 | tf_op jit(solution)/shard_map/ppermute | solution.py:186
  105.6 3.9 %collective-permute-start.11 = (f32[]{:T(128)}, f32[]{:T(128)}, u32[]{:S(2)}, u32[]{:S(2)}) collective-permute-start(f32[]{:T(128)} %add.57), channel_id=1, source_target_pairs={{0,8},{1,9},{2,10},{3,11},{4,12},{5,13},{6,14},{7,15},{8,0},{9,1},... | collective-permute-start | bytes 20 | tf_op jit(solution)/shard_map/ppermute | solution.py:186
  110.1 2.4 %collective-permute-start.12 = (f32[]{:T(128)}, f32[]{:T(128)}, u32[]{:S(2)}, u32[]{:S(2)}) collective-permute-start(f32[]{:T(128)} %add.58), channel_id=1, source_target_pairs={{0,4},{1,5},{2,6},{3,7},{4,0},{5,1},{6,2},{7,3},{8,12},{9,13},{10,... | collective-permute-start | bytes 20 | tf_op jit(solution)/shard_map/ppermute | solution.py:186

commit v3 on v2

v3 whole, which is shorter than its diff:
```python
import functools

import jax
import jax.numpy as jnp
from jax import lax
from jax.experimental import pallas as pl
from jax.experimental.pallas import tpu as pltpu
from jax.sharding import PartitionSpec as P

AXES = ("dp", "mp")
ROW = 4
LOG2_E = 1.4426950408889634
NT = (((1,), (1,)), ((), ()))
TN = (((0,), (0,)), ((), ()))
VMEM = pl.BlockSpec(memory_space=pltpu.VMEM)
SMEM = pl.BlockSpec(memory_space=pltpu.SMEM)
ANY = pl.BlockSpec(memory_space=pl.ANY)


def mm(a, b, dims=(((1,), (0,)), ((), ()))):
    return lax.dot_general(a, b, dims, preferred_element_type=jnp.float32)


def from_behind(block, distance):
    count = lax.axis_size(AXES)
    return lax.ppermute(block, AXES, [((i - distance) % count, i) for i in range(count)])


def project_kernel(*refs):
    blocks = (len(refs) - 3) // 2
    xs, weights, outs = refs[:blocks], refs[blocks : blocks + 3], refs[blocks + 3 :]
    for n, w_ref in enumerate(weights):
        for x_ref, out_ref in zip(xs, outs):
            recs, seq, width = x_ref.shape
            made = mm(x_ref[...].reshape(recs * seq, width), w_ref[...])
            out_ref[:, :, n * width : (n + 1) * width] = made.astype(jnp.bfloat16).reshape(recs, seq, width)


def project(blocks, weights):
    rows = sum(block.shape[0] * block.shape[1] for block in blocks)
    width = blocks[0].shape[2]
    return pl.pallas_call(
        project_kernel,
        out_shape=[jax.ShapeDtypeStruct(block.shape[:2] + (3 * width,), jnp.bfloat16) for block in blocks],
        in_specs=[VMEM] * (len(blocks) + 3),
        out_specs=[VMEM] * len(blocks),
        compiler_params=pltpu.CompilerParams(vmem_limit_bytes=18 << 20),
        cost_estimate=pl.CostEstimate(flops=6 * rows * width * width, bytes_accessed=14 << 20, transcendentals=0),
        name="project",
    )(*blocks, *weights)


def pairs_kernel(
    info_ref, own_ref, left_x, right_x, wq_ref, wk_ref, wv_ref, grads_ref, z_ref, loss_ref, win, sem, *, count
):
    _, seq, full = win.shape
    recs, width = own_ref.shape[0], full // 3
    rows = recs * seq
    copy = pltpu.make_async_copy(own_ref, win.at[pl.ds(recs, recs)], sem)
    copy.start()
    x = jnp.concatenate([left_x[...].reshape(rows, width), right_x[...].reshape(rows, width)], axis=0)
    for n, w_ref in enumerate((wq_ref, wk_ref, wv_ref)):
        made = mm(x, w_ref[...]).astype(jnp.bfloat16)
        at = slice(n * width, (n + 1) * width)
        win[:recs, :, at] = made[:rows].reshape(recs, seq, width)
        win[2 * recs :, :, at] = made[rows:].reshape(recs, seq, width)

    lane = lax.broadcasted_iota(jnp.int32, (seq, 128), 1)
    first = lane < 64
    row = lax.broadcasted_iota(jnp.int32, (2 * seq, 128), 0)
    col = lax.broadcasted_iota(jnp.int32, (2 * seq, 128), 1)
    ends = jnp.where((row < seq) == (col < 64), 1.0, 0.0).astype(jnp.bfloat16)
    zero = jnp.zeros((seq, 128), jnp.bfloat16)
    copy.wait()
    loss_ref[...] = jnp.zeros_like(loss_ref)

    def one_pair(p, _):
        a, b = info_ref[p], info_ref[count + p]
        jobs = []
        for i in range(width // 128):
            at = [slice(n * width + i * 128, n * width + (i + 1) * 128) for n in range(3)]
            qa, ka, va = (win[a, :, s] for s in at)
            qb, kb, vb = (win[b, :, s] for s in at)
            jobs.append((at, 0, count, qa, kb, vb))
            jobs.append((at, count, 0, qb, ka, va))
        qs = [
            jnp.concatenate([jnp.where(first, job[3], zero), jnp.where(first, zero, job[3])], axis=0) for job in jobs
        ]
        scores = [mm(job[4], q, NT) for job, q in zip(jobs, qs)]
        probs = []
        for s in scores:
            top = jnp.max(s, axis=0, keepdims=True)
            e = jnp.exp2((s - top) * (LOG2_E / 8.0))
            probs.append(e * (1.0 / jnp.sum(e, axis=0, keepdims=True)))
        mass = [mm(prob.astype(jnp.bfloat16), ends) for prob in probs]
        pooled = [
            jnp.sum(m * job[5].astype(jnp.float32), axis=0, keepdims=True) * (1.0 / seq) for m, job in zip(mass, jobs)
        ]
        z = jnp.zeros((1, 128), jnp.float32)
        for i in range(width // 128):
            z = z + pooled[2 * i] * pooled[2 * i + 1]
        z = 4.0 * jnp.sum(z)
        z_ref[p] = z
        c = info_ref[2 * count + p].astype(jnp.float32) * (1.0 / 256.0)
        y = info_ref[3 * count + p].astype(jnp.float32)
        z = jnp.full(loss_ref.shape, z, jnp.float32)
        loss_ref[...] += c * (jnp.maximum(z, 0.0) + jnp.log1p(jnp.exp(-jnp.abs(z))) - y * z)
        dps = [pooled[n ^ 1] * (4.0 / seq) for n in range(len(jobs))]
        ts = [
            mm((job[5].astype(jnp.float32) * (dp * 0.125)).astype(jnp.bfloat16), ends, NT)
            for dp, job in zip(dps, jobs)
        ]
        dss = []
        for prob, t in zip(probs, ts):
            r = jnp.sum(prob * t, axis=0, keepdims=True)
            dss.append((prob * (t - r)).astype(jnp.bfloat16))
        dks = [mm(ds, q) for ds, q in zip(dss, qs)]
        dqs = [mm(ds, job[4], TN) for ds, job in zip(dss, jobs)]
        for n, (at, qrow, krow, _, _, _) in enumerate(jobs):
            grads_ref[krow + p, :, at[2]] = (mass[n] * dps[n]).astype(jnp.bfloat16)
            grads_ref[krow + p, :, at[1]] = dks[n].astype(jnp.bfloat16)
            grads_ref[qrow + p, :, at[0]] = jnp.where(first, dqs[n][:seq], dqs[n][seq:]).astype(jnp.bfloat16)
        return 0

    lax.fori_loop(0, count, one_pair, 0)


def pairs(info, own, left_x, right_x, weights, count):
    recs, seq, full = own.shape
    return pl.pallas_call(
        functools.partial(pairs_kernel, count=count),
        out_shape=(
            jax.ShapeDtypeStruct((2 * count, seq, full), jnp.bfloat16),
            jax.ShapeDtypeStruct((count,), jnp.float32),
            jax.ShapeDtypeStruct((8, 128), jnp.float32),
        ),
        in_specs=[SMEM, ANY] + [VMEM] * 5,
        out_specs=(VMEM, SMEM, VMEM),
        scratch_shapes=[pltpu.VMEM((3 * recs, seq, full), jnp.bfloat16), pltpu.SemaphoreType.DMA],
        compiler_params=pltpu.CompilerParams(vmem_limit_bytes=28 << 20),
        cost_estimate=pl.CostEstimate(flops=12 << 30, bytes_accessed=12 << 20, transcendentals=2 << 20),
        name="pairs",
    )(info, own, left_x, right_x, *weights)


def terms_kernel(info_ref, z_ref, g_ref, wq_ref, wk_ref, wv_ref, left_ref, own_ref, right_ref, acc, *, count):
    _, seq, full = g_ref.shape
    width, recs, tile = full // 3, left_ref.shape[0], acc.shape[2]
    scales = []
    for p in range(count):
        z = jnp.full((8, 128), z_ref[p], jnp.float32)
        c = info_ref[2 * count + p].astype(jnp.float32) * (1.0 / 256.0)
        y = info_ref[3 * count + p].astype(jnp.float32)
        scales.append((seq * c * (jax.nn.sigmoid(z) - y))[0:1, 0:1])
    for start in range(0, left_ref.shape[2], tile):
        columns = slice(start, start + tile)
        made = None
        for n, w_ref in enumerate((wq_ref, wk_ref, wv_ref)):
            grads = g_ref[:, :, n * width : (n + 1) * width].reshape(2 * count * seq, width)
            part = mm(grads, w_ref[columns, :], NT)
            made = part if made is None else made + part
        acc[...] = jnp.zeros_like(acc)
        for n in range(2 * count):
            acc[info_ref[n]] += made[n * seq : (n + 1) * seq] * scales[n % count]
        for n, out in enumerate((left_ref, own_ref, right_ref)):
            out[:, :, columns] = acc[n * recs : (n + 1) * recs].astype(jnp.bfloat16)


def terms(info, z, grads, weights, recs, count):
    _, seq, full = grads.shape
    size = weights[0].shape[0]
    made = jax.ShapeDtypeStruct((recs, seq, size), jnp.bfloat16)
    return pl.pallas_call(
        functools.partial(terms_kernel, count=count),
        out_shape=(made, made, made),
        in_specs=[SMEM, SMEM] + [VMEM] * 4,
        out_specs=(VMEM,) * 3,
        scratch_shapes=[pltpu.VMEM((3 * recs, seq, 512), jnp.float32)],
        compiler_params=pltpu.CompilerParams(vmem_limit_bytes=18 << 20),
        cost_estimate=pl.CostEstimate(
            flops=4 * count * seq * full * size, bytes_accessed=12 << 20, transcendentals=0
        ),
        name="terms",
    )(info, z, grads, *weights)


def row_total(value):
    count = lax.axis_size(AXES)
    routes = [[(i, i - i % ROW + (i + k) % ROW) for i in range(count)] for k in range(1, ROW)]
    return sum([lax.ppermute(value, AXES, route) for route in routes], value)


def column_total(value):
    rows = lax.axis_size(AXES) // ROW
    groups = [[h * ROW + x for h in range(rows)] for x in range(ROW)]
    spread = jnp.broadcast_to(value[0:1], (rows, value.shape[1]))
    met = lax.all_to_all(spread, AXES, 0, 0, axis_index_groups=groups, tiled=True)
    return jnp.sum(met, axis=0)[0]


def on_device(records, w_query, w_key, w_value, pair_owner, pair_partner, confidence, labels):
    recs, seq, width = records.shape
    count = pair_owner.shape[0]
    devices = lax.axis_size(AXES)
    first_id = lax.axis_index(AXES) * recs
    weights = (w_query, w_key, w_value)

    left_records = from_behind(records, 1)
    right_records = from_behind(records, -1)
    own_info = jnp.concatenate(
        [pair_owner - first_id, jnp.mod(pair_partner - first_id, recs * devices), confidence, labels]
    )
    info = from_behind(own_info, 1)
    (own,) = project([records], weights)
    grads, z, loss = pairs(info, own, left_records, right_records, weights, count)

    z, loss = lax.optimization_barrier((z, loss))
    loss = row_total(loss)
    to_left, kept, to_right = terms(info, z, grads, weights, recs, count)
    to_left, to_right, loss = lax.optimization_barrier((to_left, to_right, loss))
    from_right, from_left = from_behind(to_left, -1), from_behind(to_right, 1)
    loss = column_total(loss) / (count * devices)
    record_grad = from_right.astype(jnp.float32) + kept.astype(jnp.float32) + from_left.astype(jnp.float32)
    return (loss, record_grad)


def solution(mesh):
    blocks = P(AXES, None, None)
    in_specs = (blocks, P(), P(), P(), P(AXES), P(AXES), P(AXES), P(AXES))
    return jax.shard_map(
        on_device, mesh=mesh, in_specs=in_specs, out_specs=(P(), blocks), check_vma=False
    )
```

time: 118 us -> 98.3 us (0.83)
  starting transfers between devices: 41.2 us -> 9.74 us
  blocking collectives: 0 us -> 20.1 us
  local copies, waits for them, and re-layouts: 15.9 us -> 6.03 us
  waiting for transfers between devices: 17.8 us -> 27.2 us
  between operations: 7.42 us -> 1.93 us
  Pallas kernels: 31.1 us -> 28 us
    ppermute x8 -> x3, starting transfers between devices: 22.4 us -> 1.53 us  [row_total(): return sum([lax.ppermute(value, AXES, route) for route in routes], value)]
    all_to_all x0 -> x1, blocking collectives: none -> 20.1 us  [column_total(): lax.all_to_all(spread, AXES, 0, 0, axis_index_groups=groups, tiled=True)]
    ppermute x9 -> x5, waiting for transfers between devices: 11.4 us -> 27.2 us  [from_behind(): lax.ppermute(block, AXES, [((i - distance) % count, i) for i in range(cou...]
    ppermute x9 -> x5, starting transfers between devices: 18.8 us -> 8.21 us  [from_behind(): lax.ppermute(block, AXES, [((i - distance) % count, i) for i in range(cou...]
    ppermute x8 -> x3, waiting for transfers between devices: 6.43 us -> 0.01 us  [row_total(): return sum([lax.ppermute(value, AXES, route) for route in routes], value)]
    pallas_call x2 -> x1, Pallas kernels: 9.6 us -> 3.41 us  [project(): pl.pallas_call(project_kernel, out_shape=[jax.ShapeDtypeStruct(block.shap...]
    unnamed x32 -> x14, local copies, waits for them, and re-layouts: 12 us -> 6 us
    pallas_call x1, Pallas kernels: 12.3 us -> 16.8 us  [pairs(): pl.pallas_call(functools.partial(pairs_kernel, count=count), out_shape=(j...]
  transfers between devices with their start and end apart: 17 -> 8, of which waited for: 7 -> 3; matrix products, arithmetic and copies ran while one was open for 3% -> 2% of each run, Pallas kernels for 16% -> 12%
where the time goes in v3:
time: 98.3 us; the launch traced here: 97.9 us
  Pallas kernels  28 us (28%)
  waiting for transfers between devices  27.2 us (28%)
  blocking collectives  20.1 us (20%)
  starting transfers between devices  9.74 us (10%)
  local copies, waits for them, and re-layouts  6.03 us (6%)
  other arithmetic  4.9 us (5%)
  between operations  1.93 us (2%)
    ppermute x5, waiting for transfers between devices, from_behind(): lax.ppermute(block, AXES, [((i - distance) % count, i) for i in range(cou...  27.2 us
    all_to_all x1, blocking collectives, column_total(): lax.all_to_all(spread, AXES, 0, 0, axis_index_groups=groups, tiled=True)  20.1 us
    pallas_call x1, Pallas kernels, pairs(): pl.pallas_call(functools.partial(pairs_kernel, count=count), out_shape=(j...  16.8 us
    ppermute x5, starting transfers between devices, from_behind(): lax.ppermute(block, AXES, [((i - distance) % count, i) for i in range(cou...  8.21 us
    pallas_call x1, Pallas kernels, terms(): pl.pallas_call(functools.partial(terms_kernel, count=count), out_shape=(m...  7.85 us
    unnamed x14, local copies, waits for them, and re-layouts  6 us
    add x1, other arithmetic, on_device(): from_right.astype(jnp.float32) + kept.astype(jnp.float32)  3.44 us
    pallas_call x1, Pallas kernels, project(): pl.pallas_call(project_kernel, out_shape=[jax.ShapeDtypeStruct(block.shap...  3.41 us
  transfers between devices with their start and end apart: 8, of which 3 were waited for; matrix products, arithmetic and copies ran while one was open for 2% of the time, Pallas kernels for 12%

profile of v3, /device:TPU:1, one launch (start us, length us, event | category | flops | bytes accessed | tf_op | source)
XLA Modules:
  0.0 97.9 jit_solution(16881504846621199073)
XLA Ops:
  0.6 6.4 %collective-permute-start.2 = (bf16[4,128,1024]{2,1,0:T(8,128)(2,1)}, bf16[4,128,1024]{2,1,0:T(8,128)(2,1)S(1)}, u32[]{:S(2)}, u32[]{:S(2)}) collective-permute-start(bf16[4,128,1024]{2,1,0:T(8,128)(2,1)} %refs_0_.1), channel_id=1, source_target_pairs={{1,0},{2,1},{3,2},{4,3},{5,4},{6,5},{7,6},{8,7},{9,8},{10,9},{11,1... | collective-permute-start | bytes 3145736 | tf_op jit(solution)/shard_map/ppermute | solution.py:26
  7.0 0.0 collective-permute-start.1
  7.0 0.7 and_select_fusion
  7.7 0.7 pad_add_fusion
  8.5 0.0 collective-permute-start
  8.5 0.0 copy-start
  8.5 1.6 %copy-done = bf16[1024,1024]{1,0:T(8,128)(2,1)S(1)} copy-done((bf16[1024,1024]{1,0:T(8,128)(2,1)S(1)}, bf16[1024,1024]{1,0:T(8,128)(2,1)}, u32[]{:S(2)}) %copy-start) | copy-done | bytes 2097176
  10.1 0.0 copy-start.2
  10.1 1.6 %copy-done.2 = bf16[1024,1024]{1,0:T(8,128)(2,1)S(1)} copy-done((bf16[1024,1024]{1,0:T(8,128)(2,1)S(1)}, bf16[1024,1024]{1,0:T(8,128)(2,1)}, u32[]{:S(2)}) %copy-start.2) | copy-done | bytes 2097176
  11.7 0.0 copy-start.4
  11.7 1.6 %copy-done.4 = bf16[1024,1024]{1,0:T(8,128)(2,1)S(1)} copy-done((bf16[1024,1024]{1,0:T(8,128)(2,1)S(1)}, bf16[1024,1024]{1,0:T(8,128)(2,1)}, u32[]{:S(2)}) %copy-start.4) | copy-done | bytes 2097176
  13.3 0.0 copy-start.6
  13.3 1.2 %copy-done.6 = bf16[4,128,1024]{2,1,0:T(8,128)(2,1)S(1)} copy-done((bf16[4,128,1024]{2,1,0:T(8,128)(2,1)S(1)}, bf16[4,128,1024]{2,1,0:T(8,128)(2,1)}, u32[]{:S(2)}) %copy-start.6) | copy-done | bytes 1048600
  14.5 0.0 copy-start.1
  14.5 0.0 copy-start.3
  14.5 0.0 copy-start.5
  14.5 3.4 %project.1.own_ref = bf16[4,128,3072]{2,1,0:T(8,128)(2,1)S(1)} custom-call(bf16[4,128,1024]{2,1,0:T(8,128)(2,1)S(1)} %copy-done.6, bf16[1024,1024]{1,0:T(8,128)(2,1)S(1)} %copy-done, bf16[1024,1024]{1,0:T(8,128)(2,1)S(1)} %copy-done.2, bf16[1024,1024]{1,0:T(8,128)(2,1)S(1)} %copy-done.4), custom_call_target="tpu_custom_call" | custom-call | flops 3221225472 | bytes 14680064 | tf_op jit(solution)/shard_map/project/pallas_call | solution.py:42
  17.9 18.2 %collective-permute-done.info_ref = s32[16]{0:T(128)S(1)} collective-permute-done((s32[16]{0:T(128)S(1)}, s32[16]{0:T(128)S(1)}, u32[]{:S(2)}, u32[]{:S(2)}) %collective-permute-start) | collective-permute-done | bytes 96 | tf_op jit(solution)/shard_map/ppermute | solution.py:26
  36.1 0.0 collective-permute-done.2.right_x
  36.1 0.0 collective-permute-done.1.left_x
  36.1 0.0 copy-done.1
  36.1 0.0 copy-done.3
  36.1 0.0 copy-done.5
  36.1 16.8 %pairs.1 = (bf16[8,128,3072]{2,1,0:T(8,128)(2,1)S(1)}, f32[4]{0:T(128)S(1)}, f32[8,128]{1,0:T(8,128)S(1)}) custom-call(s32[16]{0:T(128)S(1)} %collective-permute-done.info_ref, bf16[4,128,3072]{2,1,0:T(8,128)(2,1)S(1)} %project.1.own_ref, bf16[4,128,1024]{2,1,0:T(8,128)(2,1)S(1)} %collective-permute-done.1.left_x, ...), custom_call_target="tpu_custom_call" | custom-call | flops 12884901888 | bytes 12582912 | tf_op jit(solution)/shard_map/pairs/pallas_call | solution.py:130
  52.9 0.1 collective-permute-start.5
  53.0 0.1 collective-permute-start.4
  53.1 1.4 %collective-permute-start.3 = (f32[8,128]{1,0:T(8,128)S(1)}, f32[8,128]{1,0:T(8,128)S(1)}, u32[]{:S(2)}, u32[]{:S(2)}) collective-permute-start(f32[8,128]{1,0:T(8,128)S(1)} %get-tuple-element.19), channel_id=1, source_target_pairs={{0,1},{1,2},{2,3},{3,0},{4,5},{5,6},{6,7},{7,4},{8,9},{9,10},{10,1... | collective-permute-start | bytes 12296 | tf_op jit(solution)/shard_map/ppermute | solution.py:190
  54.4 7.9 %terms.1 = (bf16[4,128,1024]{2,1,0:T(8,128)(2,1)S(1)}, bf16[4,128,1024]{2,1,0:T(8,128)(2,1)S(1)}, bf16[4,128,1024]{2,1,0:T(8,128)(2,1)S(1)}) custom-call(s32[16]{0:T(128)S(1)} %collective-permute-done.info_ref, f32[4]{0:T(128)S(1)} %get-tuple-element.15.z_ref, bf16[8,128,3072]{2,1,0:T(8,128)(2,1)S(1)} %get-tuple-element.16.g_ref, ...), custom_call_target="tpu_custom_call" | custom-call | flops 6442450944 | bytes 12582912 | tf_op jit(solution)/shard_map/terms/pallas_call | solution.py:173
  62.3 0.0 collective-permute-done.5
  62.3 0.0 collective-permute-done.4
  62.3 0.0 collective-permute-done.3
  62.3 1.8 %collective-permute-start.6 = (bf16[4,128,1024]{2,1,0:T(8,128)(2,1)S(1)}, bf16[4,128,1024]{2,1,0:T(8,128)(2,1)}, u32[]{:S(2)}, u32[]{:S(2)}) collective-permute-start(bf16[4,128,1024]{2,1,0:T(8,128)(2,1)S(1)} %get-tuple-element.21), channel_id=1, source_target_pairs={{1,0},{2,1},{3,2},{4,3},{5,4},{6,5},{7,6},{8,7},{9,8},{10,9},{11,1... | collective-permute-start | bytes 3145736 | tf_op jit(solution)/shard_map/ppermute | solution.py:26
  64.1 0.0 collective-permute-start.7
  64.2 20.1 %all_to_all.6 = f32[64,1,128]{2,1,0:T(1,128)S(1)} all-to-all(f32[64,1,128]{2,1,0:T(1,128)S(1)} %broadcast_in_dim.2), channel_id=1, replica_groups={{0,4,8,12,16,20,24,28,32,36,40,44,48,52,56,60,64,68,72,76,80,84,88,92,9..., dimensions={0} | all-to-all | bytes 65536 | tf_op jit(solution)/shard_map/all_to_all | solution.py:197
  84.3 1.8 %collective-permute-done.6 = bf16[4,128,1024]{2,1,0:T(8,128)(2,1)} collective-permute-done((bf16[4,128,1024]{2,1,0:T(8,128)(2,1)S(1)}, bf16[4,128,1024]{2,1,0:T(8,128)(2,1)}, u32[]{:S(2)}, u32[]{:S(2)}) %collective-permute-start.6) | collective-permute-done | bytes 1048608 | tf_op jit(solution)/shard_map/ppermute | solution.py:26
  86.2 7.2 %collective-permute-done.7 = bf16[4,128,1024]{2,1,0:T(8,128)(2,1)} collective-permute-done((bf16[4,128,1024]{2,1,0:T(8,128)(2,1)S(1)}, bf16[4,128,1024]{2,1,0:T(8,128)(2,1)}, u32[]{:S(2)}, u32[]{:S(2)}) %collective-permute-start.7) | collective-permute-done | bytes 1048608 | tf_op jit(solution)/shard_map/ppermute | solution.py:26
  93.4 3.4 %convert_add_fusion = f32[4,128,1024]{2,1,0:T(8,128)} fusion(bf16[4,128,1024]{2,1,0:T(8,128)(2,1)} %collective-permute-done.7, bf16[4,128,1024]{2,1,0:T(8,128)(2,1)S(1)} %get-tuple-element.22, bf16[4,128,1024]{2,1,0:T(8,128)(2,1)} %collective-permute-done.6), kind=kLoop, calls=%fused_computation | loop fusion | flops 2621440 | bytes 5242880 | tf_op jit(solution)/shard_map/add | solution.py:223
  (4 shorter events, 0.1 us)
Async XLA Ops:
  0.6 35.5 %collective-permute-start.2 = (bf16[4,128,1024]{2,1,0:T(8,128)(2,1)}, bf16[4,128,1024]{2,1,0:T(8,128)(2,1)S(1)}, u32[]{:S(2)}, u32[]{:S(2)}) collective-permute-start(bf16[4,128,1024]{2,1,0:T(8,128)(2,1)} %refs_0_.1), channel_id=1, source_target_pairs={{1,0},{2,1},{3,2},{4,3},{5,4},{6,5},{7,6},{8,7},{9,8},{10,9},{11,1... | collective-permute-start | bytes 3145736 | tf_op jit(solution)/shard_map/ppermute | solution.py:26
  7.0 29.1 %collective-permute-start.1 = (bf16[4,128,1024]{2,1,0:T(8,128)(2,1)}, bf16[4,128,1024]{2,1,0:T(8,128)(2,1)S(1)}, u32[]{:S(2)}, u32[]{:S(2)}) collective-permute-start(bf16[4,128,1024]{2,1,0:T(8,128)(2,1)} %refs_0_.1), channel_id=1, source_target_pairs={{255,0},{0,1},{1,2},{2,3},{3,4},{4,5},{5,6},{6,7},{7,8},{8,9},{9,1... | collective-permute-start | bytes 3145736 | tf_op jit(solution)/shard_map/ppermute | solution.py:26
  8.5 27.6 %collective-permute-start = (s32[16]{0:T(128)S(1)}, s32[16]{0:T(128)S(1)}, u32[]{:S(2)}, u32[]{:S(2)}) collective-permute-start(s32[16]{0:T(128)S(1)} %pad_add_fusion), channel_id=1, source_target_pairs={{255,0},{0,1},{1,2},{2,3},{3,4},{4,5},{5,6},{6,7},{7,8},{8,9},{9,1... | collective-permute-start | bytes 200 | tf_op jit(solution)/shard_map/ppermute | solution.py:26
  8.5 1.6 %copy-start = (bf16[1024,1024]{1,0:T(8,128)(2,1)S(1)}, bf16[1024,1024]{1,0:T(8,128)(2,1)}, u32[]{:S(2)}) copy-start(bf16[1024,1024]{1,0:T(8,128)(2,1)} %wq_ref.3) | copy-start | bytes 6291460
  10.1 1.6 %copy-start.2 = (bf16[1024,1024]{1,0:T(8,128)(2,1)S(1)}, bf16[1024,1024]{1,0:T(8,128)(2,1)}, u32[]{:S(2)}) copy-start(bf16[1024,1024]{1,0:T(8,128)(2,1)} %wk_ref.3) | copy-start | bytes 6291460
  11.7 1.6 %copy-start.4 = (bf16[1024,1024]{1,0:T(8,128)(2,1)S(1)}, bf16[1024,1024]{1,0:T(8,128)(2,1)}, u32[]{:S(2)}) copy-start(bf16[1024,1024]{1,0:T(8,128)(2,1)} %wv_ref.3) | copy-start | bytes 6291460
  13.3 1.2 %copy-start.6 = (bf16[4,128,1024]{2,1,0:T(8,128)(2,1)S(1)}, bf16[4,128,1024]{2,1,0:T(8,128)(2,1)}, u32[]{:S(2)}) copy-start(bf16[4,128,1024]{2,1,0:T(8,128)(2,1)} %refs_0_.1) | copy-start | bytes 3145732
  14.5 21.6 %copy-start.1 = (bf16[1024,1024]{1,0:T(8,128)(2,1)S(1)}, bf16[1024,1024]{1,0:T(8,128)(2,1)}, u32[]{:S(2)}) copy-start(bf16[1024,1024]{1,0:T(8,128)(2,1)} %wq_ref.3) | copy-start | bytes 6291460
  14.5 21.6 %copy-start.3 = (bf16[1024,1024]{1,0:T(8,128)(2,1)S(1)}, bf16[1024,1024]{1,0:T(8,128)(2,1)}, u32[]{:S(2)}) copy-start(bf16[1024,1024]{1,0:T(8,128)(2,1)} %wk_ref.3) | copy-start | bytes 6291460
  14.5 21.6 %copy-start.5 = (bf16[1024,1024]{1,0:T(8,128)(2,1)S(1)}, bf16[1024,1024]{1,0:T(8,128)(2,1)}, u32[]{:S(2)}) copy-start(bf16[1024,1024]{1,0:T(8,128)(2,1)} %wv_ref.3) | copy-start | bytes 6291460
  52.9 9.4 %collective-permute-start.5 = (f32[8,128]{1,0:T(8,128)S(1)}, f32[8,128]{1,0:T(8,128)S(1)}, u32[]{:S(2)}, u32[]{:S(2)}) collective-permute-start(f32[8,128]{1,0:T(8,128)S(1)} %get-tuple-element.19), channel_id=1, source_target_pairs={{0,3},{1,0},{2,1},{3,2},{4,7},{5,4},{6,5},{7,6},{8,11},{9,8},{10,9... | collective-permute-start | bytes 12296 | tf_op jit(solution)/shard_map/ppermute | solution.py:190
  53.0 9.3 %collective-permute-start.4 = (f32[8,128]{1,0:T(8,128)S(1)}, f32[8,128]{1,0:T(8,128)S(1)}, u32[]{:S(2)}, u32[]{:S(2)}) collective-permute-start(f32[8,128]{1,0:T(8,128)S(1)} %get-tuple-element.19), channel_id=1, source_target_pairs={{0,2},{1,3},{2,0},{3,1},{4,6},{5,7},{6,4},{7,5},{8,10},{9,11},{10,... | collective-permute-start | bytes 12296 | tf_op jit(solution)/shard_map/ppermute | solution.py:190
  53.1 9.2 %collective-permute-start.3 = (f32[8,128]{1,0:T(8,128)S(1)}, f32[8,128]{1,0:T(8,128)S(1)}, u32[]{:S(2)}, u32[]{:S(2)}) collective-permute-start(f32[8,128]{1,0:T(8,128)S(1)} %get-tuple-element.19), channel_id=1, source_target_pairs={{0,1},{1,2},{2,3},{3,0},{4,5},{5,6},{6,7},{7,4},{8,9},{9,10},{10,1... | collective-permute-start | bytes 12296 | tf_op jit(solution)/shard_map/ppermute | solution.py:190
  62.3 23.8 %collective-permute-start.6 = (bf16[4,128,1024]{2,1,0:T(8,128)(2,1)S(1)}, bf16[4,128,1024]{2,1,0:T(8,128)(2,1)}, u32[]{:S(2)}, u32[]{:S(2)}) collective-permute-start(bf16[4,128,1024]{2,1,0:T(8,128)(2,1)S(1)} %get-tuple-element.21), channel_id=1, source_target_pairs={{1,0},{2,1},{3,2},{4,3},{5,4},{6,5},{7,6},{8,7},{9,8},{10,9},{11,1... | collective-permute-start | bytes 3145736 | tf_op jit(solution)/shard_map/ppermute | solution.py:26
  64.1 29.2 %collective-permute-start.7 = (bf16[4,128,1024]{2,1,0:T(8,128)(2,1)S(1)}, bf16[4,128,1024]{2,1,0:T(8,128)(2,1)}, u32[]{:S(2)}, u32[]{:S(2)}) collective-permute-start(bf16[4,128,1024]{2,1,0:T(8,128)(2,1)S(1)} %get-tuple-element.23), channel_id=1, source_target_pairs={{255,0},{0,1},{1,2},{2,3},{3,4},{4,5},{5,6},{6,7},{7,8},{8,9},{9,1... | collective-permute-start | bytes 3145736 | tf_op jit(solution)/shard_map/ppermute | solution.py:26

commit v4 on v3

v4 whole, which is shorter than its diff:
```python
import functools

import jax
import jax.numpy as jnp
from jax import lax
from jax.experimental import pallas as pl
from jax.experimental.pallas import tpu as pltpu
from jax.sharding import PartitionSpec as P

AXES = ("dp", "mp")
ROW = 4
LAGS = (0, 2, 4, 6, 8, 10, 12, 14)
LOG2_E = 1.4426950408889634
NT = (((1,), (1,)), ((), ()))
TN = (((0,), (0,)), ((), ()))
VMEM = pl.BlockSpec(memory_space=pltpu.VMEM)
SMEM = pl.BlockSpec(memory_space=pltpu.SMEM)
ANY = pl.BlockSpec(memory_space=pl.ANY)


def mm(a, b, dims=(((1,), (0,)), ((), ()))):
    return lax.dot_general(a, b, dims, preferred_element_type=jnp.float32)


def from_behind(block, distance):
    count = lax.axis_size(AXES)
    return lax.ppermute(block, AXES, [((i - distance) % count, i) for i in range(count)])


def project_kernel(*refs):
    blocks = (len(refs) - 3) // 2
    xs, weights, outs = refs[:blocks], refs[blocks : blocks + 3], refs[blocks + 3 :]
    for n, w_ref in enumerate(weights):
        for x_ref, out_ref in zip(xs, outs):
            recs, seq, width = x_ref.shape
            made = mm(x_ref[...].reshape(recs * seq, width), w_ref[...])
            out_ref[:, :, n * width : (n + 1) * width] = made.astype(jnp.bfloat16).reshape(recs, seq, width)


def project(blocks, weights):
    rows = sum(block.shape[0] * block.shape[1] for block in blocks)
    width = blocks[0].shape[2]
    return pl.pallas_call(
        project_kernel,
        out_shape=[jax.ShapeDtypeStruct(block.shape[:2] + (3 * width,), jnp.bfloat16) for block in blocks],
        in_specs=[VMEM] * (len(blocks) + 3),
        out_specs=[VMEM] * len(blocks),
        compiler_params=pltpu.CompilerParams(vmem_limit_bytes=18 << 20),
        cost_estimate=pl.CostEstimate(flops=6 * rows * width * width, bytes_accessed=14 << 20, transcendentals=0),
        name="project",
    )(*blocks, *weights)


def pairs_kernel(
    info_ref, own_ref, left_x, right_x, wq_ref, wk_ref, wv_ref, to_left, kept, to_right, loss_ref, win, grads, scale, acc, sem,
    *, count, together
):
    _, seq, full = win.shape
    recs, width = own_ref.shape[0], full // 3
    rows = recs * seq
    weights = (wq_ref, wk_ref, wv_ref)
    copy = pltpu.make_async_copy(own_ref, win.at[pl.ds(recs, recs)], sem)
    copy.start()
    x = jnp.concatenate([left_x[...].reshape(rows, width), right_x[...].reshape(rows, width)], axis=0)
    for n, w_ref in enumerate(weights):
        made = mm(x, w_ref[...]).astype(jnp.bfloat16)
        at = slice(n * width, (n + 1) * width)
        win[:recs, :, at] = made[:rows].reshape(recs, seq, width)
        win[2 * recs :, :, at] = made[rows:].reshape(recs, seq, width)

    lane = lax.broadcasted_iota(jnp.int32, (seq, 128), 1)
    first = lane < 64
    row = lax.broadcasted_iota(jnp.int32, (2 * seq, 128), 0)
    col = lax.broadcasted_iota(jnp.int32, (2 * seq, 128), 1)
    ends = jnp.where((row < seq) == (col < 64), 1.0, 0.0).astype(jnp.bfloat16)
    ends_t = ends.astype(jnp.float32).T.astype(jnp.bfloat16)
    zero = jnp.zeros((seq, 128), jnp.bfloat16)
    copy.wait()
    loss_ref[...] = jnp.zeros_like(loss_ref)

    def some_pairs(i, _):
        blocks = width // 128
        jobs = []
        for k in range(together):
            p = i * together + k
            a, b = info_ref[p], info_ref[count + p]
            for j in range(blocks):
                jobs.append((k, j, a, b, p, count + p))
                jobs.append((k, j, b, a, count + p, p))
        qs, ks, probs, mass, pooled, dps, ts, dss, out = ({} for _ in range(9))

        def part(which, j):
            return slice(which * width + j * 128, which * width + (j + 1) * 128)

        def scores(n):
            _, j, mine, other, _, _ = jobs[n]
            q = win[mine, :, part(0, j)]
            qs[n] = jnp.concatenate([jnp.where(first, q, zero), jnp.where(first, zero, q)], axis=0)
            ks[n] = win[other, :, part(1, j)]
            probs[n] = mm(ks[n], qs[n], NT)

        def softmax(n):
            top = jnp.max(probs[n], axis=0, keepdims=True)
            e = jnp.exp2((probs[n] - top) * (LOG2_E / 8.0))
            probs[n] = e * (1.0 / jnp.sum(e, axis=0, keepdims=True))

        def masses(n):
            mass[n] = mm(probs[n].astype(jnp.bfloat16), ends)

        def pool(n):
            _, j, _, other, _, _ = jobs[n]
            v = win[other, :, part(2, j)].astype(jnp.float32)
            pooled[n] = jnp.sum(mass[n] * v, axis=0, keepdims=True) * (1.0 / seq)

        def t(n):
            _, j, _, other, _, _ = jobs[n]
            v = win[other, :, part(2, j)].astype(jnp.float32)
            dps[n] = pooled[n ^ 1] * (4.0 / seq)
            ts[n] = mm((v * (dps[n] * 0.125)).astype(jnp.bfloat16), ends_t)

        def ds(n):
            r = jnp.sum(probs[n] * ts[n], axis=0, keepdims=True)
            dss[n] = (probs[n] * (ts[n] - r)).astype(jnp.bfloat16)

        def products(n):
            out[n] = mm(dss[n], qs[n]), mm(dss[n], ks[n], TN)

        def store(n):
            _, j, _, _, mine, other = jobs[n]
            dk, dq = out[n]
            grads[other, :, part(2, j)] = (mass[n] * dps[n]).astype(jnp.bfloat16)
            grads[other, :, part(1, j)] = dk.astype(jnp.bfloat16)
            grads[mine, :, part(0, j)] = jnp.where(first, dq[:seq], dq[seq:]).astype(jnp.bfloat16)

        stages = list(zip((scores, softmax, masses, pool, t, ds, products, store), LAGS))
        for step in range(len(jobs) + LAGS[-1]):
            for stage, lag in stages:
                if 0 <= step - lag < len(jobs):
                    stage(step - lag)

        for k in range(together):
            p = i * together + k
            z = sum(pooled[n] * pooled[n + 1] for n in range(2 * blocks * k, 2 * blocks * (k + 1), 2))
            z = jnp.full((8, 128), 4.0 * jnp.sum(z), jnp.float32)
            c = info_ref[2 * count + p].astype(jnp.float32) * (1.0 / 256.0)
            y = info_ref[3 * count + p].astype(jnp.float32)
            loss_ref[...] += c * (jnp.maximum(z, 0.0) + jnp.log1p(jnp.exp(-jnp.abs(z))) - y * z)
            scale[p] = seq * c * (jax.nn.sigmoid(z) - y)
        return 0

    lax.fori_loop(0, count // together, some_pairs, 0)

    tile = acc.shape[2]
    for start in range(0, width, tile):
        columns = slice(start, start + tile)
        made = None
        for n, w_ref in enumerate(weights):
            part = grads[:, :, n * width : (n + 1) * width].reshape(2 * count * seq, width)
            part = mm(part, w_ref[columns, :], NT)
            made = part if made is None else made + part
        acc[...] = jnp.zeros_like(acc)
        for n in range(2 * count):
            acc[info_ref[n]] += made[n * seq : (n + 1) * seq] * scale[n % count, 0:1, 0:1]
        for n, out in enumerate((to_left, kept, to_right)):
            out[:, :, columns] = acc[n * recs : (n + 1) * recs].astype(jnp.bfloat16)


def pairs(info, own, left_x, right_x, weights, count):
    recs, seq, full = own.shape
    width = full // 3
    made = jax.ShapeDtypeStruct((recs, seq, width), jnp.bfloat16)
    return pl.pallas_call(
        functools.partial(pairs_kernel, count=count, together=1),
        out_shape=(made, made, made, jax.ShapeDtypeStruct((8, 128), jnp.float32)),
        in_specs=[SMEM, ANY] + [VMEM] * 5,
        out_specs=(VMEM,) * 4,
        scratch_shapes=[
            pltpu.VMEM((3 * recs, seq, full), jnp.bfloat16),
            pltpu.VMEM((2 * count, seq, full), jnp.bfloat16),
            pltpu.VMEM((count, 8, 128), jnp.float32),
            pltpu.VMEM((3 * recs, seq, 512), jnp.float32),
            pltpu.SemaphoreType.DMA,
        ],
        compiler_params=pltpu.CompilerParams(vmem_limit_bytes=34 << 20),
        cost_estimate=pl.CostEstimate(flops=20 << 30, bytes_accessed=12 << 20, transcendentals=2 << 20),
        name="pairs",
    )(info, own, left_x, right_x, *weights)


def row_total(value):
    count = lax.axis_size(AXES)
    routes = [[(i, i - i % ROW + (i + k) % ROW) for i in range(count)] for k in range(1, ROW)]
    return sum([lax.ppermute(value, AXES, route) for route in routes], value)


def column_total(value):
    rows = lax.axis_size(AXES) // ROW
    groups = [[h * ROW + x for h in range(rows)] for x in range(ROW)]
    spread = jnp.broadcast_to(value[0:1], (rows, value.shape[1]))
    met = lax.all_to_all(spread, AXES, 0, 0, axis_index_groups=groups, tiled=True)
    return jnp.sum(met, axis=0, keepdims=True)


def combine_kernel(a_ref, b_ref, c_ref, out_ref):
    i = pl.program_id(0)
    out_ref[0] = a_ref[i].astype(jnp.float32) + b_ref[i].astype(jnp.float32) + c_ref[i].astype(jnp.float32)


def combine(first, second, third):
    recs, seq, width = first.shape
    return pl.pallas_call(
        combine_kernel,
        grid=(recs,),
        out_shape=jax.ShapeDtypeStruct(first.shape, jnp.float32),
        in_specs=[VMEM] * 3,
        out_specs=pl.BlockSpec((1, seq, width), lambda i: (i, 0, 0)),
        compiler_params=pltpu.CompilerParams(vmem_limit_bytes=16 << 20),
        cost_estimate=pl.CostEstimate(flops=2 * first.size, bytes_accessed=4 * first.size, transcendentals=0),
        name="combine",
    )(first, second, third)


def on_device(records, w_query, w_key, w_value, pair_owner, pair_partner, confidence, labels):
    recs, seq, width = records.shape
    count = pair_owner.shape[0]
    devices = lax.axis_size(AXES)
    first_id = lax.axis_index(AXES) * recs
    weights = (w_query, w_key, w_value)

    left_records = from_behind(records, 1)
    right_records = from_behind(records, -1)
    own_info = jnp.concatenate(
        [pair_owner - first_id, jnp.mod(pair_partner - first_id, recs * devices), confidence, labels]
    )
    info = from_behind(own_info, 1)
    (own,) = project([records], weights)
    to_left, kept, to_right, loss = pairs(info, own, left_records, right_records, weights, count)
    from_right, from_left = from_behind(to_left, -1), from_behind(to_right, 1)
    loss = row_total(column_total(loss)) / (count * devices)
    record_grad = combine(from_right, kept, from_left)
    return (loss[0, 0], record_grad)


def solution(mesh):
    blocks = P(AXES, None, None)
    in_specs = (blocks, P(), P(), P(), P(AXES), P(AXES), P(AXES), P(AXES))
    return jax.shard_map(
        on_device, mesh=mesh, in_specs=in_specs, out_specs=(P(), blocks), check_vma=False
    )
```

time: 98.3 us -> 92.6 us (0.942)
  waiting for transfers between devices: 27.2 us -> 23.1 us
  other arithmetic: 4.9 us -> 1.97 us
  starting transfers between devices: 9.74 us -> 12.1 us
  Pallas kernels: 28 us -> 29.9 us
  blocking collectives: 20.1 us -> 18.5 us
  between operations: 1.93 us -> 0.71 us
    ppermute x5, waiting for transfers between devices: 27.2 us -> 20 us  [from_behind(): lax.ppermute(block, AXES, [((i - distance) % count, i) for i in range(cou...]
    add x2 -> x0, other arithmetic: 3.45 us -> none  [the longest x1 3.44 us: on_device(): from_right.astype(jnp.float32) + kept.astype(jnp.float32)]
    ppermute x3, waiting for transfers between devices: 0.01 us -> 3.11 us  [row_total(): return sum([lax.ppermute(value, AXES, route) for route in routes], value)]
    ppermute x3, starting transfers between devices: 1.53 us -> 4.18 us  [row_total(): return sum([lax.ppermute(value, AXES, route) for route in routes], value)]
    pallas_call x2, Pallas kernels: 24.6 us -> 26.5 us  [the longest x1 24.6 us: pairs(): pl.pallas_call(functools.partial(pairs_kernel, count=count, together=1),...]
    all_to_all x1, blocking collectives: 20.1 us -> 18.5 us  [column_total(): lax.all_to_all(spread, AXES, 0, 0, axis_index_groups=groups, tiled=True)]
  transfers between devices with their start and end apart: 8 -> 8, of which waited for: 3 -> 4; matrix products, arithmetic and copies ran while one was open for 2% -> 2% of each run, Pallas kernels for 12% -> 4%
where the time goes in v4:
time: 92.6 us; the launch traced here: 92.4 us
  Pallas kernels  29.9 us (32%)
  waiting for transfers between devices  23.1 us (25%)
  blocking collectives  18.5 us (20%)
  starting transfers between devices  12.1 us (13%)
  local copies, waits for them, and re-layouts  6.03 us (7%)
  other arithmetic  1.97 us (2%)
    pallas_call x1, Pallas kernels, pairs(): pl.pallas_call(functools.partial(pairs_kernel, count=count, together=1),...  24.6 us
    ppermute x5, waiting for transfers between devices, from_behind(): lax.ppermute(block, AXES, [((i - distance) % count, i) for i in range(cou...  20 us
    all_to_all x1, blocking collectives, column_total(): lax.all_to_all(spread, AXES, 0, 0, axis_index_groups=groups, tiled=True)  18.5 us
    ppermute x5, starting transfers between devices, from_behind(): lax.ppermute(block, AXES, [((i - distance) % count, i) for i in range(cou...  7.96 us
    unnamed x14, local copies, waits for them, and re-layouts  6 us
    ppermute x3, starting transfers between devices, row_total(): return sum([lax.ppermute(value, AXES, route) for route in routes], value)  4.18 us
    pallas_call x1, Pallas kernels, project(): pl.pallas_call(project_kernel, out_shape=[jax.ShapeDtypeStruct(block.shap...  3.42 us
    ppermute x3, waiting for transfers between devices, row_total(): return sum([lax.ppermute(value, AXES, route) for route in routes], value)  3.11 us
  transfers between devices with their start and end apart: 8, of which 4 were waited for; matrix products, arithmetic and copies ran while one was open for 2% of the time, Pallas kernels for 4%

profile of v4, /device:TPU:1, one launch (start us, length us, event | category | flops | bytes accessed | tf_op | source)
XLA Modules:
  0.0 92.4 jit_solution(11671986452849726934)
XLA Ops:
  0.6 6.4 %collective-permute-start.2 = (bf16[4,128,1024]{2,1,0:T(8,128)(2,1)}, bf16[4,128,1024]{2,1,0:T(8,128)(2,1)S(1)}, u32[]{:S(2)}, u32[]{:S(2)}) collective-permute-start(bf16[4,128,1024]{2,1,0:T(8,128)(2,1)} %refs_0_.1), channel_id=1, source_target_pairs={{1,0},{2,1},{3,2},{4,3},{5,4},{6,5},{7,6},{8,7},{9,8},{10,9},{11,1... | collective-permute-start | bytes 3145736 | tf_op jit(solution)/shard_map/ppermute | solution.py:27
  7.0 0.0 collective-permute-start.1
  7.0 0.7 and_select_fusion
  7.7 0.7 pad_add_fusion
  8.5 0.0 collective-permute-start
  8.5 0.0 copy-start
  8.5 1.6 %copy-done = bf16[1024,1024]{1,0:T(8,128)(2,1)S(1)} copy-done((bf16[1024,1024]{1,0:T(8,128)(2,1)S(1)}, bf16[1024,1024]{1,0:T(8,128)(2,1)}, u32[]{:S(2)}) %copy-start) | copy-done | bytes 2097176
  10.1 0.0 copy-start.2
  10.1 1.6 %copy-done.2 = bf16[1024,1024]{1,0:T(8,128)(2,1)S(1)} copy-done((bf16[1024,1024]{1,0:T(8,128)(2,1)S(1)}, bf16[1024,1024]{1,0:T(8,128)(2,1)}, u32[]{:S(2)}) %copy-start.2) | copy-done | bytes 2097176
  11.7 0.0 copy-start.4
  11.7 1.6 %copy-done.4 = bf16[1024,1024]{1,0:T(8,128)(2,1)S(1)} copy-done((bf16[1024,1024]{1,0:T(8,128)(2,1)S(1)}, bf16[1024,1024]{1,0:T(8,128)(2,1)}, u32[]{:S(2)}) %copy-start.4) | copy-done | bytes 2097176
  13.3 0.0 copy-start.6
  13.3 1.2 %copy-done.6 = bf16[4,128,1024]{2,1,0:T(8,128)(2,1)S(1)} copy-done((bf16[4,128,1024]{2,1,0:T(8,128)(2,1)S(1)}, bf16[4,128,1024]{2,1,0:T(8,128)(2,1)}, u32[]{:S(2)}) %copy-start.6) | copy-done | bytes 1048600
  14.5 0.0 copy-start.1
  14.5 0.0 copy-start.3
  14.5 0.0 copy-start.5
  14.5 3.4 %project.1.own_ref = bf16[4,128,3072]{2,1,0:T(8,128)(2,1)S(1)} custom-call(bf16[4,128,1024]{2,1,0:T(8,128)(2,1)S(1)} %copy-done.6, bf16[1024,1024]{1,0:T(8,128)(2,1)S(1)} %copy-done, bf16[1024,1024]{1,0:T(8,128)(2,1)S(1)} %copy-done.2, bf16[1024,1024]{1,0:T(8,128)(2,1)S(1)} %copy-done.4), custom_call_target="tpu_custom_call" | custom-call | flops 3221225472 | bytes 14680064 | tf_op jit(solution)/shard_map/project/pallas_call | solution.py:43
  17.9 18.2 %collective-permute-done.info_ref = s32[16]{0:T(128)S(1)} collective-permute-done((s32[16]{0:T(128)S(1)}, s32[16]{0:T(128)S(1)}, u32[]{:S(2)}, u32[]{:S(2)}) %collective-permute-start) | collective-permute-done | bytes 96 | tf_op jit(solution)/shard_map/ppermute | solution.py:27
  36.1 0.0 collective-permute-done.2.right_x
  36.1 0.0 collective-permute-done.1.left_x
  36.1 0.0 copy-done.1
  36.1 0.0 copy-done.3
  36.1 0.0 copy-done.5
  36.1 24.6 %pairs.1 = (bf16[4,128,1024]{2,1,0:T(8,128)(2,1)}, bf16[4,128,1024]{2,1,0:T(8,128)(2,1)S(1)}, bf16[4,128,1024]{2,1,0:T(8,128)(2,1)}, f32[8,128]{1,0:T(8,128)S(1)}) custom-call(s32[16]{0:T(128)S(1)} %collective-permute-done.info_ref, bf16[4,128,3072]{2,1,0:T(8,128)(2,1)S(1)} %project.1.own_ref, bf16[4,128,1024]{2,1,0:T(8,128)(2,1)S(1)} %collective-permute-done.1.left_x, ...), custom_call_target="tpu_custom_call" | custom-call | flops 21474836480 | bytes 12582912 | tf_op jit(solution)/shard_map/pairs/pallas_call | solution.py:172
  60.7 0.1 collective-permute-start.6
  60.8 1.5 %collective-permute-start.7 = (bf16[4,128,1024]{2,1,0:T(8,128)(2,1)}, bf16[4,128,1024]{2,1,0:T(8,128)(2,1)S(1)}, u32[]{:S(2)}, u32[]{:S(2)}) collective-permute-start(bf16[4,128,1024]{2,1,0:T(8,128)(2,1)} %get-tuple-element.9), channel_id=1, source_target_pairs={{255,0},{0,1},{1,2},{2,3},{3,4},{4,5},{5,6},{6,7},{7,8},{8,9},{9,1... | collective-permute-start | bytes 3145736 | tf_op jit(solution)/shard_map/ppermute | solution.py:27
  62.3 18.5 %all_to_all.6 = f32[64,1,128]{2,1,0:T(1,128)S(1)} all-to-all(f32[64,1,128]{2,1,0:T(1,128)S(1)} %broadcast_in_dim.8), channel_id=1, replica_groups={{0,4,8,12,16,20,24,28,32,36,40,44,48,52,56,60,64,68,72,76,80,84,88,92,9..., dimensions={0} | all-to-all | bytes 65536 | tf_op jit(solution)/shard_map/all_to_all | solution.py:200
  80.8 0.1 collective-permute-start.4
  80.9 3.6 %collective-permute-start.5 = (f32[1,128]{1,0:T(1,128)S(1)}, f32[1,128]{1,0:T(1,128)S(1)}, u32[]{:S(2)}, u32[]{:S(2)}) collective-permute-start(f32[1,128]{1,0:T(1,128)S(1)} %bitcast.9), channel_id=1, source_target_pairs={{0,3},{1,0},{2,1},{3,2},{4,7},{5,4},{6,5},{7,6},{8,11},{9,8},{10,9... | collective-permute-start | bytes 1544 | tf_op jit(solution)/shard_map/ppermute | solution.py:193
  84.5 0.5 collective-permute-start.3
  85.0 0.0 collective-permute-done.4
  85.0 0.9 collective-permute-done.5
  85.9 2.2 %collective-permute-done.3 = f32[1,128]{1,0:T(1,128)S(1)} collective-permute-done((f32[1,128]{1,0:T(1,128)S(1)}, f32[1,128]{1,0:T(1,128)S(1)}, u32[]{:S(2)}, u32[]{:S(2)}) %collective-permute-start.3) | collective-permute-done | bytes 544 | tf_op jit(solution)/shard_map/ppermute | solution.py:193
  88.1 0.5 add_multiply_fusion
  88.6 0.0 collective-permute-done.6.a_ref
  88.6 1.8 %collective-permute-done.7.c_ref = bf16[4,128,1024]{2,1,0:T(8,128)(2,1)S(1)} collective-permute-done((bf16[4,128,1024]{2,1,0:T(8,128)(2,1)}, bf16[4,128,1024]{2,1,0:T(8,128)(2,1)S(1)}, u32[]{:S(2)}, u32[]{:S(2)}) %collective-permute-start.7) | collective-permute-done | bytes 1048608 | tf_op jit(solution)/shard_map/ppermute | solution.py:27
  90.4 1.9 %combine.1 = f32[4,128,1024]{2,1,0:T(8,128)} custom-call(bf16[4,128,1024]{2,1,0:T(8,128)(2,1)S(1)} %collective-permute-done.6.a_ref, bf16[4,128,1024]{2,1,0:T(8,128)(2,1)S(1)} %get-tuple-element.8.b_ref, bf16[4,128,1024]{2,1,0:T(8,128)(2,1)S(1)} %collective-permute-done.7.c_ref), custom_call_target="tpu_custom_call" | custom-call | flops 1048576 | bytes 2097152 | tf_op jit(solution)/shard_map/combine/pallas_call | solution.py:211
  (3 shorter events, 0.0 us)
Async XLA Ops:
  0.6 35.5 %collective-permute-start.2 = (bf16[4,128,1024]{2,1,0:T(8,128)(2,1)}, bf16[4,128,1024]{2,1,0:T(8,128)(2,1)S(1)}, u32[]{:S(2)}, u32[]{:S(2)}) collective-permute-start(bf16[4,128,1024]{2,1,0:T(8,128)(2,1)} %refs_0_.1), channel_id=1, source_target_pairs={{1,0},{2,1},{3,2},{4,3},{5,4},{6,5},{7,6},{8,7},{9,8},{10,9},{11,1... | collective-permute-start | bytes 3145736 | tf_op jit(solution)/shard_map/ppermute | solution.py:27
  7.0 29.1 %collective-permute-start.1 = (bf16[4,128,1024]{2,1,0:T(8,128)(2,1)}, bf16[4,128,1024]{2,1,0:T(8,128)(2,1)S(1)}, u32[]{:S(2)}, u32[]{:S(2)}) collective-permute-start(bf16[4,128,1024]{2,1,0:T(8,128)(2,1)} %refs_0_.1), channel_id=1, source_target_pairs={{255,0},{0,1},{1,2},{2,3},{3,4},{4,5},{5,6},{6,7},{7,8},{8,9},{9,1... | collective-permute-start | bytes 3145736 | tf_op jit(solution)/shard_map/ppermute | solution.py:27
  8.5 27.6 %collective-permute-start = (s32[16]{0:T(128)S(1)}, s32[16]{0:T(128)S(1)}, u32[]{:S(2)}, u32[]{:S(2)}) collective-permute-start(s32[16]{0:T(128)S(1)} %pad_add_fusion), channel_id=1, source_target_pairs={{255,0},{0,1},{1,2},{2,3},{3,4},{4,5},{5,6},{6,7},{7,8},{8,9},{9,1... | collective-permute-start | bytes 200 | tf_op jit(solution)/shard_map/ppermute | solution.py:27
  8.5 1.6 %copy-start = (bf16[1024,1024]{1,0:T(8,128)(2,1)S(1)}, bf16[1024,1024]{1,0:T(8,128)(2,1)}, u32[]{:S(2)}) copy-start(bf16[1024,1024]{1,0:T(8,128)(2,1)} %wq_ref.1) | copy-start | bytes 6291460
  10.1 1.6 %copy-start.2 = (bf16[1024,1024]{1,0:T(8,128)(2,1)S(1)}, bf16[1024,1024]{1,0:T(8,128)(2,1)}, u32[]{:S(2)}) copy-start(bf16[1024,1024]{1,0:T(8,128)(2,1)} %wk_ref.1) | copy-start | bytes 6291460
  11.7 1.6 %copy-start.4 = (bf16[1024,1024]{1,0:T(8,128)(2,1)S(1)}, bf16[1024,1024]{1,0:T(8,128)(2,1)}, u32[]{:S(2)}) copy-start(bf16[1024,1024]{1,0:T(8,128)(2,1)} %wv_ref.1) | copy-start | bytes 6291460
  13.3 1.2 %copy-start.6 = (bf16[4,128,1024]{2,1,0:T(8,128)(2,1)S(1)}, bf16[4,128,1024]{2,1,0:T(8,128)(2,1)}, u32[]{:S(2)}) copy-start(bf16[4,128,1024]{2,1,0:T(8,128)(2,1)} %refs_0_.1) | copy-start | bytes 3145732
  14.5 21.6 %copy-start.1 = (bf16[1024,1024]{1,0:T(8,128)(2,1)S(1)}, bf16[1024,1024]{1,0:T(8,128)(2,1)}, u32[]{:S(2)}) copy-start(bf16[1024,1024]{1,0:T(8,128)(2,1)} %wq_ref.1) | copy-start | bytes 6291460
  14.5 21.6 %copy-start.3 = (bf16[1024,1024]{1,0:T(8,128)(2,1)S(1)}, bf16[1024,1024]{1,0:T(8,128)(2,1)}, u32[]{:S(2)}) copy-start(bf16[1024,1024]{1,0:T(8,128)(2,1)} %wk_ref.1) | copy-start | bytes 6291460
  14.5 21.6 %copy-start.5 = (bf16[1024,1024]{1,0:T(8,128)(2,1)S(1)}, bf16[1024,1024]{1,0:T(8,128)(2,1)}, u32[]{:S(2)}) copy-start(bf16[1024,1024]{1,0:T(8,128)(2,1)} %wv_ref.1) | copy-start | bytes 6291460
  60.7 27.9 %collective-permute-start.6 = (bf16[4,128,1024]{2,1,0:T(8,128)(2,1)}, bf16[4,128,1024]{2,1,0:T(8,128)(2,1)S(1)}, u32[]{:S(2)}, u32[]{:S(2)}) collective-permute-start(bf16[4,128,1024]{2,1,0:T(8,128)(2,1)} %get-tuple-element.7), channel_id=1, source_target_pairs={{1,0},{2,1},{3,2},{4,3},{5,4},{6,5},{7,6},{8,7},{9,8},{10,9},{11,1... | collective-permute-start | bytes 3145736 | tf_op jit(solution)/shard_map/ppermute | solution.py:27
  60.8 29.6 %collective-permute-start.7 = (bf16[4,128,1024]{2,1,0:T(8,128)(2,1)}, bf16[4,128,1024]{2,1,0:T(8,128)(2,1)S(1)}, u32[]{:S(2)}, u32[]{:S(2)}) collective-permute-start(bf16[4,128,1024]{2,1,0:T(8,128)(2,1)} %get-tuple-element.9), channel_id=1, source_target_pairs={{255,0},{0,1},{1,2},{2,3},{3,4},{4,5},{5,6},{6,7},{7,8},{8,9},{9,1... | collective-permute-start | bytes 3145736 | tf_op jit(solution)/shard_map/ppermute | solution.py:27
  80.8 4.2 %collective-permute-start.4 = (f32[1,128]{1,0:T(1,128)S(1)}, f32[1,128]{1,0:T(1,128)S(1)}, u32[]{:S(2)}, u32[]{:S(2)}) collective-permute-start(f32[1,128]{1,0:T(1,128)S(1)} %bitcast.8), channel_id=1, source_target_pairs={{0,2},{1,3},{2,0},{3,1},{4,6},{5,7},{6,4},{7,5},{8,10},{9,11},{10,... | collective-permute-start | bytes 1544 | tf_op jit(solution)/shard_map/ppermute | solution.py:193
  80.9 5.0 %collective-permute-start.5 = (f32[1,128]{1,0:T(1,128)S(1)}, f32[1,128]{1,0:T(1,128)S(1)}, u32[]{:S(2)}, u32[]{:S(2)}) collective-permute-start(f32[1,128]{1,0:T(1,128)S(1)} %bitcast.9), channel_id=1, source_target_pairs={{0,3},{1,0},{2,1},{3,2},{4,7},{5,4},{6,5},{7,6},{8,11},{9,8},{10,9... | collective-permute-start | bytes 1544 | tf_op jit(solution)/shard_map/ppermute | solution.py:193
  84.5 3.6 %collective-permute-start.3 = (f32[1,128]{1,0:T(1,128)S(1)}, f32[1,128]{1,0:T(1,128)S(1)}, u32[]{:S(2)}, u32[]{:S(2)}) collective-permute-start(f32[1,128]{1,0:T(1,128)S(1)} %bitcast.10), channel_id=1, source_target_pairs={{0,1},{1,2},{2,3},{3,0},{4,5},{5,6},{6,7},{7,4},{8,9},{9,10},{10,1... | collective-permute-start | bytes 1544 | tf_op jit(solution)/shard_map/ppermute | solution.py:193

commit v5 on v4

--- a/solution.py
+++ b/solution.py
@@ -170,7 +170,7 @@
     width = full // 3
     made = jax.ShapeDtypeStruct((recs, seq, width), jnp.bfloat16)
     return pl.pallas_call(
-        functools.partial(pairs_kernel, count=count, together=1),
+        functools.partial(pairs_kernel, count=count, together=2),
         out_shape=(made, made, made, jax.ShapeDtypeStruct((8, 128), jnp.float32)),
         in_specs=[SMEM, ANY] + [VMEM] * 5,
         out_specs=(VMEM,) * 4,
@@ -187,10 +187,10 @@
     )(info, own, left_x, right_x, *weights)
 
 
-def row_total(value):
+def row_met(value):
     count = lax.axis_size(AXES)
     routes = [[(i, i - i % ROW + (i + k) % ROW) for i in range(count)] for k in range(1, ROW)]
-    return sum([lax.ppermute(value, AXES, route) for route in routes], value)
+    return [lax.ppermute(value, AXES, route) for route in routes]
 
 
 def column_total(value):
@@ -236,8 +236,10 @@
     (own,) = project([records], weights)
     to_left, kept, to_right, loss = pairs(info, own, left_records, right_records, weights, count)
     from_right, from_left = from_behind(to_left, -1), from_behind(to_right, 1)
-    loss = row_total(column_total(loss)) / (count * devices)
-    record_grad = combine(from_right, kept, from_left)
+    loss = column_total(loss)
+    met = row_met(loss)
+    record_grad, loss = lax.optimization_barrier((combine(from_right, kept, from_left), loss))
+    loss = sum(met, loss) / (count * devices)
     return (loss[0, 0], record_grad)
 
 

time: 92.6 us -> 92.3 us (level)
    ppermute x5, waiting for transfers between devices: 20 us -> 23.4 us  [from_behind(): lax.ppermute(block, AXES, [((i - distance) % count, i) for i in range(cou...]
    ppermute x3, waiting for transfers between devices: 3.11 us -> 0.01 us  [row_met(): return [lax.ppermute(value, AXES, route) for route in routes]]
  transfers between devices with their start and end apart: 8 -> 8, of which waited for: 4 -> 2; matrix products, arithmetic and copies ran while one was open for 2% -> 2% of each run, Pallas kernels for 4% -> 6%
where the time goes in v5:
time: 92.3 us; the launch traced here: 92 us
  Pallas kernels  29.2 us (32%)
  waiting for transfers between devices  23.4 us (25%)
  blocking collectives  18.5 us (20%)
  starting transfers between devices  12.2 us (13%)
  local copies, waits for them, and re-layouts  6.03 us (7%)
  other arithmetic  1.97 us (2%)
    pallas_call x1, Pallas kernels, pairs(): pl.pallas_call(functools.partial(pairs_kernel, count=count, together=2),...  23.9 us
    ppermute x5, waiting for transfers between devices, from_behind(): lax.ppermute(block, AXES, [((i - distance) % count, i) for i in range(cou...  23.4 us
    all_to_all x1, blocking collectives, column_total(): lax.all_to_all(spread, AXES, 0, 0, axis_index_groups=groups, tiled=True)  18.5 us
    ppermute x5, starting transfers between devices, from_behind(): lax.ppermute(block, AXES, [((i - distance) % count, i) for i in range(cou...  8.14 us
    unnamed x14, local copies, waits for them, and re-layouts  6 us
    ppermute x3, starting transfers between devices, row_met(): return [lax.ppermute(value, AXES, route) for route in routes]  4.05 us
    pallas_call x1, Pallas kernels, project(): pl.pallas_call(project_kernel, out_shape=[jax.ShapeDtypeStruct(block.shap...  3.42 us
    pallas_call x1, Pallas kernels, combine(): pl.pallas_call(combine_kernel, grid=(recs,), out_shape=jax.ShapeDtypeStru...  1.93 us
  transfers between devices with their start and end apart: 8, of which 2 were waited for; matrix products, arithmetic and copies ran while one was open for 2% of the time, Pallas kernels for 6%

profile of v5, /device:TPU:1, one launch (start us, length us, event | category | flops | bytes accessed | tf_op | source)
XLA Modules:
  0.0 92.0 jit_solution(15597801009958355004)
XLA Ops:
  0.6 6.4 %collective-permute-start.2 = (bf16[4,128,1024]{2,1,0:T(8,128)(2,1)}, bf16[4,128,1024]{2,1,0:T(8,128)(2,1)S(1)}, u32[]{:S(2)}, u32[]{:S(2)}) collective-permute-start(bf16[4,128,1024]{2,1,0:T(8,128)(2,1)} %refs_0_.1), channel_id=1, source_target_pairs={{1,0},{2,1},{3,2},{4,3},{5,4},{6,5},{7,6},{8,7},{9,8},{10,9},{11,1... | collective-permute-start | bytes 3145736 | tf_op jit(solution)/shard_map/ppermute | solution.py:27
  7.0 0.0 collective-permute-start.1
  7.0 0.7 and_select_fusion
  7.7 0.7 pad_add_fusion
  8.5 0.2 collective-permute-start
  8.7 0.0 copy-start
  8.7 1.6 %copy-done = bf16[1024,1024]{1,0:T(8,128)(2,1)S(1)} copy-done((bf16[1024,1024]{1,0:T(8,128)(2,1)S(1)}, bf16[1024,1024]{1,0:T(8,128)(2,1)}, u32[]{:S(2)}) %copy-start) | copy-done | bytes 2097176
  10.3 0.0 copy-start.2
  10.3 1.6 %copy-done.2 = bf16[1024,1024]{1,0:T(8,128)(2,1)S(1)} copy-done((bf16[1024,1024]{1,0:T(8,128)(2,1)S(1)}, bf16[1024,1024]{1,0:T(8,128)(2,1)}, u32[]{:S(2)}) %copy-start.2) | copy-done | bytes 2097176
  11.9 0.0 copy-start.4
  11.9 1.6 %copy-done.4 = bf16[1024,1024]{1,0:T(8,128)(2,1)S(1)} copy-done((bf16[1024,1024]{1,0:T(8,128)(2,1)S(1)}, bf16[1024,1024]{1,0:T(8,128)(2,1)}, u32[]{:S(2)}) %copy-start.4) | copy-done | bytes 2097176
  13.5 0.0 copy-start.6
  13.5 1.2 %copy-done.6 = bf16[4,128,1024]{2,1,0:T(8,128)(2,1)S(1)} copy-done((bf16[4,128,1024]{2,1,0:T(8,128)(2,1)S(1)}, bf16[4,128,1024]{2,1,0:T(8,128)(2,1)}, u32[]{:S(2)}) %copy-start.6) | copy-done | bytes 1048600
  14.7 0.0 copy-start.1
  14.7 0.0 copy-start.3
  14.7 0.0 copy-start.5
  14.7 3.4 %project.1.own_ref = bf16[4,128,3072]{2,1,0:T(8,128)(2,1)S(1)} custom-call(bf16[4,128,1024]{2,1,0:T(8,128)(2,1)S(1)} %copy-done.6, bf16[1024,1024]{1,0:T(8,128)(2,1)S(1)} %copy-done, bf16[1024,1024]{1,0:T(8,128)(2,1)S(1)} %copy-done.2, bf16[1024,1024]{1,0:T(8,128)(2,1)S(1)} %copy-done.4), custom_call_target="tpu_custom_call" | custom-call | flops 3221225472 | bytes 14680064 | tf_op jit(solution)/shard_map/project/pallas_call | solution.py:43
  18.1 18.0 %collective-permute-done.info_ref = s32[16]{0:T(128)S(1)} collective-permute-done((s32[16]{0:T(128)S(1)}, s32[16]{0:T(128)S(1)}, u32[]{:S(2)}, u32[]{:S(2)}) %collective-permute-start) | collective-permute-done | bytes 96 | tf_op jit(solution)/shard_map/ppermute | solution.py:27
  36.1 0.0 collective-permute-done.2.right_x
  36.1 0.0 collective-permute-done.1.left_x
  36.1 0.0 copy-done.1
  36.1 0.0 copy-done.3
  36.1 0.0 copy-done.5
  36.1 23.9 %pairs.1 = (bf16[4,128,1024]{2,1,0:T(8,128)(2,1)}, bf16[4,128,1024]{2,1,0:T(8,128)(2,1)S(1)}, bf16[4,128,1024]{2,1,0:T(8,128)(2,1)}, f32[8,128]{1,0:T(8,128)S(1)}) custom-call(s32[16]{0:T(128)S(1)} %collective-permute-done.info_ref, bf16[4,128,3072]{2,1,0:T(8,128)(2,1)S(1)} %project.1.own_ref, bf16[4,128,1024]{2,1,0:T(8,128)(2,1)S(1)} %collective-permute-done.1.left_x, ...), custom_call_target="tpu_custom_call" | custom-call | flops 21474836480 | bytes 12582912 | tf_op jit(solution)/shard_map/pairs/pallas_call | solution.py:172
  60.0 0.1 collective-permute-start.3
  60.1 1.5 %collective-permute-start.4 = (bf16[4,128,1024]{2,1,0:T(8,128)(2,1)}, bf16[4,128,1024]{2,1,0:T(8,128)(2,1)S(1)}, u32[]{:S(2)}, u32[]{:S(2)}) collective-permute-start(bf16[4,128,1024]{2,1,0:T(8,128)(2,1)} %get-tuple-element.10), channel_id=1, source_target_pairs={{255,0},{0,1},{1,2},{2,3},{3,4},{4,5},{5,6},{6,7},{7,8},{8,9},{9,1... | collective-permute-start | bytes 3145736 | tf_op jit(solution)/shard_map/ppermute | solution.py:27
  61.6 18.5 %all_to_all.6 = f32[64,1,128]{2,1,0:T(1,128)S(1)} all-to-all(f32[64,1,128]{2,1,0:T(1,128)S(1)} %broadcast_in_dim.8), channel_id=1, replica_groups={{0,4,8,12,16,20,24,28,32,36,40,44,48,52,56,60,64,68,72,76,80,84,88,92,9..., dimensions={0} | all-to-all | bytes 65536 | tf_op jit(solution)/shard_map/all_to_all | solution.py:200
  80.1 3.4 %collective-permute-start.7 = (f32[1,128]{1,0:T(1,128)S(1)}, f32[1,128]{1,0:T(1,128)S(1)}, u32[]{:S(2)}, u32[]{:S(2)}) collective-permute-start(f32[1,128]{1,0:T(1,128)S(1)} %bitcast.7), channel_id=1, source_target_pairs={{0,3},{1,0},{2,1},{3,2},{4,7},{5,4},{6,5},{7,6},{8,11},{9,8},{10,9... | collective-permute-start | bytes 1544 | tf_op jit(solution)/shard_map/ppermute | solution.py:193
  83.5 0.0 collective-permute-start.6
  83.5 0.7 collective-permute-start.5
  84.2 0.0 collective-permute-done.3.a_ref
  84.2 5.4 %collective-permute-done.4.c_ref = bf16[4,128,1024]{2,1,0:T(8,128)(2,1)S(1)} collective-permute-done((bf16[4,128,1024]{2,1,0:T(8,128)(2,1)}, bf16[4,128,1024]{2,1,0:T(8,128)(2,1)S(1)}, u32[]{:S(2)}, u32[]{:S(2)}) %collective-permute-start.4) | collective-permute-done | bytes 1048608 | tf_op jit(solution)/shard_map/ppermute | solution.py:27
  89.5 1.9 %combine.1 = f32[4,128,1024]{2,1,0:T(8,128)} custom-call(bf16[4,128,1024]{2,1,0:T(8,128)(2,1)S(1)} %collective-permute-done.3.a_ref, bf16[4,128,1024]{2,1,0:T(8,128)(2,1)S(1)} %get-tuple-element.9.b_ref, bf16[4,128,1024]{2,1,0:T(8,128)(2,1)S(1)} %collective-permute-done.4.c_ref), custom_call_target="tpu_custom_call" | custom-call | flops 1048576 | bytes 2097152 | tf_op jit(solution)/shard_map/combine/pallas_call | solution.py:211
  91.5 0.0 collective-permute-done.7
  91.5 0.0 collective-permute-done.6
  91.5 0.0 collective-permute-done.5
  91.5 0.5 add_multiply_fusion
  (3 shorter events, 0.0 us)
Async XLA Ops:
  0.6 35.5 %collective-permute-start.2 = (bf16[4,128,1024]{2,1,0:T(8,128)(2,1)}, bf16[4,128,1024]{2,1,0:T(8,128)(2,1)S(1)}, u32[]{:S(2)}, u32[]{:S(2)}) collective-permute-start(bf16[4,128,1024]{2,1,0:T(8,128)(2,1)} %refs_0_.1), channel_id=1, source_target_pairs={{1,0},{2,1},{3,2},{4,3},{5,4},{6,5},{7,6},{8,7},{9,8},{10,9},{11,1... | collective-permute-start | bytes 3145736 | tf_op jit(solution)/shard_map/ppermute | solution.py:27
  7.0 29.1 %collective-permute-start.1 = (bf16[4,128,1024]{2,1,0:T(8,128)(2,1)}, bf16[4,128,1024]{2,1,0:T(8,128)(2,1)S(1)}, u32[]{:S(2)}, u32[]{:S(2)}) collective-permute-start(bf16[4,128,1024]{2,1,0:T(8,128)(2,1)} %refs_0_.1), channel_id=1, source_target_pairs={{255,0},{0,1},{1,2},{2,3},{3,4},{4,5},{5,6},{6,7},{7,8},{8,9},{9,1... | collective-permute-start | bytes 3145736 | tf_op jit(solution)/shard_map/ppermute | solution.py:27
  8.5 27.6 %collective-permute-start = (s32[16]{0:T(128)S(1)}, s32[16]{0:T(128)S(1)}, u32[]{:S(2)}, u32[]{:S(2)}) collective-permute-start(s32[16]{0:T(128)S(1)} %pad_add_fusion), channel_id=1, source_target_pairs={{255,0},{0,1},{1,2},{2,3},{3,4},{4,5},{5,6},{6,7},{7,8},{8,9},{9,1... | collective-permute-start | bytes 200 | tf_op jit(solution)/shard_map/ppermute | solution.py:27
  8.7 1.6 %copy-start = (bf16[1024,1024]{1,0:T(8,128)(2,1)S(1)}, bf16[1024,1024]{1,0:T(8,128)(2,1)}, u32[]{:S(2)}) copy-start(bf16[1024,1024]{1,0:T(8,128)(2,1)} %wq_ref.1) | copy-start | bytes 6291460
  10.3 1.6 %copy-start.2 = (bf16[1024,1024]{1,0:T(8,128)(2,1)S(1)}, bf16[1024,1024]{1,0:T(8,128)(2,1)}, u32[]{:S(2)}) copy-start(bf16[1024,1024]{1,0:T(8,128)(2,1)} %wk_ref.1) | copy-start | bytes 6291460
  11.9 1.6 %copy-start.4 = (bf16[1024,1024]{1,0:T(8,128)(2,1)S(1)}, bf16[1024,1024]{1,0:T(8,128)(2,1)}, u32[]{:S(2)}) copy-start(bf16[1024,1024]{1,0:T(8,128)(2,1)} %wv_ref.1) | copy-start | bytes 6291460
  13.5 1.2 %copy-start.6 = (bf16[4,128,1024]{2,1,0:T(8,128)(2,1)S(1)}, bf16[4,128,1024]{2,1,0:T(8,128)(2,1)}, u32[]{:S(2)}) copy-start(bf16[4,128,1024]{2,1,0:T(8,128)(2,1)} %refs_0_.1) | copy-start | bytes 3145732
  14.7 21.4 %copy-start.1 = (bf16[1024,1024]{1,0:T(8,128)(2,1)S(1)}, bf16[1024,1024]{1,0:T(8,128)(2,1)}, u32[]{:S(2)}) copy-start(bf16[1024,1024]{1,0:T(8,128)(2,1)} %wq_ref.1) | copy-start | bytes 6291460
  14.7 21.4 %copy-start.3 = (bf16[1024,1024]{1,0:T(8,128)(2,1)S(1)}, bf16[1024,1024]{1,0:T(8,128)(2,1)}, u32[]{:S(2)}) copy-start(bf16[1024,1024]{1,0:T(8,128)(2,1)} %wk_ref.1) | copy-start | bytes 6291460
  14.7 21.4 %copy-start.5 = (bf16[1024,1024]{1,0:T(8,128)(2,1)S(1)}, bf16[1024,1024]{1,0:T(8,128)(2,1)}, u32[]{:S(2)}) copy-start(bf16[1024,1024]{1,0:T(8,128)(2,1)} %wv_ref.1) | copy-start | bytes 6291460
  60.0 24.1 %collective-permute-start.3 = (bf16[4,128,1024]{2,1,0:T(8,128)(2,1)}, bf16[4,128,1024]{2,1,0:T(8,128)(2,1)S(1)}, u32[]{:S(2)}, u32[]{:S(2)}) collective-permute-start(bf16[4,128,1024]{2,1,0:T(8,128)(2,1)} %get-tuple-element.8), channel_id=1, source_target_pairs={{1,0},{2,1},{3,2},{4,3},{5,4},{6,5},{7,6},{8,7},{9,8},{10,9},{11,1... | collective-permute-start | bytes 3145736 | tf_op jit(solution)/shard_map/ppermute | solution.py:27
  60.1 29.4 %collective-permute-start.4 = (bf16[4,128,1024]{2,1,0:T(8,128)(2,1)}, bf16[4,128,1024]{2,1,0:T(8,128)(2,1)S(1)}, u32[]{:S(2)}, u32[]{:S(2)}) collective-permute-start(bf16[4,128,1024]{2,1,0:T(8,128)(2,1)} %get-tuple-element.10), channel_id=1, source_target_pairs={{255,0},{0,1},{1,2},{2,3},{3,4},{4,5},{5,6},{6,7},{7,8},{8,9},{9,1... | collective-permute-start | bytes 3145736 | tf_op jit(solution)/shard_map/ppermute | solution.py:27
  80.1 11.4 %collective-permute-start.7 = (f32[1,128]{1,0:T(1,128)S(1)}, f32[1,128]{1,0:T(1,128)S(1)}, u32[]{:S(2)}, u32[]{:S(2)}) collective-permute-start(f32[1,128]{1,0:T(1,128)S(1)} %bitcast.7), channel_id=1, source_target_pairs={{0,3},{1,0},{2,1},{3,2},{4,7},{5,4},{6,5},{7,6},{8,11},{9,8},{10,9... | collective-permute-start | bytes 1544 | tf_op jit(solution)/shard_map/ppermute | solution.py:193
  83.5 8.0 %collective-permute-start.6 = (f32[1,128]{1,0:T(1,128)S(1)}, f32[1,128]{1,0:T(1,128)S(1)}, u32[]{:S(2)}, u32[]{:S(2)}) collective-permute-start(f32[1,128]{1,0:T(1,128)S(1)} %bitcast.8), channel_id=1, source_target_pairs={{0,2},{1,3},{2,0},{3,1},{4,6},{5,7},{6,4},{7,5},{8,10},{9,11},{10,... | collective-permute-start | bytes 1544 | tf_op jit(solution)/shard_map/ppermute | solution.py:193
  83.5 8.0 %collective-permute-start.5 = (f32[1,128]{1,0:T(1,128)S(1)}, f32[1,128]{1,0:T(1,128)S(1)}, u32[]{:S(2)}, u32[]{:S(2)}) collective-permute-start(f32[1,128]{1,0:T(1,128)S(1)} %bitcast.9), channel_id=1, source_target_pairs={{0,1},{1,2},{2,3},{3,0},{4,5},{5,6},{6,7},{7,4},{8,9},{9,10},{10,1... | collective-permute-start | bytes 1544 | tf_op jit(solution)/shard_map/ppermute | solution.py:193

commit v6 on v5

--- a/solution.py
+++ b/solution.py
@@ -170,7 +170,7 @@
     width = full // 3
     made = jax.ShapeDtypeStruct((recs, seq, width), jnp.bfloat16)
     return pl.pallas_call(
-        functools.partial(pairs_kernel, count=count, together=2),
+        functools.partial(pairs_kernel, count=count, together=4),
         out_shape=(made, made, made, jax.ShapeDtypeStruct((8, 128), jnp.float32)),
         in_specs=[SMEM, ANY] + [VMEM] * 5,
         out_specs=(VMEM,) * 4,
@@ -201,19 +201,27 @@
     return jnp.sum(met, axis=0, keepdims=True)
 
 
-def combine_kernel(a_ref, b_ref, c_ref, out_ref):
-    i = pl.program_id(0)
-    out_ref[0] = a_ref[i].astype(jnp.float32) + b_ref[i].astype(jnp.float32) + c_ref[i].astype(jnp.float32)
+def combine_kernel(a_ref, b_ref, c_ref, out_ref, made, sems):
+    parts = sems.shape[0]
+    recs, seq, _ = made.shape
+    rows = recs * seq // parts
+    leaving = []
+    for n in range(parts):
+        at = (n * rows // seq, slice(n * rows % seq, n * rows % seq + rows))
+        made[at] = a_ref[at].astype(jnp.float32) + b_ref[at].astype(jnp.float32) + c_ref[at].astype(jnp.float32)
+        leaving.append(pltpu.make_async_copy(made.at[at], out_ref.at[at], sems.at[n]))
+        leaving[-1].start()
+    for copy in leaving:
+        copy.wait()
 
 
 def combine(first, second, third):
-    recs, seq, width = first.shape
     return pl.pallas_call(
         combine_kernel,
-        grid=(recs,),
         out_shape=jax.ShapeDtypeStruct(first.shape, jnp.float32),
         in_specs=[VMEM] * 3,
-        out_specs=pl.BlockSpec((1, seq, width), lambda i: (i, 0, 0)),
+        out_specs=pl.BlockSpec(memory_space=pltpu.HBM),
+        scratch_shapes=[pltpu.VMEM(first.shape, jnp.float32), pltpu.SemaphoreType.DMA((4,))],
         compiler_params=pltpu.CompilerParams(vmem_limit_bytes=16 << 20),
         cost_estimate=pl.CostEstimate(flops=2 * first.size, bytes_accessed=4 * first.size, transcendentals=0),
         name="combine",

time: 92.3 us -> 91.4 us (level)
    pallas_call x2, Pallas kernels: 25.8 us -> 24.9 us  [the longest x1 23.5 us: pairs(): pl.pallas_call(functools.partial(pairs_kernel, count=count, together=4),...]
  transfers between devices with their start and end apart: 8 -> 8, of which waited for: 2 -> 2; matrix products, arithmetic and copies ran while one was open for 2% -> 2% of each run, Pallas kernels for 6% -> 5%
where the time goes in v6:
time: 91.4 us; the launch traced here: 91.1 us
  Pallas kernels  28.3 us (31%)
  waiting for transfers between devices  23.5 us (26%)
  blocking collectives  18.5 us (20%)
  starting transfers between devices  12 us (13%)
  local copies, waits for them, and re-layouts  6.03 us (7%)
  other arithmetic  1.97 us (2%)
    ppermute x5, waiting for transfers between devices, from_behind(): lax.ppermute(block, AXES, [((i - distance) % count, i) for i in range(cou...  23.5 us
    pallas_call x1, Pallas kernels, pairs(): pl.pallas_call(functools.partial(pairs_kernel, count=count, together=4),...  23.5 us
    all_to_all x1, blocking collectives, column_total(): lax.all_to_all(spread, AXES, 0, 0, axis_index_groups=groups, tiled=True)  18.5 us
    ppermute x5, starting transfers between devices, from_behind(): lax.ppermute(block, AXES, [((i - distance) % count, i) for i in range(cou...  7.96 us
    unnamed x14, local copies, waits for them, and re-layouts  6 us
    ppermute x3, starting transfers between devices, row_met(): return [lax.ppermute(value, AXES, route) for route in routes]  4.05 us
    pallas_call x1, Pallas kernels, project(): pl.pallas_call(project_kernel, out_shape=[jax.ShapeDtypeStruct(block.shap...  3.42 us
  transfers between devices with their start and end apart: 8, of which 2 were waited for; matrix products, arithmetic and copies ran while one was open for 2% of the time, Pallas kernels for 5%

profile of v6, /device:TPU:1, one launch (start us, length us, event | category | flops | bytes accessed | tf_op | source)
XLA Modules:
  0.0 91.1 jit_solution(7383860222663390734)
XLA Ops:
  0.6 6.4 %collective-permute-start.2 = (bf16[4,128,1024]{2,1,0:T(8,128)(2,1)}, bf16[4,128,1024]{2,1,0:T(8,128)(2,1)S(1)}, u32[]{:S(2)}, u32[]{:S(2)}) collective-permute-start(bf16[4,128,1024]{2,1,0:T(8,128)(2,1)} %refs_0_.1), channel_id=1, source_target_pairs={{1,0},{2,1},{3,2},{4,3},{5,4},{6,5},{7,6},{8,7},{9,8},{10,9},{11,1... | collective-permute-start | bytes 3145736 | tf_op jit(solution)/shard_map/ppermute | solution.py:27
  7.0 0.0 collective-permute-start.1
  7.0 0.7 and_select_fusion
  7.7 0.7 pad_add_fusion
  8.5 0.0 collective-permute-start
  8.5 0.0 copy-start
  8.5 1.6 %copy-done = bf16[1024,1024]{1,0:T(8,128)(2,1)S(1)} copy-done((bf16[1024,1024]{1,0:T(8,128)(2,1)S(1)}, bf16[1024,1024]{1,0:T(8,128)(2,1)}, u32[]{:S(2)}) %copy-start) | copy-done | bytes 2097176
  10.1 0.0 copy-start.2
  10.1 1.6 %copy-done.2 = bf16[1024,1024]{1,0:T(8,128)(2,1)S(1)} copy-done((bf16[1024,1024]{1,0:T(8,128)(2,1)S(1)}, bf16[1024,1024]{1,0:T(8,128)(2,1)}, u32[]{:S(2)}) %copy-start.2) | copy-done | bytes 2097176
  11.7 0.0 copy-start.4
  11.7 1.6 %copy-done.4 = bf16[1024,1024]{1,0:T(8,128)(2,1)S(1)} copy-done((bf16[1024,1024]{1,0:T(8,128)(2,1)S(1)}, bf16[1024,1024]{1,0:T(8,128)(2,1)}, u32[]{:S(2)}) %copy-start.4) | copy-done | bytes 2097176
  13.3 0.0 copy-start.6
  13.3 1.2 %copy-done.6 = bf16[4,128,1024]{2,1,0:T(8,128)(2,1)S(1)} copy-done((bf16[4,128,1024]{2,1,0:T(8,128)(2,1)S(1)}, bf16[4,128,1024]{2,1,0:T(8,128)(2,1)}, u32[]{:S(2)}) %copy-start.6) | copy-done | bytes 1048600
  14.5 0.0 copy-start.1
  14.5 0.0 copy-start.3
  14.5 0.0 copy-start.5
  14.5 3.4 %project.1.own_ref = bf16[4,128,3072]{2,1,0:T(8,128)(2,1)S(1)} custom-call(bf16[4,128,1024]{2,1,0:T(8,128)(2,1)S(1)} %copy-done.6, bf16[1024,1024]{1,0:T(8,128)(2,1)S(1)} %copy-done, bf16[1024,1024]{1,0:T(8,128)(2,1)S(1)} %copy-done.2, bf16[1024,1024]{1,0:T(8,128)(2,1)S(1)} %copy-done.4), custom_call_target="tpu_custom_call" | custom-call | flops 3221225472 | bytes 14680064 | tf_op jit(solution)/shard_map/project/pallas_call | solution.py:43
  17.9 18.2 %collective-permute-done.info_ref = s32[16]{0:T(128)S(1)} collective-permute-done((s32[16]{0:T(128)S(1)}, s32[16]{0:T(128)S(1)}, u32[]{:S(2)}, u32[]{:S(2)}) %collective-permute-start) | collective-permute-done | bytes 96 | tf_op jit(solution)/shard_map/ppermute | solution.py:27
  36.1 0.0 collective-permute-done.2.right_x
  36.1 0.0 collective-permute-done.1.left_x
  36.1 0.0 copy-done.1
  36.1 0.0 copy-done.3
  36.1 0.0 copy-done.5
  36.1 23.5 %pairs.1 = (bf16[4,128,1024]{2,1,0:T(8,128)(2,1)}, bf16[4,128,1024]{2,1,0:T(8,128)(2,1)S(1)}, bf16[4,128,1024]{2,1,0:T(8,128)(2,1)}, f32[8,128]{1,0:T(8,128)S(1)}) custom-call(s32[16]{0:T(128)S(1)} %collective-permute-done.info_ref, bf16[4,128,3072]{2,1,0:T(8,128)(2,1)S(1)} %project.1.own_ref, bf16[4,128,1024]{2,1,0:T(8,128)(2,1)S(1)} %collective-permute-done.1.left_x, ...), custom_call_target="tpu_custom_call" | custom-call | flops 21474836480 | bytes 12582912 | tf_op jit(solution)/shard_map/pairs/pallas_call | solution.py:172
  59.6 0.1 collective-permute-start.3
  59.7 1.5 %collective-permute-start.4 = (bf16[4,128,1024]{2,1,0:T(8,128)(2,1)}, bf16[4,128,1024]{2,1,0:T(8,128)(2,1)S(1)}, u32[]{:S(2)}, u32[]{:S(2)}) collective-permute-start(bf16[4,128,1024]{2,1,0:T(8,128)(2,1)} %get-tuple-element.10), channel_id=1, source_target_pairs={{255,0},{0,1},{1,2},{2,3},{3,4},{4,5},{5,6},{6,7},{7,8},{8,9},{9,1... | collective-permute-start | bytes 3145736 | tf_op jit(solution)/shard_map/ppermute | solution.py:27
  61.2 18.5 %all_to_all.6 = f32[64,1,128]{2,1,0:T(1,128)S(1)} all-to-all(f32[64,1,128]{2,1,0:T(1,128)S(1)} %broadcast_in_dim.8), channel_id=1, replica_groups={{0,4,8,12,16,20,24,28,32,36,40,44,48,52,56,60,64,68,72,76,80,84,88,92,9..., dimensions={0} | all-to-all | bytes 65536 | tf_op jit(solution)/shard_map/all_to_all | solution.py:200
  79.7 3.4 %collective-permute-start.7 = (f32[1,128]{1,0:T(1,128)S(1)}, f32[1,128]{1,0:T(1,128)S(1)}, u32[]{:S(2)}, u32[]{:S(2)}) collective-permute-start(f32[1,128]{1,0:T(1,128)S(1)} %bitcast.7), channel_id=1, source_target_pairs={{0,3},{1,0},{2,1},{3,2},{4,7},{5,4},{6,5},{7,6},{8,11},{9,8},{10,9... | collective-permute-start | bytes 1544 | tf_op jit(solution)/shard_map/ppermute | solution.py:193
  83.1 0.0 collective-permute-start.6
  83.1 0.7 collective-permute-start.5
  83.7 0.0 collective-permute-done.3.a_ref
  83.7 5.4 %collective-permute-done.4.c_ref = bf16[4,128,1024]{2,1,0:T(8,128)(2,1)S(1)} collective-permute-done((bf16[4,128,1024]{2,1,0:T(8,128)(2,1)}, bf16[4,128,1024]{2,1,0:T(8,128)(2,1)S(1)}, u32[]{:S(2)}, u32[]{:S(2)}) %collective-permute-start.4) | collective-permute-done | bytes 1048608 | tf_op jit(solution)/shard_map/ppermute | solution.py:27
  89.1 1.4 %combine.1 = f32[4,128,1024]{2,1,0:T(8,128)} custom-call(bf16[4,128,1024]{2,1,0:T(8,128)(2,1)S(1)} %collective-permute-done.3.a_ref, bf16[4,128,1024]{2,1,0:T(8,128)(2,1)S(1)} %get-tuple-element.9.b_ref, bf16[4,128,1024]{2,1,0:T(8,128)(2,1)S(1)} %collective-permute-done.4.c_ref), custom_call_target="tpu_custom_call" | custom-call | flops 1048576 | bytes 2097152 | tf_op jit(solution)/shard_map/combine/pallas_call | solution.py:219
  90.5 0.0 collective-permute-done.7
  90.6 0.0 collective-permute-done.6
  90.6 0.0 collective-permute-done.5
  90.6 0.5 add_multiply_fusion
  (3 shorter events, 0.0 us)
Async XLA Ops:
  0.6 35.5 %collective-permute-start.2 = (bf16[4,128,1024]{2,1,0:T(8,128)(2,1)}, bf16[4,128,1024]{2,1,0:T(8,128)(2,1)S(1)}, u32[]{:S(2)}, u32[]{:S(2)}) collective-permute-start(bf16[4,128,1024]{2,1,0:T(8,128)(2,1)} %refs_0_.1), channel_id=1, source_target_pairs={{1,0},{2,1},{3,2},{4,3},{5,4},{6,5},{7,6},{8,7},{9,8},{10,9},{11,1... | collective-permute-start | bytes 3145736 | tf_op jit(solution)/shard_map/ppermute | solution.py:27
  7.0 29.1 %collective-permute-start.1 = (bf16[4,128,1024]{2,1,0:T(8,128)(2,1)}, bf16[4,128,1024]{2,1,0:T(8,128)(2,1)S(1)}, u32[]{:S(2)}, u32[]{:S(2)}) collective-permute-start(bf16[4,128,1024]{2,1,0:T(8,128)(2,1)} %refs_0_.1), channel_id=1, source_target_pairs={{255,0},{0,1},{1,2},{2,3},{3,4},{4,5},{5,6},{6,7},{7,8},{8,9},{9,1... | collective-permute-start | bytes 3145736 | tf_op jit(solution)/shard_map/ppermute | solution.py:27
  8.5 27.6 %collective-permute-start = (s32[16]{0:T(128)S(1)}, s32[16]{0:T(128)S(1)}, u32[]{:S(2)}, u32[]{:S(2)}) collective-permute-start(s32[16]{0:T(128)S(1)} %pad_add_fusion), channel_id=1, source_target_pairs={{255,0},{0,1},{1,2},{2,3},{3,4},{4,5},{5,6},{6,7},{7,8},{8,9},{9,1... | collective-permute-start | bytes 200 | tf_op jit(solution)/shard_map/ppermute | solution.py:27
  8.5 1.6 %copy-start = (bf16[1024,1024]{1,0:T(8,128)(2,1)S(1)}, bf16[1024,1024]{1,0:T(8,128)(2,1)}, u32[]{:S(2)}) copy-start(bf16[1024,1024]{1,0:T(8,128)(2,1)} %wq_ref.1) | copy-start | bytes 6291460
  10.1 1.6 %copy-start.2 = (bf16[1024,1024]{1,0:T(8,128)(2,1)S(1)}, bf16[1024,1024]{1,0:T(8,128)(2,1)}, u32[]{:S(2)}) copy-start(bf16[1024,1024]{1,0:T(8,128)(2,1)} %wk_ref.1) | copy-start | bytes 6291460
  11.7 1.6 %copy-start.4 = (bf16[1024,1024]{1,0:T(8,128)(2,1)S(1)}, bf16[1024,1024]{1,0:T(8,128)(2,1)}, u32[]{:S(2)}) copy-start(bf16[1024,1024]{1,0:T(8,128)(2,1)} %wv_ref.1) | copy-start | bytes 6291460
  13.3 1.2 %copy-start.6 = (bf16[4,128,1024]{2,1,0:T(8,128)(2,1)S(1)}, bf16[4,128,1024]{2,1,0:T(8,128)(2,1)}, u32[]{:S(2)}) copy-start(bf16[4,128,1024]{2,1,0:T(8,128)(2,1)} %refs_0_.1) | copy-start | bytes 3145732
  14.5 21.6 %copy-start.1 = (bf16[1024,1024]{1,0:T(8,128)(2,1)S(1)}, bf16[1024,1024]{1,0:T(8,128)(2,1)}, u32[]{:S(2)}) copy-start(bf16[1024,1024]{1,0:T(8,128)(2,1)} %wq_ref.1) | copy-start | bytes 6291460
  14.5 21.6 %copy-start.3 = (bf16[1024,1024]{1,0:T(8,128)(2,1)S(1)}, bf16[1024,1024]{1,0:T(8,128)(2,1)}, u32[]{:S(2)}) copy-start(bf16[1024,1024]{1,0:T(8,128)(2,1)} %wk_ref.1) | copy-start | bytes 6291460
  14.5 21.6 %copy-start.5 = (bf16[1024,1024]{1,0:T(8,128)(2,1)S(1)}, bf16[1024,1024]{1,0:T(8,128)(2,1)}, u32[]{:S(2)}) copy-start(bf16[1024,1024]{1,0:T(8,128)(2,1)} %wv_ref.1) | copy-start | bytes 6291460
  59.6 24.1 %collective-permute-start.3 = (bf16[4,128,1024]{2,1,0:T(8,128)(2,1)}, bf16[4,128,1024]{2,1,0:T(8,128)(2,1)S(1)}, u32[]{:S(2)}, u32[]{:S(2)}) collective-permute-start(bf16[4,128,1024]{2,1,0:T(8,128)(2,1)} %get-tuple-element.8), channel_id=1, source_target_pairs={{1,0},{2,1},{3,2},{4,3},{5,4},{6,5},{7,6},{8,7},{9,8},{10,9},{11,1... | collective-permute-start | bytes 3145736 | tf_op jit(solution)/shard_map/ppermute | solution.py:27
  59.7 29.4 %collective-permute-start.4 = (bf16[4,128,1024]{2,1,0:T(8,128)(2,1)}, bf16[4,128,1024]{2,1,0:T(8,128)(2,1)S(1)}, u32[]{:S(2)}, u32[]{:S(2)}) collective-permute-start(bf16[4,128,1024]{2,1,0:T(8,128)(2,1)} %get-tuple-element.10), channel_id=1, source_target_pairs={{255,0},{0,1},{1,2},{2,3},{3,4},{4,5},{5,6},{6,7},{7,8},{8,9},{9,1... | collective-permute-start | bytes 3145736 | tf_op jit(solution)/shard_map/ppermute | solution.py:27
  79.7 10.9 %collective-permute-start.7 = (f32[1,128]{1,0:T(1,128)S(1)}, f32[1,128]{1,0:T(1,128)S(1)}, u32[]{:S(2)}, u32[]{:S(2)}) collective-permute-start(f32[1,128]{1,0:T(1,128)S(1)} %bitcast.7), channel_id=1, source_target_pairs={{0,3},{1,0},{2,1},{3,2},{4,7},{5,4},{6,5},{7,6},{8,11},{9,8},{10,9... | collective-permute-start | bytes 1544 | tf_op jit(solution)/shard_map/ppermute | solution.py:193
  83.1 7.5 %collective-permute-start.6 = (f32[1,128]{1,0:T(1,128)S(1)}, f32[1,128]{1,0:T(1,128)S(1)}, u32[]{:S(2)}, u32[]{:S(2)}) collective-permute-start(f32[1,128]{1,0:T(1,128)S(1)} %bitcast.8), channel_id=1, source_target_pairs={{0,2},{1,3},{2,0},{3,1},{4,6},{5,7},{6,4},{7,5},{8,10},{9,11},{10,... | collective-permute-start | bytes 1544 | tf_op jit(solution)/shard_map/ppermute | solution.py:193
  83.1 7.5 %collective-permute-start.5 = (f32[1,128]{1,0:T(1,128)S(1)}, f32[1,128]{1,0:T(1,128)S(1)}, u32[]{:S(2)}, u32[]{:S(2)}) collective-permute-start(f32[1,128]{1,0:T(1,128)S(1)} %bitcast.9), channel_id=1, source_target_pairs={{0,1},{1,2},{2,3},{3,0},{4,5},{5,6},{6,7},{7,4},{8,9},{9,10},{10,1... | collective-permute-start | bytes 1544 | tf_op jit(solution)/shard_map/ppermute | solution.py:193

commit v7 on v6

--- a/solution.py
+++ b/solution.py
@@ -9,7 +9,7 @@
 
 AXES = ("dp", "mp")
 ROW = 4
-LAGS = (0, 2, 4, 6, 8, 10, 12, 14)
+LAGS = (0, 3, 6, 9, 12, 15, 18, 21)
 LOG2_E = 1.4426950408889634
 NT = (((1,), (1,)), ((), ()))
 TN = (((0,), (0,)), ((), ()))

time: 91.4 us -> 90.9 us (level)
  no operation moved by 1% of the time
where the time goes in v7:
time: 90.9 us; the launch traced here: 90.6 us
  Pallas kernels  27.9 us (31%)
  waiting for transfers between devices  23.5 us (26%)
  blocking collectives  18.5 us (20%)
  starting transfers between devices  12 us (13%)
  local copies, waits for them, and re-layouts  6.03 us (7%)
  other arithmetic  1.97 us (2%)
    ppermute x5, waiting for transfers between devices, from_behind(): lax.ppermute(block, AXES, [((i - distance) % count, i) for i in range(cou...  23.5 us
    pallas_call x1, Pallas kernels, pairs(): pl.pallas_call(functools.partial(pairs_kernel, count=count, together=4),...  23 us
    all_to_all x1, blocking collectives, column_total(): lax.all_to_all(spread, AXES, 0, 0, axis_index_groups=groups, tiled=True)  18.5 us
    ppermute x5, starting transfers between devices, from_behind(): lax.ppermute(block, AXES, [((i - distance) % count, i) for i in range(cou...  7.96 us
    unnamed x14, local copies, waits for them, and re-layouts  6 us
    ppermute x3, starting transfers between devices, row_met(): return [lax.ppermute(value, AXES, route) for route in routes]  4.05 us
    pallas_call x1, Pallas kernels, project(): pl.pallas_call(project_kernel, out_shape=[jax.ShapeDtypeStruct(block.shap...  3.42 us
  transfers between devices with their start and end apart: 8, of which 2 were waited for; matrix products, arithmetic and copies ran while one was open for 2% of the time, Pallas kernels for 5%

profile of v7, /device:TPU:1, one launch (start us, length us, event | category | flops | bytes accessed | tf_op | source)
XLA Modules:
  0.0 90.6 jit_solution(4686418109858820882)
XLA Ops:
  0.6 6.4 %collective-permute-start.2 = (bf16[4,128,1024]{2,1,0:T(8,128)(2,1)}, bf16[4,128,1024]{2,1,0:T(8,128)(2,1)S(1)}, u32[]{:S(2)}, u32[]{:S(2)}) collective-permute-start(bf16[4,128,1024]{2,1,0:T(8,128)(2,1)} %refs_0_.1), channel_id=1, source_target_pairs={{1,0},{2,1},{3,2},{4,3},{5,4},{6,5},{7,6},{8,7},{9,8},{10,9},{11,1... | collective-permute-start | bytes 3145736 | tf_op jit(solution)/shard_map/ppermute | solution.py:27
  7.0 0.0 collective-permute-start.1
  7.0 0.7 and_select_fusion
  7.7 0.7 pad_add_fusion
  8.5 0.0 collective-permute-start
  8.5 0.0 copy-start
  8.5 1.6 %copy-done = bf16[1024,1024]{1,0:T(8,128)(2,1)S(1)} copy-done((bf16[1024,1024]{1,0:T(8,128)(2,1)S(1)}, bf16[1024,1024]{1,0:T(8,128)(2,1)}, u32[]{:S(2)}) %copy-start) | copy-done | bytes 2097176
  10.1 0.0 copy-start.2
  10.1 1.6 %copy-done.2 = bf16[1024,1024]{1,0:T(8,128)(2,1)S(1)} copy-done((bf16[1024,1024]{1,0:T(8,128)(2,1)S(1)}, bf16[1024,1024]{1,0:T(8,128)(2,1)}, u32[]{:S(2)}) %copy-start.2) | copy-done | bytes 2097176
  11.7 0.0 copy-start.4
  11.7 1.6 %copy-done.4 = bf16[1024,1024]{1,0:T(8,128)(2,1)S(1)} copy-done((bf16[1024,1024]{1,0:T(8,128)(2,1)S(1)}, bf16[1024,1024]{1,0:T(8,128)(2,1)}, u32[]{:S(2)}) %copy-start.4) | copy-done | bytes 2097176
  13.3 0.0 copy-start.6
  13.3 1.2 %copy-done.6 = bf16[4,128,1024]{2,1,0:T(8,128)(2,1)S(1)} copy-done((bf16[4,128,1024]{2,1,0:T(8,128)(2,1)S(1)}, bf16[4,128,1024]{2,1,0:T(8,128)(2,1)}, u32[]{:S(2)}) %copy-start.6) | copy-done | bytes 1048600
  14.5 0.0 copy-start.1
  14.5 0.0 copy-start.3
  14.5 0.0 copy-start.5
  14.5 3.4 %project.1.own_ref = bf16[4,128,3072]{2,1,0:T(8,128)(2,1)S(1)} custom-call(bf16[4,128,1024]{2,1,0:T(8,128)(2,1)S(1)} %copy-done.6, bf16[1024,1024]{1,0:T(8,128)(2,1)S(1)} %copy-done, bf16[1024,1024]{1,0:T(8,128)(2,1)S(1)} %copy-done.2, bf16[1024,1024]{1,0:T(8,128)(2,1)S(1)} %copy-done.4), custom_call_target="tpu_custom_call" | custom-call | flops 3221225472 | bytes 14680064 | tf_op jit(solution)/shard_map/project/pallas_call | solution.py:43
  17.9 18.2 %collective-permute-done.info_ref = s32[16]{0:T(128)S(1)} collective-permute-done((s32[16]{0:T(128)S(1)}, s32[16]{0:T(128)S(1)}, u32[]{:S(2)}, u32[]{:S(2)}) %collective-permute-start) | collective-permute-done | bytes 96 | tf_op jit(solution)/shard_map/ppermute | solution.py:27
  36.1 0.0 collective-permute-done.2.right_x
  36.1 0.0 collective-permute-done.1.left_x
  36.1 0.0 copy-done.1
  36.1 0.0 copy-done.3
  36.1 0.0 copy-done.5
  36.1 23.0 %pairs.1 = (bf16[4,128,1024]{2,1,0:T(8,128)(2,1)}, bf16[4,128,1024]{2,1,0:T(8,128)(2,1)S(1)}, bf16[4,128,1024]{2,1,0:T(8,128)(2,1)}, f32[8,128]{1,0:T(8,128)S(1)}) custom-call(s32[16]{0:T(128)S(1)} %collective-permute-done.info_ref, bf16[4,128,3072]{2,1,0:T(8,128)(2,1)S(1)} %project.1.own_ref, bf16[4,128,1024]{2,1,0:T(8,128)(2,1)S(1)} %collective-permute-done.1.left_x, ...), custom_call_target="tpu_custom_call" | custom-call | flops 21474836480 | bytes 12582912 | tf_op jit(solution)/shard_map/pairs/pallas_call | solution.py:172
  59.1 0.1 collective-permute-start.3
  59.2 1.5 %collective-permute-start.4 = (bf16[4,128,1024]{2,1,0:T(8,128)(2,1)}, bf16[4,128,1024]{2,1,0:T(8,128)(2,1)S(1)}, u32[]{:S(2)}, u32[]{:S(2)}) collective-permute-start(bf16[4,128,1024]{2,1,0:T(8,128)(2,1)} %get-tuple-element.10), channel_id=1, source_target_pairs={{255,0},{0,1},{1,2},{2,3},{3,4},{4,5},{5,6},{6,7},{7,8},{8,9},{9,1... | collective-permute-start | bytes 3145736 | tf_op jit(solution)/shard_map/ppermute | solution.py:27
  60.7 18.5 %all_to_all.6 = f32[64,1,128]{2,1,0:T(1,128)S(1)} all-to-all(f32[64,1,128]{2,1,0:T(1,128)S(1)} %broadcast_in_dim.8), channel_id=1, replica_groups={{0,4,8,12,16,20,24,28,32,36,40,44,48,52,56,60,64,68,72,76,80,84,88,92,9..., dimensions={0} | all-to-all | bytes 65536 | tf_op jit(solution)/shard_map/all_to_all | solution.py:200
  79.2 3.4 %collective-permute-start.7 = (f32[1,128]{1,0:T(1,128)S(1)}, f32[1,128]{1,0:T(1,128)S(1)}, u32[]{:S(2)}, u32[]{:S(2)}) collective-permute-start(f32[1,128]{1,0:T(1,128)S(1)} %bitcast.7), channel_id=1, source_target_pairs={{0,3},{1,0},{2,1},{3,2},{4,7},{5,4},{6,5},{7,6},{8,11},{9,8},{10,9... | collective-permute-start | bytes 1544 | tf_op jit(solution)/shard_map/ppermute | solution.py:193
  82.6 0.0 collective-permute-start.6
  82.6 0.7 collective-permute-start.5
  83.3 0.0 collective-permute-done.3.a_ref
  83.3 5.4 %collective-permute-done.4.c_ref = bf16[4,128,1024]{2,1,0:T(8,128)(2,1)S(1)} collective-permute-done((bf16[4,128,1024]{2,1,0:T(8,128)(2,1)}, bf16[4,128,1024]{2,1,0:T(8,128)(2,1)S(1)}, u32[]{:S(2)}, u32[]{:S(2)}) %collective-permute-start.4) | collective-permute-done | bytes 1048608 | tf_op jit(solution)/shard_map/ppermute | solution.py:27
  88.7 1.4 %combine.1 = f32[4,128,1024]{2,1,0:T(8,128)} custom-call(bf16[4,128,1024]{2,1,0:T(8,128)(2,1)S(1)} %collective-permute-done.3.a_ref, bf16[4,128,1024]{2,1,0:T(8,128)(2,1)S(1)} %get-tuple-element.9.b_ref, bf16[4,128,1024]{2,1,0:T(8,128)(2,1)S(1)} %collective-permute-done.4.c_ref), custom_call_target="tpu_custom_call" | custom-call | flops 1048576 | bytes 2097152 | tf_op jit(solution)/shard_map/combine/pallas_call | solution.py:219
  90.1 0.0 collective-permute-done.7
  90.1 0.0 collective-permute-done.6
  90.1 0.0 collective-permute-done.5
  90.1 0.5 add_multiply_fusion
  (3 shorter events, 0.0 us)
Async XLA Ops:
  0.6 35.5 %collective-permute-start.2 = (bf16[4,128,1024]{2,1,0:T(8,128)(2,1)}, bf16[4,128,1024]{2,1,0:T(8,128)(2,1)S(1)}, u32[]{:S(2)}, u32[]{:S(2)}) collective-permute-start(bf16[4,128,1024]{2,1,0:T(8,128)(2,1)} %refs_0_.1), channel_id=1, source_target_pairs={{1,0},{2,1},{3,2},{4,3},{5,4},{6,5},{7,6},{8,7},{9,8},{10,9},{11,1... | collective-permute-start | bytes 3145736 | tf_op jit(solution)/shard_map/ppermute | solution.py:27
  7.0 29.1 %collective-permute-start.1 = (bf16[4,128,1024]{2,1,0:T(8,128)(2,1)}, bf16[4,128,1024]{2,1,0:T(8,128)(2,1)S(1)}, u32[]{:S(2)}, u32[]{:S(2)}) collective-permute-start(bf16[4,128,1024]{2,1,0:T(8,128)(2,1)} %refs_0_.1), channel_id=1, source_target_pairs={{255,0},{0,1},{1,2},{2,3},{3,4},{4,5},{5,6},{6,7},{7,8},{8,9},{9,1... | collective-permute-start | bytes 3145736 | tf_op jit(solution)/shard_map/ppermute | solution.py:27
  8.5 27.6 %collective-permute-start = (s32[16]{0:T(128)S(1)}, s32[16]{0:T(128)S(1)}, u32[]{:S(2)}, u32[]{:S(2)}) collective-permute-start(s32[16]{0:T(128)S(1)} %pad_add_fusion), channel_id=1, source_target_pairs={{255,0},{0,1},{1,2},{2,3},{3,4},{4,5},{5,6},{6,7},{7,8},{8,9},{9,1... | collective-permute-start | bytes 200 | tf_op jit(solution)/shard_map/ppermute | solution.py:27
  8.5 1.6 %copy-start = (bf16[1024,1024]{1,0:T(8,128)(2,1)S(1)}, bf16[1024,1024]{1,0:T(8,128)(2,1)}, u32[]{:S(2)}) copy-start(bf16[1024,1024]{1,0:T(8,128)(2,1)} %wq_ref.1) | copy-start | bytes 6291460
  10.1 1.6 %copy-start.2 = (bf16[1024,1024]{1,0:T(8,128)(2,1)S(1)}, bf16[1024,1024]{1,0:T(8,128)(2,1)}, u32[]{:S(2)}) copy-start(bf16[1024,1024]{1,0:T(8,128)(2,1)} %wk_ref.1) | copy-start | bytes 6291460
  11.7 1.6 %copy-start.4 = (bf16[1024,1024]{1,0:T(8,128)(2,1)S(1)}, bf16[1024,1024]{1,0:T(8,128)(2,1)}, u32[]{:S(2)}) copy-start(bf16[1024,1024]{1,0:T(8,128)(2,1)} %wv_ref.1) | copy-start | bytes 6291460
  13.3 1.2 %copy-start.6 = (bf16[4,128,1024]{2,1,0:T(8,128)(2,1)S(1)}, bf16[4,128,1024]{2,1,0:T(8,128)(2,1)}, u32[]{:S(2)}) copy-start(bf16[4,128,1024]{2,1,0:T(8,128)(2,1)} %refs_0_.1) | copy-start | bytes 3145732
  14.5 21.6 %copy-start.1 = (bf16[1024,1024]{1,0:T(8,128)(2,1)S(1)}, bf16[1024,1024]{1,0:T(8,128)(2,1)}, u32[]{:S(2)}) copy-start(bf16[1024,1024]{1,0:T(8,128)(2,1)} %wq_ref.1) | copy-start | bytes 6291460
  14.5 21.6 %copy-start.3 = (bf16[1024,1024]{1,0:T(8,128)(2,1)S(1)}, bf16[1024,1024]{1,0:T(8,128)(2,1)}, u32[]{:S(2)}) copy-start(bf16[1024,1024]{1,0:T(8,128)(2,1)} %wk_ref.1) | copy-start | bytes 6291460
  14.5 21.6 %copy-start.5 = (bf16[1024,1024]{1,0:T(8,128)(2,1)S(1)}, bf16[1024,1024]{1,0:T(8,128)(2,1)}, u32[]{:S(2)}) copy-start(bf16[1024,1024]{1,0:T(8,128)(2,1)} %wv_ref.1) | copy-start | bytes 6291460
  59.1 24.1 %collective-permute-start.3 = (bf16[4,128,1024]{2,1,0:T(8,128)(2,1)}, bf16[4,128,1024]{2,1,0:T(8,128)(2,1)S(1)}, u32[]{:S(2)}, u32[]{:S(2)}) collective-permute-start(bf16[4,128,1024]{2,1,0:T(8,128)(2,1)} %get-tuple-element.8), channel_id=1, source_target_pairs={{1,0},{2,1},{3,2},{4,3},{5,4},{6,5},{7,6},{8,7},{9,8},{10,9},{11,1... | collective-permute-start | bytes 3145736 | tf_op jit(solution)/shard_map/ppermute | solution.py:27
  59.2 29.4 %collective-permute-start.4 = (bf16[4,128,1024]{2,1,0:T(8,128)(2,1)}, bf16[4,128,1024]{2,1,0:T(8,128)(2,1)S(1)}, u32[]{:S(2)}, u32[]{:S(2)}) collective-permute-start(bf16[4,128,1024]{2,1,0:T(8,128)(2,1)} %get-tuple-element.10), channel_id=1, source_target_pairs={{255,0},{0,1},{1,2},{2,3},{3,4},{4,5},{5,6},{6,7},{7,8},{8,9},{9,1... | collective-permute-start | bytes 3145736 | tf_op jit(solution)/shard_map/ppermute | solution.py:27
  79.2 10.9 %collective-permute-start.7 = (f32[1,128]{1,0:T(1,128)S(1)}, f32[1,128]{1,0:T(1,128)S(1)}, u32[]{:S(2)}, u32[]{:S(2)}) collective-permute-start(f32[1,128]{1,0:T(1,128)S(1)} %bitcast.7), channel_id=1, source_target_pairs={{0,3},{1,0},{2,1},{3,2},{4,7},{5,4},{6,5},{7,6},{8,11},{9,8},{10,9... | collective-permute-start | bytes 1544 | tf_op jit(solution)/shard_map/ppermute | solution.py:193
  82.6 7.5 %collective-permute-start.6 = (f32[1,128]{1,0:T(1,128)S(1)}, f32[1,128]{1,0:T(1,128)S(1)}, u32[]{:S(2)}, u32[]{:S(2)}) collective-permute-start(f32[1,128]{1,0:T(1,128)S(1)} %bitcast.8), channel_id=1, source_target_pairs={{0,2},{1,3},{2,0},{3,1},{4,6},{5,7},{6,4},{7,5},{8,10},{9,11},{10,... | collective-permute-start | bytes 1544 | tf_op jit(solution)/shard_map/ppermute | solution.py:193
  82.6 7.5 %collective-permute-start.5 = (f32[1,128]{1,0:T(1,128)S(1)}, f32[1,128]{1,0:T(1,128)S(1)}, u32[]{:S(2)}, u32[]{:S(2)}) collective-permute-start(f32[1,128]{1,0:T(1,128)S(1)} %bitcast.9), channel_id=1, source_target_pairs={{0,1},{1,2},{2,3},{3,0},{4,5},{5,6},{6,7},{7,4},{8,9},{9,10},{10,1... | collective-permute-start | bytes 1544 | tf_op jit(solution)/shard_map/ppermute | solution.py:193
